TPU v7x, 32 devices: a whole 2x2x4 slice. The times are simulated.
32 devices in a mesh: dp: 16 (over z, x, core), tensor: 2 (over y).
Axes of the slice: x: 2, y: 2, z: 4, core: 2. Of those that a mesh axis runs over, the one named last changes fastest.
Arguments:
- hidden_in: bfloat16 [16384, 1024], P('dp'), may hold values from -6 to 6
- piece_starts: int32 [16, 2], P('dp'), may hold values from 0 to 768, as said below
- ln1_gain: float32 [1024], replicated, may hold values from 0.25 to 1.75
- ln1_bias: float32 [1024], replicated, may hold values from -1.75 to 1.75
- ln2_gain: float32 [1024], replicated, may hold values from 0.25 to 1.75
- ln2_bias: float32 [1024], replicated, may hold values from -1.75 to 1.75
- qkv_weight: bfloat16 [1024, 3072], P(None, 'tensor'), may hold values from -0.25 to 0.25
- qkv_bias: float32 [3072], P('tensor'), may hold values from -3 to 3
- out_weight: bfloat16 [1024, 1024], P('tensor'), may hold values from -0.75 to 0.75
- out_bias: float32 [1024], replicated, may hold values from -3 to 3
- fc1_weight: bfloat16 [1024, 4096], P(None, 'tensor'), may hold values from -0.1875 to 0.1875
- fc1_bias: float32 [4096], P('tensor'), may hold values from -3 to 3
- fc2_weight: bfloat16 [4096, 1024], P('tensor'), may hold values from -0.125 to 0.125
- fc2_bias: float32 [1024], replicated, may hold values from -3 to 3
- cotangent: bfloat16 [16384, 1024], P('dp'), may hold values from -6 to 6
Outputs:
- hidden_out: bfloat16 [16384, 1024], P('dp')
- hidden_grad: bfloat16 [16384, 1024], P('dp')
- ln1_gain_grad: float32 [1024], replicated
- ln1_bias_grad: float32 [1024], replicated
- qkv_weight_grad: float32 [1024, 3072], P('dp', 'tensor')
- qkv_bias_grad: float32 [3072], P('tensor')
- out_weight_grad: float32 [1024, 1024], P('tensor', 'dp')
- out_bias_grad: float32 [1024], replicated
- ln2_gain_grad: float32 [1024], replicated
- ln2_bias_grad: float32 [1024], replicated
- fc1_weight_grad: float32 [1024, 4096], P('dp', 'tensor')
- fc1_bias_grad: float32 [4096], P('tensor')
- fc2_weight_grad: float32 [4096, 1024], P('tensor', 'dp')
- fc2_bias_grad: float32 [1024], replicated
Inputs may be any that keep to these rules, and one draw needn't show every extreme that they name: `piece_starts`: each row lists the first positions of 2 picture pieces of 256 tokens of one sequence in rising order; the pieces don't intersect and lie inside the sequence of 1024 tokens.
All inputs are finite; a program needn't handle non-finite values.
Results may differ from a plain program's by a relative error of at most 0.012.
The roundings to bfloat16 on the way count: a program that leaves them out, or rounds other values in their place, can miss the bound.
Values sent between devices are 32-bit elements; how exact they have to be, the bound alone decides.
A program may use at most 256 MiB of HBM per device.

v0:
```python
import math

import jax
import jax.numpy as jnp
from jax import lax
from jax.sharding import PartitionSpec as P

HD = 64
ROT = 16
PIECE = 256


epsilon = 1e-05
masked_score = -1e30


def rotary_tables(length, rotary):
    half_rot = rotary // 2
    freqs = 10000.0 ** (-jnp.arange(half_rot, dtype=jnp.float32) * 2.0 / rotary)
    angles = jnp.arange(length, dtype=jnp.float32)[:, None] * freqs[None, :]
    cosine = jnp.cos(angles)
    sine = jnp.sin(angles)
    return (jnp.concatenate([cosine, cosine], axis=1), jnp.concatenate([sine, sine], axis=1))


def rotate(values, cosine, sine, rotary):
    turned_part = values[..., :rotary]
    first_half = turned_part[..., : rotary // 2]
    second_half = turned_part[..., rotary // 2 :]
    swapped = jnp.concatenate([-second_half, first_half], axis=-1)
    result = turned_part * cosine[:, None, :] + swapped * sine[:, None, :]
    return jnp.concatenate([result, values[..., rotary:]], axis=-1)


def rotate_back(grads, cosine, sine, rotary):
    turned_part = grads[..., :rotary]
    scaled = turned_part * sine[:, None, :]
    first_half = scaled[..., : rotary // 2]
    second_half = scaled[..., rotary // 2 :]
    result = turned_part * cosine[:, None, :] + jnp.concatenate([second_half, -first_half], axis=-1)
    return jnp.concatenate([result, grads[..., rotary:]], axis=-1)


def block_mask(owner, start_row, block_rows, length):
    positions = jnp.arange(length, dtype=jnp.int32)
    query_pos = start_row + jnp.arange(block_rows, dtype=jnp.int32)
    query_owner = owner[start_row : start_row + block_rows]
    causal = positions[None, :] <= query_pos[:, None]
    same_piece = (query_owner[:, None] == owner[None, :]) & (query_owner[:, None] >= 0)
    return causal | same_piece


def gelu_slope(hidden_pre):
    cumul = 0.5 * (1.0 + lax.erf(hidden_pre / math.sqrt(2.0)))
    density = jnp.exp(-0.5 * hidden_pre * hidden_pre) / math.sqrt(2.0 * math.pi)
    return cumul + hidden_pre * density


def local(
    hidden_in,
    piece_starts,
    ln1_gain,
    ln1_bias,
    ln2_gain,
    ln2_bias,
    qkv_weight,
    qkv_bias,
    out_weight,
    out_bias,
    fc1_weight,
    fc1_bias,
    fc2_weight,
    fc2_bias,
    cotangent,
):
    seq_count = piece_starts.shape[0]
    row_count = hidden_in.shape[0]
    length = row_count // seq_count
    heads_here = qkv_weight.shape[1] // (3 * HD)
    inner = heads_here * HD
    block_rows = min(512, length)
    scale = 1.0 / math.sqrt(HD)
    inputs = hidden_in.astype(jnp.float32)
    centred = inputs - jnp.mean(inputs, axis=1, keepdims=True)
    inv_std = lax.rsqrt(jnp.mean(centred * centred, axis=1, keepdims=True) + epsilon)
    normed = centred * inv_std
    attn_in = (normed * ln1_gain + ln1_bias).astype(jnp.bfloat16)
    mlp_in = (normed * ln2_gain + ln2_bias).astype(jnp.bfloat16)
    packed = jnp.dot(attn_in, qkv_weight, preferred_element_type=jnp.float32) + qkv_bias
    packed = packed.reshape(seq_count, length, heads_here, 3, HD)
    cosine, sine = rotary_tables(length, ROT)
    queries = (rotate(packed[:, :, :, 0], cosine, sine, ROT) * scale).astype(jnp.bfloat16)
    keys = rotate(packed[:, :, :, 1], cosine, sine, ROT).astype(jnp.bfloat16)
    values = packed[:, :, :, 2].astype(jnp.bfloat16)
    positions = jnp.arange(length, dtype=jnp.int32)
    owner = jnp.full((seq_count, length), -1, jnp.int32)
    for piece_index in range(piece_starts.shape[1]):
        begins = piece_starts[:, piece_index : piece_index + 1]
        inside = (positions[None, :] >= begins) & (positions[None, :] < begins + PIECE)
        owner = jnp.where(inside, jnp.int32(piece_index), owner)

    def attend(items):
        seq_queries, seq_keys, seq_values, seq_owner = items
        outputs = []
        log_sums = []
        for start_row in range(0, length, block_rows):
            block_queries = seq_queries[start_row : start_row + block_rows]
            scores = jnp.einsum(
                "qhd,khd->hqk", block_queries, seq_keys, preferred_element_type=jnp.float32
            )
            allowed = block_mask(seq_owner, start_row, block_rows, length)
            scores = jnp.where(allowed[None], scores, masked_score)
            largest = jnp.max(scores, axis=-1, keepdims=True)
            expo = jnp.exp(scores - largest)
            totals = jnp.sum(expo, axis=-1, keepdims=True)
            weights = (expo / totals).astype(jnp.bfloat16)
            outputs.append(
                jnp.einsum("hqk,khd->qhd", weights, seq_values, preferred_element_type=jnp.float32)
            )
            log_sums.append(largest[..., 0] + jnp.log(totals[..., 0]))
        return (jnp.concatenate(outputs, axis=0), jnp.concatenate(log_sums, axis=1))

    mixed, log_sum = lax.map(attend, (queries, keys, values, owner))
    attn_out = mixed.reshape(row_count, inner).astype(jnp.bfloat16)
    hidden_pre = jnp.dot(mlp_in, fc1_weight, preferred_element_type=jnp.float32) + fc1_bias
    activated = jax.nn.gelu(hidden_pre, approximate=False).astype(jnp.bfloat16)
    partial_value = jnp.dot(attn_out, out_weight, preferred_element_type=jnp.float32)
    partial_value = partial_value + jnp.dot(
        activated, fc2_weight, preferred_element_type=jnp.float32
    )
    branches = lax.psum(partial_value, "tensor")
    hidden_out = (inputs + branches + out_bias + fc2_bias).astype(jnp.bfloat16)
    grad_float = cotangent.astype(jnp.float32)
    out_weight_grad = jnp.einsum(
        "ni,nd->id", attn_out, cotangent, preferred_element_type=jnp.float32
    )
    fc2_weight_grad = jnp.einsum(
        "nf,nd->fd", activated, cotangent, preferred_element_type=jnp.float32
    )
    bias_grad = jnp.sum(grad_float, axis=0)
    hidden_back = jnp.einsum("nd,fd->nf", cotangent, fc2_weight, preferred_element_type=jnp.float32)
    pre_grad = (hidden_back * gelu_slope(hidden_pre)).astype(jnp.bfloat16)
    fc1_weight_grad = jnp.einsum("nd,nf->df", mlp_in, pre_grad, preferred_element_type=jnp.float32)
    fc1_bias_grad = jnp.sum(pre_grad.astype(jnp.float32), axis=0)
    mlp_in_grad = jnp.einsum("nf,df->nd", pre_grad, fc1_weight, preferred_element_type=jnp.float32)
    out_grad = jnp.einsum("nd,id->ni", cotangent, out_weight, preferred_element_type=jnp.float32)
    out_grad = out_grad.astype(jnp.bfloat16).reshape(seq_count, length, heads_here, HD)

    def attend_back(items):
        seq_queries, seq_keys, seq_values, seq_owner, seq_grad, seq_sum = items
        keys_acc = jnp.zeros(seq_keys.shape, jnp.float32)
        values_acc = jnp.zeros(seq_values.shape, jnp.float32)
        query_parts = []
        for start_row in range(0, length, block_rows):
            block_queries = seq_queries[start_row : start_row + block_rows]
            block_grad = seq_grad[start_row : start_row + block_rows]
            block_sum = seq_sum[:, start_row : start_row + block_rows]
            scores = jnp.einsum(
                "qhd,khd->hqk", block_queries, seq_keys, preferred_element_type=jnp.float32
            )
            allowed = block_mask(seq_owner, start_row, block_rows, length)
            scores = jnp.where(allowed[None], scores, masked_score)
            weights = jnp.exp(scores - block_sum[:, :, None])
            weight_grad = jnp.einsum(
                "qhd,khd->hqk", block_grad, seq_values, preferred_element_type=jnp.float32
            )
            values_acc = values_acc + jnp.einsum(
                "hqk,qhd->khd",
                weights.astype(jnp.bfloat16),
                block_grad,
                preferred_element_type=jnp.float32,
            )
            row_dot = jnp.sum(weights * weight_grad, axis=-1, keepdims=True)
            score_grad = (weights * (weight_grad - row_dot)).astype(jnp.bfloat16)
            query_parts.append(
                jnp.einsum("hqk,khd->qhd", score_grad, seq_keys, preferred_element_type=jnp.float32)
            )
            keys_acc = keys_acc + jnp.einsum(
                "hqk,qhd->khd", score_grad, block_queries, preferred_element_type=jnp.float32
            )
        return (jnp.concatenate(query_parts, axis=0), keys_acc, values_acc)

    queries_grad, keys_grad, values_grad = lax.map(
        attend_back, (queries, keys, values, owner, out_grad, log_sum)
    )
    query_pre = rotate_back(queries_grad * scale, cosine, sine, ROT)
    key_pre = rotate_back(keys_grad, cosine, sine, ROT)
    packed_grad = jnp.stack([query_pre, key_pre, values_grad], axis=3)
    packed_grad = packed_grad.reshape(row_count, 3 * inner).astype(jnp.bfloat16)
    qkv_weight_grad = jnp.einsum(
        "nd,nc->dc", attn_in, packed_grad, preferred_element_type=jnp.float32
    )
    qkv_bias_grad = jnp.sum(packed_grad.astype(jnp.float32), axis=0)
    attn_in_grad = jnp.einsum(
        "nc,dc->nd", packed_grad, qkv_weight, preferred_element_type=jnp.float32
    )
    mixed_grad = attn_in_grad * ln1_gain + mlp_in_grad * ln2_gain
    part_grad = inv_std * (
        mixed_grad
        - jnp.mean(mixed_grad, axis=1, keepdims=True)
        - normed * jnp.mean(mixed_grad * normed, axis=1, keepdims=True)
    )
    gain_one = jnp.sum(attn_in_grad * normed, axis=0)
    shift_one = jnp.sum(attn_in_grad, axis=0)
    gain_two = jnp.sum(mlp_in_grad * normed, axis=0)
    shift_two = jnp.sum(mlp_in_grad, axis=0)
    summed_grad, gain_one, shift_one, gain_two, shift_two = lax.psum(
        (part_grad, gain_one, shift_one, gain_two, shift_two), "tensor"
    )
    hidden_grad = (grad_float + summed_grad).astype(jnp.bfloat16)
    gain_one, shift_one, gain_two, shift_two, qkv_bias_sum, bias_sum, fc1_bias_sum = lax.psum(
        (gain_one, shift_one, gain_two, shift_two, qkv_bias_grad, bias_grad, fc1_bias_grad), "dp"
    )
    qkv_weight_part, out_weight_part, fc1_weight_part, fc2_weight_part = (
        lax.psum_scatter(qkv_weight_grad, "dp", scatter_dimension=0, tiled=True),
        lax.psum_scatter(out_weight_grad, "dp", scatter_dimension=1, tiled=True),
        lax.psum_scatter(fc1_weight_grad, "dp", scatter_dimension=0, tiled=True),
        lax.psum_scatter(fc2_weight_grad, "dp", scatter_dimension=1, tiled=True),
    )
    return (
        hidden_out,
        hidden_grad,
        gain_one,
        shift_one,
        qkv_weight_part,
        qkv_bias_sum,
        out_weight_part,
        bias_sum,
        gain_two,
        shift_two,
        fc1_weight_part,
        fc1_bias_sum,
        fc2_weight_part,
        bias_sum,
    )


def solution(mesh):
    in_specs = (
        P("dp", None),
        P("dp", None),
        P(),
        P(),
        P(),
        P(),
        P(None, "tensor"),
        P("tensor"),
        P("tensor", None),
        P(),
        P(None, "tensor"),
        P("tensor"),
        P("tensor", None),
        P(),
        P("dp", None),
    )
    out_specs = (
        P("dp", None),
        P("dp", None),
        P(),
        P(),
        P("dp", "tensor"),
        P("tensor"),
        P("tensor", "dp"),
        P(),
        P(),
        P(),
        P("dp", "tensor"),
        P("tensor"),
        P("tensor", "dp"),
        P(),
    )
    return jax.shard_map(local, mesh=mesh, in_specs=in_specs, out_specs=out_specs, check_vma=False)
```

profile of v0, /device:TPU:0, one launch (start us, length us, event | category | flops | bytes accessed | tf_op | source)
XLA Modules:
  0.0 611.1 jit_solution(9433117442661734023)
XLA Ops:
  13.2 5.7 convolution_add_fusion
  18.9 6.6 %copy.37 = f32[1024,1536]{0,1:T(8,128)} copy(f32[1024,1536]{1,0:T(8,128)} %convolution_add_fusion) | data formatting | bytes 12582912 | tf_op jit(solution)/shard_map/add | solution.py:89
  36.2 2.7 select_reduce_fusion.1
  38.9 3.9 fusion
  42.9 2.7 copy-done.2
  50.6 4.1 fusion.1
  56.4 12.0 %multiply_reduce_fusion.1 = (f32[8,512]{1,0:T(8,128)S(1)}, f32[8,512,1024]{2,1,0:T(8,128)}) fusion(f32[8,512,1024]{2,1,0:T(8,128)} %copy-done.2, f32[8,512]{1,0:T(8,128)S(1)} %log_add_fusion.1, pred[512,1024]{1,0:T(8,128)(4,1)S(1)} %get-tuple-element.112, bf16[512,8,64]{0,2,1:T(8,128)(2,1)S(1)} %bitcast.110, f32[1,1024,8,3,64]{1,4,3,2,0:T(8,128)S(1)} %bitcast.100), kind=kOutput, calls=%fused_computation.4 | convolution fusion | flops 553644032 | bytes 35684352 | tf_op jit(solution)/shard_map/while/body/eval_jaxpr/qhd,khd->hqk/dot_general | solution.py:164
  68.4 12.0 %multiply_reduce_fusion = (f32[8,512]{1,0:T(8,128)S(1)}, f32[8,512,1024]{2,1,0:T(8,128)}) fusion(f32[8,512,1024]{2,1,0:T(8,128)} %copy-done.3, f32[8,512]{1,0:T(8,128)S(1)} %log_add_fusion, pred[512,1024]{1,0:T(8,128)(4,1)S(1)} %get-tuple-element.113, bf16[512,8,64]{0,2,1:T(8,128)(2,1)S(1)} %bitcast.112, f32[1,1024,8,3,64]{1,4,3,2,0:T(8,128)S(1)} %bitcast.101), kind=kOutput, calls=%fused_computation.1 | convolution fusion | flops 553644032 | bytes 35684352 | tf_op jit(solution)/shard_map/while/body/eval_jaxpr/qhd,khd->hqk/dot_general | solution.py:164
  80.4 29.0 %multiply_convert_fusion = (bf16[8,512,1024]{2,1,0:T(8,128)(2,1)}, bf16[8,512,1024]{2,1,0:T(8,128)(2,1)}) fusion(f32[8,512,1024]{2,1,0:T(8,128)} %get-tuple-element.129, f32[8,512,1024]{2,1,0:T(8,128)} %copy-done.3, f32[8,512]{1,0:T(8,128)S(1)} %get-tuple-element.128, f32[8,512]{1,0:T(8,128)S(1)} %log_add_fusion, pred[512,1024]{1,0:T(8,128)(4,1)S(1)} %get-tuple-element.113, ...), kind=kLoop, calls=%fused_computation | loop fusion | flops 41943040 | bytes 85000192 | tf_op jit(solution)/shard_map/while/body/eval_jaxpr/convert_element_type | solution.py:174
  109.4 7.2 %convolution_bitcast_fusion.1 = f32[1,512,8,64]{1,3,2,0:T(8,128)} fusion(bf16[8,512,1024]{2,1,0:T(8,128)(2,1)} %get-tuple-element.133, bf16[1024,8,48]{0,2,1:T(8,128)(2,1)S(1)} %fusion.64, bf16[1024,8,16]{0,2,1:T(8,128)(2,1)S(1)} %get-tuple-element.106), kind=kOutput, calls=%fused_computation.102 | convolution fusion | flops 538968064 | bytes 10485760 | tf_op jit(solution)/shard_map/while/body/eval_jaxpr/hqk,khd->qhd/dot_general | solution.py:176
  116.5 5.1 fusion.68
  121.7 3.6 convolution_bitcast_fusion
  132.5 9.3 %fusion.4 = f32[8,64,1024]{2,1,0:T(8,128)} fusion(bf16[512,8,64]{0,2,1:T(8,128)(2,1)S(1)} %bitcast.113, f32[8,512,1024]{2,1,0:T(8,128)} %copy-done.3, f32[8,512]{1,0:T(8,128)S(1)} %log_add_fusion, pred[512,1024]{1,0:T(8,128)(4,1)S(1)} %copy-done.10), kind=kOutput, calls=%fused_computation.18 | convolution fusion | flops 549453824 | bytes 19939328 | tf_op jit(solution)/shard_map/while/body/eval_jaxpr/hqk,qhd->khd/dot_general | solution.py:167
  141.9 7.1 %fusion.61 = bf16[512,8,64]{0,2,1:T(8,128)(2,1)} fusion(f32[8,512,1024]{2,1,0:T(8,128)S(1)} %bitcast.92, f32[8,512]{1,0:T(8,128)} %copy-done.36, f32[8,512]{1,0:T(8,128)} %copy-done.33, pred[512,1024]{1,0:T(8,128)(4,1)S(1)} %copy-done.8, f32[1,1024,8,3,64]{1,4,3,2,0:T(8,128)} %bitcast.96), kind=kOutput, calls=%fused_computation.105 | convolution fusion | flops 553910272 | bytes 18907136 | tf_op jit(solution)/shard_map/while/body/eval_jaxpr/hqk,khd->qhd/dot_general | solution.py:118
  149.0 9.5 %fusion.62 = bf16[512,8,64]{0,2,1:T(8,128)(2,1)} fusion(f32[8,512,1024]{2,1,0:T(8,128)} %copy-done.3, f32[8,512]{1,0:T(8,128)} %copy-done.37, f32[8,512]{1,0:T(8,128)S(1)} %copy-done.35, pred[512,1024]{1,0:T(8,128)(4,1)S(1)} %copy-done.10, f32[1,1024,8,3,64]{1,4,3,2,0:T(8,128)} %bitcast.97), kind=kOutput, calls=%fused_computation.106 | convolution fusion | flops 553910272 | bytes 18907136 | tf_op jit(solution)/shard_map/while/body/eval_jaxpr/hqk,khd->qhd/dot_general | solution.py:118
  161.4 6.7 %add_bitcast_fusion = bf16[1,1024,8,1,64]{1,4,2,3,0:T(8,128)(2,1)} fusion(f32[8,64,1024]{2,1,0:T(8,128)} %fusion.4, bf16[512,8,64]{0,2,1:T(8,128)(2,1)} %bitcast.111, f32[8,512,1024]{2,1,0:T(8,128)S(1)} %bitcast.92, f32[8,512]{1,0:T(8,128)S(1)} %log_add_fusion.1, pred[512,1024]{1,0:T(8,128)(4,1)S(1)} %copy-done.8), kind=kOutput, calls=%fused_computation.93 | convolution fusion | flops 550502400 | bytes 20987904 | tf_op jit(solution)/shard_map/while/body/eval_jaxpr/hqk,qhd->khd/dot_general | solution.py:167
  172.3 3.5 fusion.101
  176.3 25.4 %fusion.10 = (bf16[1024,2048]{1,0:T(8,128)(2,1)}, f32[1024,2048]{1,0:T(8,128)}) fusion(f32[2048]{0:T(1024)S(1)} %copy-done.49, bf16[1024,2048]{1,0:T(8,128)(2,1)S(1)} %copy-done.46, bf16[1024,1024]{1,0:T(8,128)(2,1)S(1)} %copy-done.5, f32[1024]{0:T(1024)S(1)} %copy-done.54, f32[1024]{0:T(1024)S(1)} %copy-done.55, f32[1024]{0:T(1024)S(1)} %copy-done.41, ...), kind=kOutput, calls=%fused_computation.22 | convolution fusion | flops 4439670784 | bytes 18898944 | tf_op jit(solution)/shard_map/dot_general | solution.py:125
  201.6 9.6 %convert_reduce_fusion = (f32[2048]{0:T(1024)S(1)}, bf16[1024,2048]{1,0:T(8,128)(2,1)S(1)}) fusion(f32[1024,2048]{1,0:T(8,128)} %get-tuple-element.121, f32[2048]{0:T(1024)S(1)} %copy-done.49, bf16[1024,1024]{1,0:T(8,128)(2,1)S(1)} %copy-done.24, bf16[2048,1024]{1,0:T(8,128)(2,1)S(1)} %copy-done.47), kind=kOutput, calls=%fused_computation.29 | convolution fusion | flops 4322228224 | bytes 18890752 | tf_op jit(solution)/shard_map/nd,fd->nf/dot_general | solution.py:141
  211.3 5.8 fusion.87
  217.1 6.4 %fusion.100 = f32[1024,1024]{1,0:T(8,128)S(1)} fusion(bf16[1024,2048]{1,0:T(8,128)(2,1)} %get-tuple-element.120, bf16[2048,1024]{1,0:T(8,128)(2,1)S(1)} %copy-done.47), kind=kOutput, calls=%fused_computation.172 | convolution fusion | flops 4294967296 | bytes 12582912 | tf_op jit(solution)/shard_map/dot_general | solution.py:128
  223.7 3.3 convolution_add_fusion.1
  229.7 4.4 fusion.102
  234.2 8.2 %fusion.84 = f32[1024,1536]{1,0:T(8,128)} fusion(bf16[1024,1536]{0,1:T(8,128)(2,1)} %bitcast.115, bf16[1024,1024]{1,0:T(8,128)(2,1)S(1)} %copy-done.6, f32[1024]{0:T(1024)S(1)} %copy-done.51, f32[1024]{0:T(1024)S(1)} %copy-done.53, f32[1024]{0:T(1024)S(1)} %copy-done.41, f32[1024]{0:T(1024)S(1)} %copy-done.39), kind=kOutput, calls=%fused_computation.162 | convolution fusion | flops 3227516928 | bytes 11550720 | tf_op jit(solution)/shard_map/nd,nc->dc/dot_general | solution.py:190
  242.5 9.5 %fusion.80 = f32[1024,2048]{1,0:T(8,128)} fusion(bf16[1024,2048]{1,0:T(8,128)(2,1)} %copy-done.56, bf16[1024,1024]{1,0:T(8,128)(2,1)S(1)} %copy-done.6, f32[1024]{0:T(1024)S(1)} %copy-done.54, f32[1024]{0:T(1024)S(1)} %copy-done.55, f32[1024]{0:T(1024)S(1)} %copy-done.41, f32[1024]{0:T(1024)S(1)} %copy-done.39), kind=kOutput, calls=%fused_computation.160 | convolution fusion | flops 4301258752 | bytes 14696448 | tf_op jit(solution)/shard_map/nd,nf->df/dot_general | solution.py:143
  253.6 9.0 %fusion.103 = f32[2048,1024]{0,1:T(8,128)} fusion(bf16[1024,2048]{1,0:T(8,128)(2,1)} %get-tuple-element.120, bf16[1024,1024]{1,0:T(8,128)(2,1)S(1)} %copy-done.25), kind=kOutput, calls=%fused_computation.175 | convolution fusion | flops 4294967296 | bytes 14680064 | tf_op jit(solution)/shard_map/nf,nd->fd/dot_general | solution.py:137
  262.8 10.3 %all-reduce.1 = (f32[1024]{0:T(1024)S(1)}, f32[1024]{0:T(1024)S(1)}, f32[1024]{0:T(1024)S(1)}, f32[1024]{0:T(1024)S(1)}) all-reduce(f32[1024]{0:T(1024)S(1)} %get-tuple-element.90, f32[1024]{0:T(1024)S(1)} %get-tuple-element.91, f32[1024]{0:T(1024)S(1)} %get-tuple-element.56, ...), channel_id=1, replica_groups=mesh['dp'=16,'tensor'=2] {'tensor'}, use_global_device_ids=true, to_apply=%region_13.14 | all-reduce | flops 4096 | bytes 32768 | tf_op jit(solution)/shard_map/psum | solution.py:207
  273.1 157.9 %all-reduce.5.cloned.1.call-done = (f32[1024,1024]{1,0:T(8,128)}, f32[1024,1024]{1,0:T(8,128)}) async-done(((f32[1024,1024]{1,0:T(8,128)}, f32[1024,1024]{1,0:T(8,128)}), (f32[1024,1024]{1,0:T(8,128)}, f32[1024,1024]{1,0:T(8,128)})) %all-reduce.5.cloned.1.call-update) | async-done | bytes 8388624 | tf_op jit(solution)/shard_map/psum | solution.py:131
  430.9 4.6 convert_reduce_fusion.3
  435.5 63.9 %all-reduce = (f32[1024]{0:T(1024)}, f32[1024]{0:T(1024)}, f32[1536]{0:T(1024)}, f32[1024]{0:T(1024)S(1)}, f32[1024]{0:T(1024)}, /*index=5*/f32[1024]{0:T(1024)}, f32[2048]{0:T(1024)}) all-reduce(f32[1024]{0:T(1024)S(1)} %get-tuple-element.78, f32[1024]{0:T(1024)S(1)} %get-tuple-element.79, ...), channel_id=1, replica_groups=mesh['dp'=16,'tensor'=2] {'dp'}, use_global_device_ids=true, to_apply=%region_14.15 | all-reduce | flops 8704 | bytes 69632 | tf_op jit(solution)/shard_map/psum | solution.py:211
  499.5 5.1 fusion.53
  504.6 98.1 %reduce-scatter.11.cloned.1.call-done = f32[2048,64]{0,1:T(8,128)} async-done(((f32[2048,1024]{0,1:T(8,128)}), f32[2048,64]{0,1:T(8,128)}) %reduce-scatter.11.cloned.1.call-update) | async-done | bytes 524304 | tf_op jit(solution)/shard_map/reduce_scatter | solution.py:218
  (194 shorter events, 40.9 us)
Async XLA Ops:
  8.1 422.9 %all-reduce.5.cloned.1.call-start = ((), (), s32[]{:S(2)}) async-start(), calls=%async_computation.8 | async-start | bytes 16777216 | tf_op jit(solution)/shard_map/psum | solution.py:131
  34.7 13.1 %copy-start.11 = (bf16[1,1024,8,64]{1,3,2,0:T(8,128)(2,1)}, bf16[1,1024,8,64]{1,3,2,0:T(8,128)(2,1)S(1)}, u32[]{:S(2)}) copy-start(bf16[1,1024,8,64]{1,3,2,0:T(8,128)(2,1)S(1)} %fusion.54) | copy-start | bytes 3145732
  36.2 44.2 %copy-start.7 = (pred[512,1024]{1,0:T(8,128)(4,1)}, pred[512,1024]{1,0:T(8,128)(4,1)S(1)}, u32[]{:S(2)}) copy-start(pred[512,1024]{1,0:T(8,128)(4,1)S(1)} %get-tuple-element.112) | copy-start | bytes 1572868
  36.2 44.2 %copy-start.9 = (pred[512,1024]{1,0:T(8,128)(4,1)}, pred[512,1024]{1,0:T(8,128)(4,1)S(1)}, u32[]{:S(2)}) copy-start(pred[512,1024]{1,0:T(8,128)(4,1)S(1)} %get-tuple-element.113) | copy-start | bytes 1572868
  38.9 6.7 %copy-start.2 = (f32[8,512,1024]{2,1,0:T(8,128)}, f32[8,512,1024]{2,1,0:T(8,128)S(1)}, u32[]{:S(2)}) copy-start(f32[8,512,1024]{2,1,0:T(8,128)S(1)} %get-tuple-element.125) | copy-start | bytes 50331652
  38.9 6.7 %copy-start.33 = (f32[8,512]{1,0:T(8,128)}, f32[8,512]{1,0:T(8,128)S(1)}, u32[]{:S(2)}) copy-start(f32[8,512]{1,0:T(8,128)S(1)} %get-tuple-element.124) | copy-start | bytes 49156
  38.9 6.7 %copy-start.23 = (bf16[1024,1024]{1,0:T(8,128)(2,1)S(1)}, bf16[1024,1024]{1,0:T(8,128)(2,1)}, u32[]{:S(2)}) copy-start(bf16[1024,1024]{1,0:T(8,128)(2,1)} %param.29) | copy-start | bytes 6291460
  38.9 6.7 %copy-start.26 = (bf16[512,1024]{1,0:T(8,128)(2,1)S(1)}, bf16[512,1024]{1,0:T(8,128)(2,1)}, u32[]{:S(2)}) copy-start(bf16[512,1024]{1,0:T(8,128)(2,1)} %param.23) | copy-start | bytes 3145732
  46.9 9.4 %slice-start.6 = ((s8[6291456]{0:T(1024)(128)(4,1)}), s8[4194304]{0:T(1024)(128)(4,1)S(1)}, s32[]{:S(2)}) async-start(s8[6291456]{0:T(1024)(128)(4,1)} %bitcast.98), calls=%async_computation.15 | async-start | bytes 8388608
  47.8 8.5 %copy-start.15 = (bf16[512,512]{0,1:T(8,128)(2,1)}, bf16[512,512]{0,1:T(8,128)(2,1)S(1)}, u32[]{:S(2)}) copy-start(bf16[512,512]{0,1:T(8,128)(2,1)S(1)} %get-tuple-element.100) | copy-start | bytes 1572868
  47.8 8.5 %slice-start.7 = ((s8[6291456]{0:T(1024)(128)(4,1)}), s8[2097152]{0:T(1024)(128)(4,1)S(1)}, s32[]{:S(2)}) async-start(s8[6291456]{0:T(1024)(128)(4,1)} %bitcast.98), calls=%async_computation.16 | async-start | bytes 4194304
  56.3 12.1 %copy-start.37 = (f32[8,512]{1,0:T(8,128)}, f32[8,512]{1,0:T(8,128)S(1)}, u32[]{:S(2)}) copy-start(f32[8,512]{1,0:T(8,128)S(1)} %fusion.1) | copy-start | bytes 49156
  56.4 12.1 %copy-start.16 = (bf16[512,512]{0,1:T(8,128)(2,1)S(1)}, bf16[512,512]{0,1:T(8,128)(2,1)}, u32[]{:S(2)}) copy-start(bf16[512,512]{0,1:T(8,128)(2,1)} %get-tuple-element.101) | copy-start | bytes 1572868
  109.4 7.2 %copy-start.12 = (bf16[1,1024,8,64]{1,3,2,0:T(8,128)(2,1)S(1)}, bf16[1,1024,8,64]{1,3,2,0:T(8,128)(2,1)}, u32[]{:S(2)}) copy-start(bf16[1,1024,8,64]{1,3,2,0:T(8,128)(2,1)} %copy-done.11) | copy-start | bytes 3145732
  109.4 12.3 %slice-start.4 = ((s8[8388608]{0:T(1024)(128)(4,1)}), s8[4194304]{0:T(1024)(128)(4,1)S(1)}, s32[]{:S(2)}) async-start(s8[8388608]{0:T(1024)(128)(4,1)} %bitcast.93), calls=%async_computation.13 | async-start | bytes 8388608
  125.3 16.5 %slice-start = ((s8[16777216]{0:T(1024)(128)(4,1)}), s8[4194304]{0:T(1024)(128)(4,1)S(1)}, s32[]{:S(2)}) async-start(s8[16777216]{0:T(1024)(128)(4,1)} %bitcast.91), calls=%async_computation.9 | async-start | bytes 8388608
  125.3 16.5 %slice-start.1 = ((s8[16777216]{0:T(1024)(128)(4,1)}), s8[4194304]{0:T(1024)(128)(4,1)S(1)}, s32[]{:S(2)}) async-start(s8[16777216]{0:T(1024)(128)(4,1)} %bitcast.91), calls=%async_computation.10 | async-start | bytes 8388608
  127.2 14.6 %slice-start.2 = ((s8[16777216]{0:T(1024)(128)(4,1)}), s8[4194304]{0:T(1024)(128)(4,1)S(1)}, s32[]{:S(2)}) async-start(s8[16777216]{0:T(1024)(128)(4,1)} %bitcast.91), calls=%async_computation.11 | async-start | bytes 8388608
  132.5 9.3 %slice-start.3 = ((s8[16777216]{0:T(1024)(128)(4,1)}), s8[4194304]{0:T(1024)(128)(4,1)S(1)}, s32[]{:S(2)}) async-start(s8[16777216]{0:T(1024)(128)(4,1)} %bitcast.91), calls=%async_computation.12 | async-start | bytes 8388608
  132.5 9.3 %copy-start.8 = (pred[512,1024]{1,0:T(8,128)(4,1)S(1)}, pred[512,1024]{1,0:T(8,128)(4,1)}, u32[]{:S(2)}) copy-start(pred[512,1024]{1,0:T(8,128)(4,1)} %copy-done.7) | copy-start | bytes 1572868
  141.9 7.1 %copy-start.35 = (f32[8,512]{1,0:T(8,128)S(1)}, f32[8,512]{1,0:T(8,128)}, u32[]{:S(2)}) copy-start(f32[8,512]{1,0:T(8,128)} %copy-done.34) | copy-start | bytes 49156
  176.2 25.4 %copy-start.24 = (bf16[1024,1024]{1,0:T(8,128)(2,1)S(1)}, bf16[1024,1024]{1,0:T(8,128)(2,1)}, u32[]{:S(2)}) copy-start(bf16[1024,1024]{1,0:T(8,128)(2,1)} %param.29) | copy-start | bytes 6291460
  176.2 25.4 %copy-start.47 = (bf16[2048,1024]{1,0:T(8,128)(2,1)S(1)}, bf16[2048,1024]{1,0:T(8,128)(2,1)}, u32[]{:S(2)}) copy-start(bf16[2048,1024]{1,0:T(8,128)(2,1)} %param.27) | copy-start | bytes 12582916
  201.6 9.6 %copy-start.53 = (f32[1024]{0:T(1024)S(1)}, f32[1024]{0:T(1024)}, u32[]{:S(2)}) copy-start(f32[1024]{0:T(1024)} %param.17) | copy-start | bytes 12292
  229.7 274.9 %reduce-scatter.7.cloned.1.call-start = ((), (), s32[]{:S(2)}) async-start(), calls=%async_computation.5 | async-start | bytes 2228224 | tf_op jit(solution)/shard_map/reduce_scatter | solution.py:216
  234.1 270.5 %reduce-scatter.5.cloned.1.call-start = ((), (), s32[]{:S(2)}) async-start(), calls=%async_computation.4 | async-start | bytes 6684672 | tf_op jit(solution)/shard_map/reduce_scatter | solution.py:215
  242.4 262.2 %reduce-scatter.9.cloned.1.call-start = ((), (), s32[]{:S(2)}) async-start(), calls=%async_computation.6 | async-start | bytes 8912896 | tf_op jit(solution)/shard_map/reduce_scatter | solution.py:217
  252.0 350.7 %reduce-scatter.11.cloned.1.call-start = ((), (), s32[]{:S(2)}) async-start(), calls=%async_computation.7 | async-start | bytes 8912896 | tf_op jit(solution)/shard_map/reduce_scatter | solution.py:218
  430.9 68.5 %copy-start.42 = (f32[1024]{0:T(1024)S(1)}, f32[1024]{0:T(1024)}, u32[]{:S(2)}) copy-start(f32[1024]{0:T(1024)} %param.28) | copy-start | bytes 12292
  430.9 68.5 %copy-start.43 = (f32[1024]{0:T(1024)S(1)}, f32[1024]{0:T(1024)}, u32[]{:S(2)}) copy-start(f32[1024]{0:T(1024)} %param.24) | copy-start | bytes 12292
  499.5 103.2 %copy-start.44 = (f32[1024]{0:T(1024)}, f32[1024]{0:T(1024)S(1)}, u32[]{:S(2)}) copy-start(f32[1024]{0:T(1024)S(1)} %get-tuple-element.161) | copy-start | bytes 12292
  499.5 103.8 %copy-start.1 = (bf16[1024,1536]{1,0:T(8,128)(2,1)S(1)}, bf16[1024,1536]{1,0:T(8,128)(2,1)}, u32[]{:S(2)}) copy-start(bf16[1024,1536]{1,0:T(8,128)(2,1)} %param.21) | copy-start | bytes 9437188
  (38 other events, 146.8 us)
Sparse Core Ops, SparseCore 0:
  229.8 201.1 all-reduce.4
Sparse Core Ops, SparseCore 1:
  234.5 64.5 reduce-scatter.6
  303.4 83.9 reduce-scatter.4
  391.8 102.9 reduce-scatter.8
  499.5 103.1 reduce-scatter.10
where the time goes:
time: 621 us; the launch traced here: 611 us
  waiting for transfers between devices  256 us (41%)
  matrix products  172 us (28%)
  blocking collectives  74.3 us (12%)
  other arithmetic  66.5 us (11%)
  local copies, waits for them, and re-layouts  24.4 us (4%)
  between operations  18.2 us (3%)
    psum x1, waiting for transfers between devices, local(): branches = lax.psum(partial_value, 'tensor')  158 us
    reduce_scatter x1, waiting for transfers between devices, local(): lax.psum_scatter(fc2_weight_grad, 'dp', scatter_dimension=1, tiled=True)  98.1 us
    psum x1, blocking collectives, local(): lax.psum((gain_one, shift_one, gain_two, shift_two, qkv_bias_grad, bias_g...  63.9 us
    convert_element_type x1, other arithmetic, attend_back(): score_grad = (weights * (weight_grad - row_dot)).astype(jnp.bfloat16)  29 us
    dot_general x1, matrix products, local(): jnp.dot(mlp_in, fc1_weight, preferred_element_type=jnp.float32) + fc1_bias  25.4 us
    dot_general x2, matrix products, attend_back(): jnp.einsum('qhd,khd->hqk', block_grad, seq_values, preferred_element_type...  24 us
    dot_general x2, matrix products, attend(): jnp.einsum('hqk,khd->qhd', weights, seq_values, preferred_element_type=jn...  16.6 us
    dot_general x2, matrix products, attend_back(): jnp.einsum('hqk,qhd->khd', weights.astype(jnp.bfloat16), block_grad, pref...  16 us
  transfers between devices with their start and end apart: 5, of which 2 were waited for; matrix products, arithmetic and copies ran while one was open for 7% of the time, Pallas kernels for 0%

commit v1 on v0

v1 whole, which is shorter than its diff:
```python
import math, functools
import numpy as np
import jax, jax.numpy as jnp
from jax import lax
from jax.sharding import PartitionSpec as P
from jax.experimental import pallas as pl
from jax.experimental.pallas import tpu as pltpu

HD=64; ROT=16; PIECE=256; EPS=1e-5; MASKED=-1e30
F32=jnp.float32; BF=jnp.bfloat16
TB=256

def dot(a,b): return jnp.dot(a,b,preferred_element_type=F32)
def dot_nt(a,b): return lax.dot_general(a,b,(((1,),(1,)),((),())),preferred_element_type=F32)
def dot_tn(a,b): return lax.dot_general(a,b,(((0,),(0,)),((),())),preferred_element_type=F32)

def normalize(x):
    xf=x.astype(F32)
    c=xf-jnp.mean(xf,axis=1,keepdims=True)
    inv=lax.rsqrt(jnp.mean(c*c,axis=1,keepdims=True)+EPS)
    return c*inv, inv

def prologue_body(dp, x_ref,g_ref,g1,b1,g2,b2,w_ref,bq_ref,wo_ref,cos_ref,sin_ref,
             m_out,aT_out,mT_out,gT_out,qkv_out,do_out,gsum_out,wT,bcol):
    step=pl.program_id(0)
    @pl.when(step==0)
    def _():
        wT[...]=w_ref[...].T
        bcol[...]=jnp.broadcast_to(bq_ref[...],(128,bq_ref.shape[1])).T
        gsum_out[...]=jnp.zeros_like(gsum_out)
    d=x_ref.shape[1]
    rows=d//dp
    normed,_=normalize(x_ref[...])
    a=normed*g1[...]+b1[...]
    m=normed*g2[...]+b2[...]
    m_out[...]=m.astype(BF)
    def perm(t):
        t=t.reshape(dp//4,2,2,rows,TB)
        parts=[]
        for core in range(2):
            for xb in range(2):
                parts.append(t[:,xb,core].reshape(d//4,TB))
        return parts
    aT=a.T
    mT=m.T
    gf=g_ref[...].astype(F32)
    gsum_out[...]+=jnp.sum(gf,axis=0,keepdims=True)
    gT=gf.T
    for t,o in ((aT,aT_out),(mT,mT_out),(gT,gT_out)):
        for j,pt in enumerate(perm(t)):
            o[j]=pt.astype(BF)
    packed=dot(wT[...],aT.astype(BF))
    do_out[...]=dot(wo_ref[...],gT.astype(BF)).astype(BF)
    c=cos_ref[...]; s=sin_ref[...]
    heads=qkv_out.shape[0]
    b2c=jnp.concatenate([bcol[...]]*(TB//128),axis=1)
    packed=packed+b2c
    for h in range(heads):
        base=h*3*HD
        for part in range(3):
            blk=packed[base+part*HD:base+(part+1)*HD]
            if part<2:
                a1=blk[0:8]; a2=blk[8:16]
                blk=jnp.concatenate([a1*c-a2*s,a2*c+a1*s,blk[16:]],axis=0)
            if part==0: blk=blk*(1.0/math.sqrt(HD))
            qkv_out[h,part*HD:(part+1)*HD]=blk.astype(BF)

def prologue(dp,x,g,g1,b1,g2,b2,w,bq,wo,cos,sin):
    n,d=x.shape; c=w.shape[1]; inner=wo.shape[0]; heads=c//(3*HD)
    row=lambda v: v.reshape(1,-1)
    full=lambda a: pl.BlockSpec(a.shape,lambda i:(0,)*a.ndim)
    tspec=pl.BlockSpec((4,d//4,TB),lambda i:(0,0,i))
    args=(x,g,row(g1),row(b1),row(g2),row(b2),w,row(bq),wo,cos,sin)
    xs=pl.BlockSpec((TB,d),lambda i:(i,0))
    ts=pl.BlockSpec((8,TB),lambda i:(0,i))
    return pl.pallas_call(functools.partial(prologue_body,dp),name="prologue",
        grid=(n//TB,),
        in_specs=[xs,xs]+[full(a) for a in args[2:9]]+[ts,ts],
        out_specs=[xs,tspec,tspec,tspec,pl.BlockSpec((heads,3*HD,TB),lambda i:(0,0,i)),
                   pl.BlockSpec((inner,TB),lambda i:(0,i)),pl.BlockSpec((1,d),lambda i:(0,0))],
        out_shape=[jax.ShapeDtypeStruct((n,d),BF)]+[jax.ShapeDtypeStruct((4,d//4,n),BF)]*3+
            [jax.ShapeDtypeStruct((heads,3*HD,n),BF),jax.ShapeDtypeStruct((inner,n),BF),jax.ShapeDtypeStruct((1,d),F32)],
        scratch_shapes=[pltpu.VMEM((c,d),BF),pltpu.VMEM((c,128),F32)],
        compiler_params=pltpu.CompilerParams(vmem_limit_bytes=60*2**20),
        cost_estimate=pl.CostEstimate(flops=2*n*d*(c+inner),bytes_accessed=20*2**20,transcendentals=0),
    )(*args)

FB=512; SUB=256
def mlp_body(aliased, *refs):
    if aliased:
        m_ref,g_ref,w1,b1,w2,_,_,act_out,pg_out,part_out,dm_out,bs_out=refs
    else:
        m_ref,g_ref,w1,b1,w2,act_out,pg_out,part_out,dm_out,bs_out=refs
    r=pl.program_id(0); f=pl.program_id(1)
    mi=m_ref[...]; gi=g_ref[...]
    fb=w1.shape[1]
    us=[]; hs=[]
    pt=None; dt=None
    for j in range(fb//SUB):
        sl=slice(j*SUB,(j+1)*SUB)
        u=dot(mi,w1[:,sl])+b1[:,sl]
        hb=dot_nt(gi,w2[sl,:])
        cum=0.5*(1.0+lax.erf(u*(1.0/math.sqrt(2.0))))
        den=jnp.exp(-0.5*u*u)*(1.0/math.sqrt(2.0*math.pi))
        act=(u*cum).astype(BF)
        pg=(hb*(cum+u*den)).astype(BF)
        act_out[:,sl]=act
        pg_out[:,sl]=pg
        bs=jnp.sum(pg.astype(F32),axis=0,keepdims=True)
        bs_out[0,:,sl]=bs
        p=dot(act,w2[sl,:]); dd=dot_nt(pg,w1[:,sl])
        pt=p if pt is None else pt+p
        dt=dd if dt is None else dt+dd
    @pl.when(f==0)
    def _():
        part_out[...]=pt; dm_out[...]=dt
    @pl.when(f>0)
    def _():
        part_out[...]+=pt; dm_out[...]+=dt

def mlp(r0,nr,m,g,w1,b1,w2,prev=None):
    n,d=m.shape; ff=w1.shape[1]
    b1=b1.reshape(1,-1)
    rs=pl.BlockSpec((TB,d),lambda r,f:(r0+r,0))
    any_=pl.BlockSpec(memory_space=pl.ANY)
    fs=pl.BlockSpec((TB,FB),lambda r,f:(r0+r,f))
    os=pl.BlockSpec((TB,d),lambda r,f:(r,0))
    args=[m,g,w1,b1,w2]+([] if prev is None else list(prev))
    return pl.pallas_call(functools.partial(mlp_body,prev is not None),name="mlp%d"%r0,
        grid=(nr,ff//FB),
        in_specs=[rs,rs,pl.BlockSpec((d,FB),lambda r,f:(0,f)),pl.BlockSpec((1,FB),lambda r,f:(0,f)),
                  pl.BlockSpec((FB,d),lambda r,f:(f,0))]+([] if prev is None else [any_,any_]),
        out_specs=[fs,fs,os,os,pl.BlockSpec((1,1,FB),lambda r,f:(r,0,f))],
        out_shape=[jax.ShapeDtypeStruct((n,ff),BF)]*2+[jax.ShapeDtypeStruct((nr*TB,d),F32)]*2+[jax.ShapeDtypeStruct((nr,1,ff),F32)],
        input_output_aliases={} if prev is None else {5:0,6:1},
        compiler_params=pltpu.CompilerParams(vmem_limit_bytes=60*2**20),
        cost_estimate=pl.CostEstimate(flops=8*nr*TB*d*ff,bytes_accessed=16*2**20,transcendentals=nr*TB*ff*2),
    )(*args)

def attn_body(i,KL,final,*refs):
    n_in=0
    starts=refs[0]; qkv,do,part_in,wo=refs[1:5]; pos=5
    acc_in=None
    if i>0: acc_in=refs[pos]; pos+=1
    cos,sin=refs[pos:pos+2]; pos+=2
    dqs=()
    if final: dqs=refs[pos:pos+i]; pos+=i
    o_out,part_out=refs[pos:pos+2]; pos+=2
    if final: pg_out=refs[pos]; pos+=1
    else:
        dq_out,acc_out=refs[pos:pos+2]; pos+=2
    bias,=refs[pos:pos+1]
    h=pl.program_id(0)
    W0=i*TB; WN=KL-W0
    @pl.when(h==0)
    def _():
        kp=W0+lax.broadcasted_iota(jnp.int32,(WN,TB),0)
        qp=W0+lax.broadcasted_iota(jnp.int32,(WN,TB),1)
        ok=kp<=qp
        for p in range(starts.shape[1]):
            s=starts[0,p]
            ok=ok|((kp>=s)&(kp<s+PIECE)&(qp>=s)&(qp<s+PIECE))
        bias[...]=jnp.where(ok,0.0,MASKED)
    qT=qkv[0,0:HD,W0:W0+TB]
    kT=qkv[0,HD:2*HD,0:KL]
    vT=qkv[0,2*HD:3*HD,0:KL]
    doT=do[0]
    k=kT.T; v=vT.T
    S=dot(k,qT)
    if W0>0: S=jnp.concatenate([S[:W0],S[W0:]+bias[...]],axis=0)
    else: S=S+bias[...]
    mx=jnp.max(S,axis=0,keepdims=True)
    e=jnp.exp(S-mx)
    inv=1.0/jnp.sum(e,axis=0,keepdims=True)
    p=e*inv
    pb=p.astype(BF)
    dP=dot(v,doT)
    o_out[0]=dot(vT,pb).astype(BF)
    rd=jnp.sum(p*dP,axis=0,keepdims=True)
    ds=(p*(dP-rd)).astype(BF)
    dq=dot(kT,ds)
    dv=dot_nt(doT,pb)
    dk=dot_nt(qT,ds)
    def back(b,c,s):
        b1=b[0:8]; b2=b[8:16]
        return jnp.concatenate([b1*c+b2*s,b2*c-b1*s,b[16:]],axis=0)
    dq=back(dq*(1.0/math.sqrt(HD)),cos[:,W0:W0+TB],sin[:,W0:W0+TB]).astype(BF)
    if i>0:
        KP=acc_in.shape[2]
        if KP<KL:
            dk=jnp.concatenate([dk[:,:KP]+acc_in[0,0:HD],dk[:,KP:]],axis=1)
            dv=jnp.concatenate([dv[:,:KP]+acc_in[0,HD:2*HD],dv[:,KP:]],axis=1)
        else:
            dk=dk+acc_in[0,0:HD]; dv=dv+acc_in[0,HD:2*HD]
    if final:
        for j,r in enumerate(dqs):
            pg_out[0,0:HD,j*TB:(j+1)*TB]=r[0]
        pg_out[0,0:HD,W0:W0+TB]=dq
        pg_out[0,HD:2*HD]=back(dk,cos[...],sin[...]).astype(BF)
        pg_out[0,2*HD:3*HD]=dv.astype(BF)
    else:
        dq_out[0]=dq
        acc_out[0,0:HD]=dk
        acc_out[0,HD:2*HD]=dv
    w=wo[...]
    @pl.when(h==0)
    def _(): part_out[...]=part_in[...]+dot_tn(o_out[0],w)
    @pl.when(h>0)
    def _(): part_out[...]+=dot_tn(o_out[0],w)

def attn(i,nb,starts,qkv,do,part,prow,wo,acc,cos,sin,dqs):
    heads,_,n=qkv.shape; d=wo.shape[1]
    KL=min((i+2)*TB,n); final=i==nb-1
    W=KL-i*TB
    do3=do.reshape(heads,HD,n)
    whole=lambda s: pl.BlockSpec(s,lambda h,*_:(0,)*len(s))
    ins=[qkv,do3,part,wo]; specs=[pl.BlockSpec((1,3*HD,n),lambda h,*_:(h,0,0)),pl.BlockSpec((1,HD,TB),lambda h,*_:(h,0,i)),
        pl.BlockSpec((TB,d),lambda h,*_:(prow,0)),pl.BlockSpec((HD,d),lambda h,*_:(h,0))]
    hs=lambda s: pl.BlockSpec((1,)+s,lambda h,*_:(h,0,0))
    if i>0: ins.append(acc); specs.append(hs(acc.shape[1:]))
    ins+= [cos,sin]; specs+=[whole(cos.shape),whole(sin.shape)]
    if final:
        ins+=list(dqs); specs+=[hs((HD,TB))]*len(dqs)
    outs=[jax.ShapeDtypeStruct((heads,HD,TB),BF),jax.ShapeDtypeStruct((TB,d),F32)]
    ospecs=[hs((HD,TB)),whole((TB,d))]
    if final:
        outs.append(jax.ShapeDtypeStruct((heads,3*HD,n),BF)); ospecs.append(hs((3*HD,n)))
    else:
        outs+=[jax.ShapeDtypeStruct((heads,HD,TB),BF),jax.ShapeDtypeStruct((heads,2*HD,KL),F32)]
        ospecs+=[hs((HD,TB)),hs((2*HD,KL))]
    return pl.pallas_call(functools.partial(attn_body,i,KL,final),name="attn%d"%i,
        grid_spec=pltpu.PrefetchScalarGridSpec(num_scalar_prefetch=1,grid=(heads,),in_specs=specs,out_specs=ospecs,
            scratch_shapes=[pltpu.VMEM((W,TB),F32)]),
        out_shape=outs,
        compiler_params=pltpu.CompilerParams(vmem_limit_bytes=60*2**20),
        cost_estimate=pl.CostEstimate(flops=12*heads*HD*TB*KL*4,bytes_accessed=8*2**20,transcendentals=heads*TB*KL),
    )(starts,*ins)

def wgrad_body(nt,keepers,*refs):
    sc=refs[0]; a_ref=refs[1]; nb=len(nt)
    b_refs=refs[2:2+nb]; pos=2+nb
    if keepers:
        recv,send,keep=refs[pos:pos+3]
    else:
        out,=refs[pos:pos+1]
    x=sc[1]
    for j in range(2):
        xi=(1-x if j==0 else x) if keepers else j
        a=a_ref[xi]
        r=None; t0=0
        for kind,b in zip(nt,b_refs):
            bv=b[...]
            if kind:
                bv=bv.reshape(-1,bv.shape[-1])
                t1=t0+bv.shape[1]; y=dot_nt(a[:,t0:t1],bv)
            else:
                t1=t0+bv.shape[0]; y=dot(a[:,t0:t1],bv)
            t0=t1
            r=y if r is None else r+y
        if keepers:
            r=r+recv[xi]
            if j==0: send[...]=r
            else: keep[...]=r
        else: out[j]=r

def wgrad(sc,a,bs,nt,recv,name):
    q,n=a.shape[1:]
    keepers=recv is not None
    if nt:
        heads,cw=bs[0].shape[:2]; c=heads*cw
        hb=max(1,512//cw)
        while heads%hb: hb-=1
        cb=hb*cw
        bspecs=[pl.BlockSpec((hb,cw,b.shape[2]),lambda i,s:(i,0,0)) for b in bs]
    else:
        c=bs[0].shape[1]; cb=min(512,c)
        bspecs=[pl.BlockSpec((b.shape[0],cb),lambda i,s:(0,i)) for b in bs]
    aspec=pl.BlockSpec((2,q,n),(lambda i,s:(s[0],0,0)) if keepers else (lambda i,s:(1-s[0],0,0)))
    pair=pl.BlockSpec((2,q,cb),lambda i,s:(0,0,i))
    one=pl.BlockSpec((q,cb),lambda i,s:(0,i))
    specs=[aspec]+bspecs+([pair] if keepers else [])
    return pl.pallas_call(functools.partial(wgrad_body,(nt,)*len(bs),keepers),name=name,
        grid_spec=pltpu.PrefetchScalarGridSpec(num_scalar_prefetch=1,grid=(c//cb,),in_specs=specs,
            out_specs=[one,one] if keepers else pair),
        out_shape=[jax.ShapeDtypeStruct((q,c),F32)]*2 if keepers else jax.ShapeDtypeStruct((2,q,c),F32),
        compiler_params=pltpu.CompilerParams(vmem_limit_bytes=60*2**20),
        cost_estimate=pl.CostEstimate(flops=4*q*n*c,bytes_accessed=8*2**20,transcendentals=0),
    )(sc,a,*bs,*([recv] if keepers else []))

def dgrad_body(pg_ref,w_ref,x_ref,dm_ref,g1,g2,e_out,cols_out,qb_out):
    @pl.when(pl.program_id(0)==0)
    def _():
        cols_out[...]=jnp.zeros_like(cols_out)
        qb_out[...]=jnp.zeros_like(qb_out)
    pgT=pg_ref[...].reshape(-1,TB)
    pg=pgT.T
    qb_out[...]+=jnp.sum(pg.astype(F32),axis=0,keepdims=True)
    ag=dot_nt(pg,w_ref[...])
    mg=dm_ref[...]
    normed,inv=normalize(x_ref[...])
    cols_out[...]+=jnp.concatenate([jnp.sum(t,axis=0,keepdims=True) for t in (ag*normed,ag,mg*normed,mg)],axis=0)
    e=ag*g1[...]+mg*g2[...]
    e_out[...]=inv*(e-jnp.mean(e,axis=1,keepdims=True)-normed*jnp.mean(e*normed,axis=1,keepdims=True))

def dgrad(r0,nr,pgT,w,x,dm,drow,g1,g2):
    heads,hw,n=pgT.shape; d,c=w.shape
    xs=pl.BlockSpec((TB,d),lambda i:(r0+i,0))
    row=pl.BlockSpec((1,d),lambda i:(0,0))
    return pl.pallas_call(dgrad_body,name="dgrad%d"%r0,grid=(nr,),
        in_specs=[pl.BlockSpec((heads,hw,TB),lambda i:(0,0,r0+i)),pl.BlockSpec((d,c),lambda i:(0,0)),xs,
            pl.BlockSpec((TB,d),lambda i:(drow+i,0)),row,row],
        out_specs=[pl.BlockSpec((TB,d),lambda i:(i,0)),pl.BlockSpec((4,d),lambda i:(0,0)),pl.BlockSpec((1,c),lambda i:(0,0))],
        out_shape=[jax.ShapeDtypeStruct((nr*TB,d),F32),jax.ShapeDtypeStruct((4,d),F32),jax.ShapeDtypeStruct((1,c),F32)],
        compiler_params=pltpu.CompilerParams(vmem_limit_bytes=60*2**20),
        cost_estimate=pl.CostEstimate(flops=2*nr*TB*d*c,bytes_accessed=12*2**20,transcendentals=0),
    )(pgT,w,x,dm,g1.reshape(1,-1),g2.reshape(1,-1))

def tables(n):
    angles=np.arange(n,dtype=np.float64)[None,:]*(10000.0**(-np.arange(ROT//2)*2.0/ROT))[:,None]
    return jnp.asarray(np.cos(angles),F32),jnp.asarray(np.sin(angles),F32)

def local(dp,x,starts,g1,b1,g2,b2,w,bq,wo,bo,w1,bf1,w2,bf2,g):
    n,d=x.shape; heads=w.shape[1]//(3*HD)
    bits=dp.bit_length()-1
    idx=lax.axis_index("dp")
    bit=lambda b:(idx>>b)&1
    sc=jnp.stack([bit(0),bit(1)]).astype(jnp.int32)
    swap=lambda v,b: lax.ppermute(v,"dp",[(i,i^(1<<b)) for i in range(dp)])
    across=lambda v: lax.ppermute(v,"tensor",[(0,1),(1,0)])
    cos,sin=tables(n)
    nb=n//TB
    m,aT,mT,gT,qkv,do,gsum=prologue(dp,x,g,g1,b1,g2,b2,w,bq,wo,cos,sin)
    act,pg,p0,dm0,bs0=mlp(0,1,m,g,w1,bf1,w2)
    outs=[]; dqs=[]; sent=[]; got=[]
    def step(i,part,prow,acc):
        r=attn(i,nb,starts,qkv,do,part,prow,wo,acc,cos,sin,dqs)
        outs.append(r[0]); sent.append(r[1]); got.append(across(r[1]))
        if i<nb-1: dqs.append(r[2]); return r[3]
        return r[2]
    acc=step(0,p0,0,None)
    act,pg,p1,dm1,bs1=mlp(1,nb-1,m,g,w1,bf1,w2,(act,pg))
    s2=wgrad(sc,gT,[act],False,None,"fc2_other"); r2=swap(s2,0)
    s1=wgrad(sc,mT,[pg],False,None,"fc1_other"); r1=swap(s1,0)
    acc=step(1,p1,0,acc)
    x2,k2=wgrad(sc,gT,[act],False,r2,"fc2_own"); r2=swap(x2,1)
    acc=step(2,p1,1,acc)
    x1,k1=wgrad(sc,mT,[pg],False,r1,"fc1_own"); r1=swap(x1,1)
    pgT=step(3,p1,2,acc)
    sq=wgrad(sc,aT,[pgT],True,None,"qkv_other"); rq=swap(sq,0)
    so=wgrad(sc,gT,outs,True,None,"out_other"); ro=swap(so,0)
    e0,c0,qb0=dgrad(0,1,pgT,w,x,dm0,0,g1,g2); h0=across(e0)
    e1,c1,qb1=dgrad(1,nb-1,pgT,w,x,dm1,0,g1,g2); h1=across(e1)
    xq,kq=wgrad(sc,aT,[pgT],True,rq,"qkv_own"); rq=swap(xq,1)
    xo,ko=wgrad(sc,gT,outs,True,ro,"out_own"); ro=swap(xo,1)
    def finish(keep,recv):
        cur=(keep+recv).reshape(dp//4,d//dp,-1)
        for b in range(2,bits):
            halves=cur.reshape(cur.shape[0]//2,2,*cur.shape[1:])
            send=lax.dynamic_index_in_dim(halves,1-bit(b),1,keepdims=False)
            own=lax.dynamic_index_in_dim(halves,bit(b),1,keepdims=False)
            cur=own+swap(send,b)
        return cur[0]
    f2=finish(k2,r2); f1=finish(k1,r1); fq=finish(kq,rq); fo=finish(ko,ro)
    cols=(c0+c1).reshape(-1)
    cols=cols+across(cols)
    vec=jnp.concatenate([cols,(qb0+qb1)[0],gsum[0],jnp.sum(bs0,axis=(0,1))+jnp.sum(bs1,axis=(0,1))])
    for b in range(bits): vec=vec+swap(vec,b)
    c=w.shape[1]; o=4*d
    gain1,shift1,gain2,shift2=[vec[j*d:(j+1)*d] for j in range(4)]
    qb=vec[o:o+c]; bg=vec[o+c:o+c+d]; fb=vec[o+c+d:]
    hidden=jnp.concatenate([x[i*TB:(i+1)*TB].astype(F32)+(sent[i]+got[i])+bo+bf2 for i in range(nb)]).astype(BF)
    hgrad=jnp.concatenate([g[:TB].astype(F32)+(e0+h0),g[TB:].astype(F32)+(e1+h1)]).astype(BF)
    return (hidden,hgrad,gain1,shift1,fq,qb,fo.T,bg,gain2,shift2,f1,fb,f2.T,bg)

def solution(mesh):
    A=P("dp",None); R=P()
    col=P(None,"tensor"); vt=P("tensor"); rw=P("tensor",None)
    in_specs=(A,A,R,R,R,R,col,vt,rw,R,col,vt,rw,R,A)
    out_specs=(A,A,R,R,P("dp","tensor"),vt,P("tensor","dp"),R,R,R,P("dp","tensor"),vt,P("tensor","dp"),R)
    return jax.shard_map(functools.partial(local,mesh.shape["dp"]),mesh=mesh,in_specs=in_specs,out_specs=out_specs,check_vma=False)
```

time: 621 us -> 470 us (0.76); the launches traced: 611 us -> 469 us
  Pallas kernels: 0 us -> 183 us
  matrix products: 172 us -> 0 us
  blocking collectives: 74.3 us -> 0 us
  other arithmetic: 66.5 us -> 22.7 us
  waiting for transfers between devices: 256 us -> 221 us
  starting transfers between devices: 0.21 us -> 34.5 us
  local copies, waits for them, and re-layouts: 24.4 us -> 6.71 us
  between operations: 18.2 us -> 0.97 us
    ppermute x0 -> x27, waiting for transfers between devices: none -> 221 us  [the longest x7 117 us: local(): across = lambda v: lax.ppermute(v, 'tensor', [(0, 1), (1, 0)])]
    pallas_call x0 -> x17, Pallas kernels: none -> 183 us  [the longest x4 69.1 us: attn(): pl.pallas_call(functools.partial(attn_body, i, KL, final), name='attn%d'...]
    dot_general x24 -> x0, matrix products: 172 us -> none  [the longest x1 25.4 us: local(): jnp.dot(mlp_in, fc1_weight, preferred_element_type=jnp.float32) + fc1_bias]
    psum x1 -> x0, waiting for transfers between devices: 158 us -> none  [local(): branches = lax.psum(partial_value, 'tensor')]
    reduce_scatter x4 -> x0, waiting for transfers between devices: 98.1 us -> none  [the longest x1 98.1 us: local(): lax.psum_scatter(fc2_weight_grad, 'dp', scatter_dimension=1, tiled=True)]
    psum x2 -> x0, blocking collectives: 74.3 us -> none  [the longest x1 63.9 us: local(): lax.psum((gain_one, shift_one, gain_two, shift_two, qkv_bias_grad, bias_g...]
    ppermute x0 -> x27, starting transfers between devices: none -> 34.5 us  [the longest x20 22.1 us: local(): lax.ppermute(v, 'dp', [(i, i ^ 1 << b) for i in range(dp)])]
    convert_element_type x3 -> x0, other arithmetic: 34.3 us -> none  [the longest x1 29 us: attend_back(): score_grad = (weights * (weight_grad - row_dot)).astype(jnp.bfloat16)]
  transfers between devices with their start and end apart: 5 -> 27, of which waited for: 2 -> 15; matrix products, arithmetic and copies ran while one was open for 7% -> 5% of each run, Pallas kernels for 0% -> 27%
where the time goes in v1:
time: 470 us; the launch traced here: 469 us
  waiting for transfers between devices  221 us (47%)
  Pallas kernels  183 us (39%)
  starting transfers between devices  34.5 us (7%)
  other arithmetic  22.7 us (5%)
  local copies, waits for them, and re-layouts  6.71 us (1%)
    ppermute x7, waiting for transfers between devices, local(): across = lambda v: lax.ppermute(v, 'tensor', [(0, 1), (1, 0)])  117 us
    ppermute x20, waiting for transfers between devices, local(): lax.ppermute(v, 'dp', [(i, i ^ 1 << b) for i in range(dp)])  104 us
    pallas_call x4, Pallas kernels, attn(): pl.pallas_call(functools.partial(attn_body, i, KL, final), name='attn%d'...  69.1 us
    pallas_call x8, Pallas kernels, wgrad(): pl.pallas_call(functools.partial(wgrad_body, (nt,) * len(bs), keepers), n...  51.6 us
    pallas_call x2, Pallas kernels, mlp(): pl.pallas_call(functools.partial(mlp_body, prev is not None), name='mlp%d...  35.7 us
    ppermute x20, starting transfers between devices, local(): lax.ppermute(v, 'dp', [(i, i ^ 1 << b) for i in range(dp)])  22.1 us
    pallas_call x2, Pallas kernels, dgrad(): pl.pallas_call(dgrad_body, name='dgrad%d' % r0, grid=(nr,), in_specs=[pl....  13.8 us
    pallas_call x1, Pallas kernels, prologue(): pl.pallas_call(functools.partial(prologue_body, dp), name='prologue', gri...  12.6 us
  transfers between devices with their start and end apart: 27, of which 15 were waited for; matrix products, arithmetic and copies ran while one was open for 5% of the time, Pallas kernels for 27%

profile of v1, /device:TPU:0, one launch (start us, length us, event | category | flops | bytes accessed | tf_op | source)
XLA Modules:
  0.0 469.0 jit_solution(384241879337523978)
XLA Ops:
  1.9 12.6 %prologue.1 = (bf16[1024,1024]{1,0:T(8,128)(2,1)}, bf16[4,256,1024]{2,1,0:T(8,128)(2,1)}, bf16[4,256,1024]{2,1,0:T(8,128)(2,1)}, bf16[4,256,1024]{2,1,0:T(8,128)...) custom-call(bf16[1024,1024]{1,0:T(8,128)(2,1)} %x_ref.5, ...), custom_call_target="tpu_custom_call" | custom-call | flops 4294967296 | bytes 20971520 | tf_op jit(solution)/shard_map/prologue/pallas_call | solution.py:76
  14.6 10.3 %mlp0.1 = (bf16[1024,2048]{1,0:T(8,128)(2,1)}, bf16[1024,2048]{1,0:T(8,128)(2,1)}, f32[256,1024]{1,0:T(8,128)}, f32[256,1024]{1,0:T(8,128)}, f32[1,1,2048]{2,1,0:T(1,128)}) custom-call(bf16[1024,1024]{1,0:T(8,128)(2,1)} %get-tuple-element.62.refs_0_, bf16[1024,1024]{1,0:T(8,128)(2,1)} %refs_1_.3, bf16[1024,2048]{1,0:T(8,128)(2,1)} %refs_2_.3, ...), custom_call_target="tpu_custom_call" | custom-call | flops 4294967296 | bytes 16777216 | tf_op jit(solution)/shard_map/mlp0/pallas_call | solution.py:129
  24.9 25.4 %mlp1.1 = (bf16[1024,2048]{1,0:T(8,128)(2,1)}, bf16[1024,2048]{1,0:T(8,128)(2,1)}, f32[768,1024]{1,0:T(8,128)}, f32[768,1024]{1,0:T(8,128)}, f32[3,1,2048]{2,1,0:T(1,128)}) custom-call(bf16[1024,1024]{1,0:T(8,128)(2,1)} %get-tuple-element.62.refs_0_, bf16[1024,1024]{1,0:T(8,128)(2,1)} %refs_1_.3, ...), custom_call_target="tpu_custom_call", output_to_operand_aliasing={{0}: (5, {}), {1}: (6, {})} | custom-call | flops 12884901888 | bytes 16777216 | tf_op jit(solution)/shard_map/mlp1/pallas_call | solution.py:129
  50.9 7.1 %fc2_other.1 = f32[2,256,2048]{2,1,0:T(8,128)} custom-call(s32[2]{0:T(128)} %pad_add_fusion.refs_0_, bf16[4,256,1024]{2,1,0:T(8,128)(2,1)} %get-tuple-element.92.refs_1_, bf16[1024,2048]{1,0:T(8,128)(2,1)} %get-tuple-element.103.refs_2_), custom_call_target="tpu_custom_call" | custom-call | flops 2147483648 | bytes 8388608 | tf_op jit(solution)/shard_map/fc2_other/pallas_call | solution.py:282
  58.5 13.9 %attn0.1 = (bf16[8,64,256]{2,1,0:T(8,128)(2,1)}, f32[256,1024]{1,0:T(8,128)}, bf16[8,64,256]{2,1,0:T(8,128)(2,1)}, f32[8,128,512]{2,1,0:T(8,128)}) custom-call(s32[1,2]{1,0:T(1,128)} %refs_0_.7, bf16[8,192,1024]{2,1,0:T(8,128)(2,1)} %get-tuple-element.60.refs_1_, bf16[8,64,1024]{2,1,0:T(8,128)(2,1)} %bitcast.71, f32[256,1024]{1,0:T(8,128)} %get-tuple-element.63.refs_3_, ...), custom_call_target="tpu_custom_call" | custom-call | flops 3221225472 | bytes 8388608 | tf_op jit(solution)/shard_map/attn0/pallas_call | solution.py:231
  72.4 16.7 %attn1.1 = (bf16[8,64,256]{2,1,0:T(8,128)(2,1)}, f32[256,1024]{1,0:T(8,128)}, bf16[8,64,256]{2,1,0:T(8,128)(2,1)}, f32[8,128,768]{2,1,0:T(8,128)}) custom-call(s32[1,2]{1,0:T(1,128)} %refs_0_.7, bf16[8,192,1024]{2,1,0:T(8,128)(2,1)} %get-tuple-element.60.refs_1_, bf16[8,64,1024]{2,1,0:T(8,128)(2,1)} %bitcast.72, f32[768,1024]{1,0:T(8,128)} %get-tuple-element.67.refs_3_, ...), custom_call_target="tpu_custom_call" | custom-call | flops 4831838208 | bytes 8388608 | tf_op jit(solution)/shard_map/attn1/pallas_call | solution.py:231
  89.1 19.2 %attn2.1 = (bf16[8,64,256]{2,1,0:T(8,128)(2,1)}, f32[256,1024]{1,0:T(8,128)}, bf16[8,64,256]{2,1,0:T(8,128)(2,1)}, f32[8,128,1024]{2,1,0:T(8,128)}) custom-call(s32[1,2]{1,0:T(1,128)} %refs_0_.7, bf16[8,192,1024]{2,1,0:T(8,128)(2,1)} %get-tuple-element.60.refs_1_, bf16[8,64,1024]{2,1,0:T(8,128)(2,1)} %bitcast.73, f32[768,1024]{1,0:T(8,128)} %get-tuple-element.67.refs_3_, ...), custom_call_target="tpu_custom_call" | custom-call | flops 6442450944 | bytes 8388608 | tf_op jit(solution)/shard_map/attn2/pallas_call | solution.py:231
  108.2 19.3 %attn3.1 = (bf16[8,64,256]{2,1,0:T(8,128)(2,1)}, f32[256,1024]{1,0:T(8,128)}, bf16[8,192,1024]{2,1,0:T(8,128)(2,1)}) custom-call(s32[1,2]{1,0:T(1,128)} %refs_0_.7, bf16[8,192,1024]{2,1,0:T(8,128)(2,1)} %get-tuple-element.60.refs_1_, bf16[8,64,1024]{2,1,0:T(8,128)(2,1)} %bitcast.74, f32[768,1024]{1,0:T(8,128)} %get-tuple-element.67.refs_3_, ...), custom_call_target="tpu_custom_call" | custom-call | flops 6442450944 | bytes 8388608 | tf_op jit(solution)/shard_map/attn3/pallas_call | solution.py:231
  127.6 3.9 out_other.1
  131.5 5.0 %dgrad0.1 = (f32[256,1024]{1,0:T(8,128)}, f32[4,1024]{1,0:T(4,128)}, f32[1,1536]{1,0:T(1,128)}) custom-call(bf16[8,192,1024]{2,1,0:T(8,128)(2,1)} %get-tuple-element.77.pg_ref.refs_2_, bf16[1024,1536]{1,0:T(8,128)(2,1)} %w_ref.5, bf16[1024,1024]{1,0:T(8,128)(2,1)} %x_ref.5, f32[256,1024]{1,0:T(8,128)} %get-tuple-element.78.dm_ref, f32[1,1024]{1,0:T(1,128)} %bitcast.58, ...), custom_call_target="tpu_custom_call" | custom-call | flops 805306368 | bytes 12582912 | tf_op jit(solution)/shard_map/dgrad0/pallas_call | solution.py:309
  136.6 8.8 %dgrad1.1 = (f32[768,1024]{1,0:T(8,128)}, f32[4,1024]{1,0:T(4,128)}, f32[1,1536]{1,0:T(1,128)}) custom-call(bf16[8,192,1024]{2,1,0:T(8,128)(2,1)} %get-tuple-element.77.pg_ref.refs_2_, bf16[1024,1536]{1,0:T(8,128)(2,1)} %w_ref.5, bf16[1024,1024]{1,0:T(8,128)(2,1)} %x_ref.5, f32[768,1024]{1,0:T(8,128)} %get-tuple-element.80.dm_ref, f32[1,1024]{1,0:T(1,128)} %bitcast.59, ...), custom_call_target="tpu_custom_call" | custom-call | flops 2415919104 | bytes 12582912 | tf_op jit(solution)/shard_map/dgrad1/pallas_call | solution.py:309
  146.1 3.0 collective-permute-start.6
  150.9 7.2 %fc1_other.1 = f32[2,256,2048]{2,1,0:T(8,128)} custom-call(s32[2]{0:T(128)} %pad_add_fusion.refs_0_, bf16[4,256,1024]{2,1,0:T(8,128)(2,1)} %get-tuple-element.99.refs_1_, bf16[1024,2048]{1,0:T(8,128)(2,1)} %get-tuple-element.100.refs_2_), custom_call_target="tpu_custom_call" | custom-call | flops 2147483648 | bytes 8388608 | tf_op jit(solution)/shard_map/fc1_other/pallas_call | solution.py:282
  166.7 3.0 collective-permute-start.10
  173.5 6.9 %qkv_other.1 = f32[2,256,1536]{2,1,0:T(8,128)} custom-call(s32[2]{0:T(128)} %pad_add_fusion.refs_0_, bf16[4,256,1024]{2,1,0:T(8,128)(2,1)} %get-tuple-element.89.refs_1_, bf16[8,192,1024]{2,1,0:T(8,128)(2,1)} %get-tuple-element.77.pg_ref.refs_2_), custom_call_target="tpu_custom_call" | custom-call | flops 1610612736 | bytes 8388608 | tf_op jit(solution)/shard_map/qkv_other/pallas_call | solution.py:282
  180.4 15.7 %collective-permute-done.3 = f32[256,1024]{1,0:T(8,128)} collective-permute-done((f32[256,1024]{1,0:T(8,128)}, f32[256,1024]{1,0:T(8,128)}, u32[]{:S(2)}, u32[]{:S(2)}) %collective-permute-start.3) | collective-permute-done | bytes 1048608 | tf_op jit(solution)/shard_map/ppermute | solution.py:329
  197.6 20.9 %collective-permute-done.2 = f32[256,1024]{1,0:T(8,128)} collective-permute-done((f32[256,1024]{1,0:T(8,128)S(1)}, f32[256,1024]{1,0:T(8,128)}, u32[]{:S(2)}, u32[]{:S(2)}) %collective-permute-start.2) | collective-permute-done | bytes 1048608 | tf_op jit(solution)/shard_map/ppermute | solution.py:329
  220.1 20.8 %collective-permute-done.1 = f32[256,1024]{1,0:T(8,128)S(1)} collective-permute-done((f32[256,1024]{1,0:T(8,128)S(1)}, f32[256,1024]{1,0:T(8,128)S(1)}, u32[]{:S(2)}, u32[]{:S(2)}) %collective-permute-start.1) | collective-permute-done | bytes 1048608 | tf_op jit(solution)/shard_map/ppermute | solution.py:329
  243.4 4.1 out_own.1
  247.5 16.0 %collective-permute-done = f32[256,1024]{1,0:T(8,128)} collective-permute-done((f32[256,1024]{1,0:T(8,128)}, f32[256,1024]{1,0:T(8,128)}, u32[]{:S(2)}, u32[]{:S(2)}) %collective-permute-start) | collective-permute-done | bytes 1048608 | tf_op jit(solution)/shard_map/ppermute | solution.py:329
  266.8 6.1 %collective-permute-done.16 = f32[256,512]{1,0:T(8,128)S(1)} collective-permute-done((f32[256,512]{1,0:T(8,128)}, f32[256,512]{1,0:T(8,128)S(1)}, u32[]{:S(2)}, u32[]{:S(2)}) %collective-permute-start.16) | collective-permute-done | bytes 524320 | tf_op jit(solution)/shard_map/ppermute | solution.py:328
  275.2 5.7 %add_convert_fusion.5 = (bf16[256,1024]{1,0:T(8,128)(2,1)S(1)}, bf16[256,1024]{1,0:T(8,128)(2,1)S(1)}, bf16[256,1024]{1,0:T(8,128)(2,1)}, bf16[256,1024]{1,0:T(8,128)(2,1)}) fusion(f32[256,1024]{1,0:T(8,128)} %get-tuple-element.64, f32[256,1024]{1,0:T(8,128)} %collective-permute-done, f32[1024]{0:T(1024)S(1)} %copy-done.21, f32[1024]{0:T(1024)S(1)} %copy-done.22, ...), kind=kLoop, calls=%fused_computation.11 | loop fusion | flops 6291456 | bytes 12591104 | tf_op jit(solution)/shard_map/convert.2
  281.0 7.1 %qkv_own.1 = (f32[256,1536]{1,0:T(8,128)}, f32[256,1536]{1,0:T(8,128)}) custom-call(s32[2]{0:T(128)} %pad_add_fusion.refs_0_, bf16[4,256,1024]{2,1,0:T(8,128)(2,1)} %get-tuple-element.89.refs_1_, bf16[8,192,1024]{2,1,0:T(8,128)(2,1)} %get-tuple-element.77.pg_ref.refs_2_, f32[2,256,1536]{2,1,0:T(8,128)} %collective-permute-done.11.refs_3_), custom_call_target="tpu_custom_call" | custom-call | flops 1610612736 | bytes 8388608 | tf_op jit(solution)/shard_map/qkv_own/pallas_call | solution.py:282
  289.5 7.7 %fc2_own.1 = (f32[256,2048]{1,0:T(8,128)}, f32[256,2048]{1,0:T(8,128)}) custom-call(s32[2]{0:T(128)} %pad_add_fusion.refs_0_, bf16[4,256,1024]{2,1,0:T(8,128)(2,1)} %get-tuple-element.92.refs_1_, bf16[1024,2048]{1,0:T(8,128)(2,1)} %get-tuple-element.103.refs_2_, f32[2,256,2048]{2,1,0:T(8,128)} %collective-permute-done.23.refs_3_), custom_call_target="tpu_custom_call" | custom-call | flops 2147483648 | bytes 8388608 | tf_op jit(solution)/shard_map/fc2_own/pallas_call | solution.py:282
  299.5 7.7 %fc1_own.1 = (f32[256,2048]{1,0:T(8,128)}, f32[256,2048]{1,0:T(8,128)}) custom-call(s32[2]{0:T(128)} %pad_add_fusion.refs_0_, bf16[4,256,1024]{2,1,0:T(8,128)(2,1)} %get-tuple-element.99.refs_1_, bf16[1024,2048]{1,0:T(8,128)(2,1)} %get-tuple-element.100.refs_2_, f32[2,256,2048]{2,1,0:T(8,128)} %collective-permute-done.19.refs_3_), custom_call_target="tpu_custom_call" | custom-call | flops 2147483648 | bytes 8388608 | tf_op jit(solution)/shard_map/fc1_own/pallas_call | solution.py:282
  307.1 42.7 %collective-permute-done.4 = f32[256,1024]{1,0:T(8,128)} collective-permute-done((f32[256,1024]{1,0:T(8,128)}, f32[256,1024]{1,0:T(8,128)}, u32[]{:S(2)}, u32[]{:S(2)}) %collective-permute-start.4) | collective-permute-done | bytes 1048608 | tf_op jit(solution)/shard_map/ppermute | solution.py:329
  356.2 5.4 %collective-permute-done.18 = f32[1,64,512]{2,1,0:T(8,128)S(1)} collective-permute-done((f32[1,64,512]{2,1,0:T(8,128)S(1)}, f32[1,64,512]{2,1,0:T(8,128)S(1)}, u32[]{:S(2)}, u32[]{:S(2)}) %collective-permute-start.18) | collective-permute-done | bytes 131104 | tf_op jit(solution)/shard_map/ppermute | solution.py:328
  365.3 2.9 add_convert_fusion
  374.1 32.4 %collective-permute-done.20 = f32[256,2048]{1,0:T(8,128)S(1)} collective-permute-done((f32[256,2048]{1,0:T(8,128)}, f32[256,2048]{1,0:T(8,128)S(1)}, u32[]{:S(2)}, u32[]{:S(2)}) %collective-permute-start.20) | collective-permute-done | bytes 2097184 | tf_op jit(solution)/shard_map/ppermute | solution.py:328
  409.3 2.6 collective-permute-start.26
  411.9 31.6 %collective-permute-done.21 = f32[2,64,2048]{2,1,0:T(8,128)S(1)} collective-permute-done((f32[2,64,2048]{2,1,0:T(8,128)S(1)}, f32[2,64,2048]{2,1,0:T(8,128)S(1)}, u32[]{:S(2)}, u32[]{:S(2)}) %collective-permute-start.21) | collective-permute-done | bytes 1048608 | tf_op jit(solution)/shard_map/ppermute | solution.py:328
  445.5 22.1 %collective-permute-done.22 = f32[1,64,2048]{2,1,0:T(8,128)S(1)} collective-permute-done((f32[1,64,2048]{2,1,0:T(8,128)S(1)}, f32[1,64,2048]{2,1,0:T(8,128)S(1)}, u32[]{:S(2)}, u32[]{:S(2)}) %collective-permute-start.22) | collective-permute-done | bytes 524320 | tf_op jit(solution)/shard_map/ppermute | solution.py:328
  (127 shorter events, 54.2 us)
Async XLA Ops:
  58.0 231.5 %collective-permute-start.23 = (f32[2,256,2048]{2,1,0:T(8,128)}, f32[2,256,2048]{2,1,0:T(8,128)}, u32[]{:S(2)}, u32[]{:S(2)}) collective-permute-start(f32[2,256,2048]{2,1,0:T(8,128)} %fc2_other.1), channel_id=1, source_target_pairs={{0,2},{2,0},{4,6},{6,4},{8,10},{10,8},{12,14},{14,12},{16,18},{18,... | collective-permute-start | bytes 12582920 | tf_op jit(solution)/shard_map/ppermute | solution.py:328
  131.4 48.9 %collective-permute-start.15 = (f32[2,256,512]{2,1,0:T(8,128)}, f32[2,256,512]{2,1,0:T(8,128)S(1)}, u32[]{:S(2)}, u32[]{:S(2)}) collective-permute-start(f32[2,256,512]{2,1,0:T(8,128)} %out_other.1), channel_id=1, source_target_pairs={{0,2},{2,0},{4,6},{6,4},{8,10},{10,8},{12,14},{14,12},{16,18},{18,... | collective-permute-start | bytes 3145736 | tf_op jit(solution)/shard_map/ppermute | solution.py:328
  146.1 4.7 %collective-permute-start.6 = (f32[4096]{0:T(1024)S(1)}, f32[4096]{0:T(1024)S(1)}, u32[]{:S(2)}, u32[]{:S(2)}) collective-permute-start(f32[4096]{0:T(1024)S(1)} %bitcast.65), channel_id=1, source_target_pairs={{0,1},{1,0},{2,3},{3,2},{4,5},{5,4},{6,7},{7,6},{8,9},{9,8},{10,11... | collective-permute-start | bytes 49160 | tf_op jit(solution)/shard_map/ppermute | solution.py:329
  150.8 7.8 %collective-permute-start.7 = (f32[8704]{0:T(1024)S(1)}, f32[8704]{0:T(1024)S(1)}, u32[]{:S(2)}, u32[]{:S(2)}) collective-permute-start(f32[8704]{0:T(1024)S(1)} %pad_maximum_fusion.2), channel_id=1, source_target_pairs={{0,2},{2,0},{4,6},{6,4},{8,10},{10,8},{12,14},{14,12},{16,18},{18,... | collective-permute-start | bytes 104456 | tf_op jit(solution)/shard_map/ppermute | solution.py:328
  158.1 139.7 %collective-permute-start.19 = (f32[2,256,2048]{2,1,0:T(8,128)}, f32[2,256,2048]{2,1,0:T(8,128)}, u32[]{:S(2)}, u32[]{:S(2)}) collective-permute-start(f32[2,256,2048]{2,1,0:T(8,128)} %fc1_other.1), channel_id=1, source_target_pairs={{0,2},{2,0},{4,6},{6,4},{8,10},{10,8},{12,14},{14,12},{16,18},{18,... | collective-permute-start | bytes 12582920 | tf_op jit(solution)/shard_map/ppermute | solution.py:328
  158.6 4.0 collective-permute-start.8
  162.7 4.0 collective-permute-start.9
  166.7 5.0 %collective-permute-start.10 = (f32[8704]{0:T(1024)S(1)}, f32[8704]{0:T(1024)S(1)}, u32[]{:S(2)}, u32[]{:S(2)}) collective-permute-start(f32[8704]{0:T(1024)S(1)} %add.208), channel_id=1, source_target_pairs={{0,16},{2,18},{4,20},{6,22},{8,24},{10,26},{12,28},{14,30},{16,0},... | collective-permute-start | bytes 104456 | tf_op jit(solution)/shard_map/ppermute | solution.py:328
  169.7 26.3 %collective-permute-start.3 = (f32[256,1024]{1,0:T(8,128)}, f32[256,1024]{1,0:T(8,128)}, u32[]{:S(2)}, u32[]{:S(2)}) collective-permute-start(f32[256,1024]{1,0:T(8,128)} %get-tuple-element.76), channel_id=1, source_target_pairs={{0,1},{1,0},{2,3},{3,2},{4,5},{5,4},{6,7},{7,6},{8,9},{9,8},{10,11... | collective-permute-start | bytes 3145736 | tf_op jit(solution)/shard_map/ppermute | solution.py:329
  171.7 46.9 %collective-permute-start.2 = (f32[256,1024]{1,0:T(8,128)S(1)}, f32[256,1024]{1,0:T(8,128)}, u32[]{:S(2)}, u32[]{:S(2)}) collective-permute-start(f32[256,1024]{1,0:T(8,128)S(1)} %copy-done.10), channel_id=1, source_target_pairs={{0,1},{1,0},{2,3},{3,2},{4,5},{5,4},{6,7},{7,6},{8,9},{9,8},{10,11... | collective-permute-start | bytes 3145736 | tf_op jit(solution)/shard_map/ppermute | solution.py:329
  180.4 63.0 %copy-start.8 = (f32[2,256,512]{2,1,0:T(8,128)}, f32[2,256,512]{2,1,0:T(8,128)S(1)}, u32[]{:S(2)}) copy-start(f32[2,256,512]{2,1,0:T(8,128)S(1)} %collective-permute-done.15.refs_6_) | copy-start | bytes 3145732
  180.4 100.6 %collective-permute-start.11 = (f32[2,256,1536]{2,1,0:T(8,128)}, f32[2,256,1536]{2,1,0:T(8,128)}, u32[]{:S(2)}, u32[]{:S(2)}) collective-permute-start(f32[2,256,1536]{2,1,0:T(8,128)} %qkv_other.1), channel_id=1, source_target_pairs={{0,2},{2,0},{4,6},{6,4},{8,10},{10,8},{12,14},{14,12},{16,18},{18,... | collective-permute-start | bytes 9437192 | tf_op jit(solution)/shard_map/ppermute | solution.py:328
  196.1 44.8 %collective-permute-start.1 = (f32[256,1024]{1,0:T(8,128)S(1)}, f32[256,1024]{1,0:T(8,128)S(1)}, u32[]{:S(2)}, u32[]{:S(2)}) collective-permute-start(f32[256,1024]{1,0:T(8,128)S(1)} %copy-done.9), channel_id=1, source_target_pairs={{0,1},{1,0},{2,3},{3,2},{4,5},{5,4},{6,7},{7,6},{8,9},{9,8},{10,11... | collective-permute-start | bytes 3145736 | tf_op jit(solution)/shard_map/ppermute | solution.py:329
  218.5 44.9 %collective-permute-start = (f32[256,1024]{1,0:T(8,128)}, f32[256,1024]{1,0:T(8,128)}, u32[]{:S(2)}, u32[]{:S(2)}) collective-permute-start(f32[256,1024]{1,0:T(8,128)} %get-tuple-element.64), channel_id=1, source_target_pairs={{0,1},{1,0},{2,3},{3,2},{4,5},{5,4},{6,7},{7,6},{8,9},{9,8},{10,11... | collective-permute-start | bytes 3145736 | tf_op jit(solution)/shard_map/ppermute | solution.py:329
  241.9 33.3 %copy-start.21 = (f32[1024]{0:T(1024)S(1)}, f32[1024]{0:T(1024)}, u32[]{:S(2)}) copy-start(f32[1024]{0:T(1024)} %param.30) | copy-start | bytes 12292
  241.9 33.3 %copy-start.22 = (f32[1024]{0:T(1024)S(1)}, f32[1024]{0:T(1024)}, u32[]{:S(2)}) copy-start(f32[1024]{0:T(1024)} %param.26) | copy-start | bytes 12292
  241.9 122.7 %collective-permute-start.5 = (f32[768,1024]{1,0:T(8,128)}, f32[768,1024]{1,0:T(8,128)}, u32[]{:S(2)}, u32[]{:S(2)}) collective-permute-start(f32[768,1024]{1,0:T(8,128)} %get-tuple-element.81), channel_id=1, source_target_pairs={{0,1},{1,0},{2,3},{3,2},{4,5},{5,4},{6,7},{7,6},{8,9},{9,8},{10,11... | collective-permute-start | bytes 9437192 | tf_op jit(solution)/shard_map/ppermute | solution.py:329
  263.5 9.4 %collective-permute-start.16 = (f32[256,512]{1,0:T(8,128)}, f32[256,512]{1,0:T(8,128)S(1)}, u32[]{:S(2)}, u32[]{:S(2)}) collective-permute-start(f32[256,512]{1,0:T(8,128)} %get-tuple-element.98), channel_id=1, source_target_pairs={{0,4},{2,6},{4,0},{6,2},{8,12},{10,14},{12,8},{14,10},{16,20},{18,... | collective-permute-start | bytes 1572872 | tf_op jit(solution)/shard_map/ppermute | solution.py:328
  266.8 201.6 %copy-start.18 = (f32[1024]{0:T(1024)}, f32[1024]{0:T(1024)S(1)}, u32[]{:S(2)}) copy-start(f32[1024]{0:T(1024)S(1)} %get-tuple-element.142) | copy-start | bytes 12292
  273.7 76.2 %collective-permute-start.4 = (f32[256,1024]{1,0:T(8,128)}, f32[256,1024]{1,0:T(8,128)}, u32[]{:S(2)}, u32[]{:S(2)}) collective-permute-start(f32[256,1024]{1,0:T(8,128)} %get-tuple-element.79), channel_id=1, source_target_pairs={{0,1},{1,0},{2,3},{3,2},{4,5},{5,4},{6,7},{7,6},{8,9},{9,8},{10,11... | collective-permute-start | bytes 3145736 | tf_op jit(solution)/shard_map/ppermute | solution.py:329
  288.1 74.2 %collective-permute-start.12 = (f32[256,1536]{1,0:T(8,128)}, f32[256,1536]{1,0:T(8,128)}, u32[]{:S(2)}, u32[]{:S(2)}) collective-permute-start(f32[256,1536]{1,0:T(8,128)} %get-tuple-element.91), channel_id=1, source_target_pairs={{0,4},{2,6},{4,0},{6,2},{8,12},{10,14},{12,8},{14,10},{16,20},{18,... | collective-permute-start | bytes 4718600 | tf_op jit(solution)/shard_map/ppermute | solution.py:328
  297.2 73.2 %collective-permute-start.24 = (f32[256,2048]{1,0:T(8,128)}, f32[256,2048]{1,0:T(8,128)S(1)}, u32[]{:S(2)}, u32[]{:S(2)}) collective-permute-start(f32[256,2048]{1,0:T(8,128)} %get-tuple-element.105), channel_id=1, source_target_pairs={{0,4},{2,6},{4,0},{6,2},{8,12},{10,14},{12,8},{14,10},{16,20},{18,... | collective-permute-start | bytes 6291464 | tf_op jit(solution)/shard_map/ppermute | solution.py:328
  297.8 55.4 %collective-permute-start.17 = (f32[2,64,512]{2,1,0:T(8,128)S(1)}, f32[2,64,512]{2,1,0:T(8,128)}, u32[]{:S(2)}, u32[]{:S(2)}) collective-permute-start(f32[2,64,512]{2,1,0:T(8,128)S(1)} %dynamic-slice_bitcast_fusion.3), channel_id=1, source_target_pairs={{0,8},{2,10},{4,12},{6,14},{8,0},{10,2},{12,4},{14,6},{16,24},{18,... | collective-permute-start | bytes 786440 | tf_op jit(solution)/shard_map/ppermute | solution.py:328
  349.8 56.6 %collective-permute-start.20 = (f32[256,2048]{1,0:T(8,128)}, f32[256,2048]{1,0:T(8,128)S(1)}, u32[]{:S(2)}, u32[]{:S(2)}) collective-permute-start(f32[256,2048]{1,0:T(8,128)} %get-tuple-element.102), channel_id=1, source_target_pairs={{0,4},{2,6},{4,0},{6,2},{8,12},{10,14},{12,8},{14,10},{16,20},{18,... | collective-permute-start | bytes 6291464 | tf_op jit(solution)/shard_map/ppermute | solution.py:328
  354.3 7.3 %collective-permute-start.18 = (f32[1,64,512]{2,1,0:T(8,128)S(1)}, f32[1,64,512]{2,1,0:T(8,128)S(1)}, u32[]{:S(2)}, u32[]{:S(2)}) collective-permute-start(f32[1,64,512]{2,1,0:T(8,128)S(1)} %constant_dynamic-slice_fusion.2), channel_id=1, source_target_pairs={{0,16},{2,18},{4,20},{6,22},{8,24},{10,26},{12,28},{14,30},{16,0},... | collective-permute-start | bytes 393224 | tf_op jit(solution)/shard_map/ppermute | solution.py:328
  364.2 44.3 %collective-permute-start.13 = (f32[2,64,1536]{2,1,0:T(8,128)S(1)}, f32[2,64,1536]{2,1,0:T(8,128)S(1)}, u32[]{:S(2)}, u32[]{:S(2)}) collective-permute-start(f32[2,64,1536]{2,1,0:T(8,128)S(1)} %dynamic-slice_bitcast_fusion.2), channel_id=1, source_target_pairs={{0,8},{2,10},{4,12},{6,14},{8,0},{10,2},{12,4},{14,6},{16,24},{18,... | collective-permute-start | bytes 2359304 | tf_op jit(solution)/shard_map/ppermute | solution.py:328
  370.9 35.6 %copy-start.3 = (f32[256,2048]{1,0:T(8,128)S(1)}, f32[256,2048]{1,0:T(8,128)}, u32[]{:S(2)}) copy-start(f32[256,2048]{1,0:T(8,128)} %get-tuple-element.101) | copy-start | bytes 6291460
  370.9 38.2 %collective-permute-start.25 = (f32[2,64,2048]{2,1,0:T(8,128)S(1)}, f32[2,64,2048]{2,1,0:T(8,128)S(1)}, u32[]{:S(2)}, u32[]{:S(2)}) collective-permute-start(f32[2,64,2048]{2,1,0:T(8,128)S(1)} %dynamic-slice_bitcast_fusion), channel_id=1, source_target_pairs={{0,8},{2,10},{4,12},{6,14},{8,0},{10,2},{12,4},{14,6},{16,24},{18,... | collective-permute-start | bytes 3145736 | tf_op jit(solution)/shard_map/ppermute | solution.py:328
  406.9 36.6 %collective-permute-start.21 = (f32[2,64,2048]{2,1,0:T(8,128)S(1)}, f32[2,64,2048]{2,1,0:T(8,128)S(1)}, u32[]{:S(2)}, u32[]{:S(2)}) collective-permute-start(f32[2,64,2048]{2,1,0:T(8,128)S(1)} %dynamic-slice_bitcast_fusion.1), channel_id=1, source_target_pairs={{0,8},{2,10},{4,12},{6,14},{8,0},{10,2},{12,4},{14,6},{16,24},{18,... | collective-permute-start | bytes 3145736 | tf_op jit(solution)/shard_map/ppermute | solution.py:328
  408.7 35.1 %collective-permute-start.14 = (f32[1,64,1536]{2,1,0:T(8,128)S(1)}, f32[1,64,1536]{2,1,0:T(8,128)S(1)}, u32[]{:S(2)}, u32[]{:S(2)}) collective-permute-start(f32[1,64,1536]{2,1,0:T(8,128)S(1)} %constant_dynamic-slice_fusion.3), channel_id=1, source_target_pairs={{0,16},{2,18},{4,20},{6,22},{8,24},{10,26},{12,28},{14,30},{16,0},... | collective-permute-start | bytes 1179656 | tf_op jit(solution)/shard_map/ppermute | solution.py:328
  409.3 35.3 %collective-permute-start.26 = (f32[1,64,2048]{2,1,0:T(8,128)S(1)}, f32[1,64,2048]{2,1,0:T(8,128)S(1)}, u32[]{:S(2)}, u32[]{:S(2)}) collective-permute-start(f32[1,64,2048]{2,1,0:T(8,128)S(1)} %constant_dynamic-slice_fusion), channel_id=1, source_target_pairs={{0,16},{2,18},{4,20},{6,22},{8,24},{10,26},{12,28},{14,30},{16,0},... | collective-permute-start | bytes 1572872 | tf_op jit(solution)/shard_map/ppermute | solution.py:328
  443.7 23.8 %collective-permute-start.22 = (f32[1,64,2048]{2,1,0:T(8,128)S(1)}, f32[1,64,2048]{2,1,0:T(8,128)S(1)}, u32[]{:S(2)}, u32[]{:S(2)}) collective-permute-start(f32[1,64,2048]{2,1,0:T(8,128)S(1)} %constant_dynamic-slice_fusion.1), channel_id=1, source_target_pairs={{0,16},{2,18},{4,20},{6,22},{8,24},{10,26},{12,28},{14,30},{16,0},... | collective-permute-start | bytes 1572872 | tf_op jit(solution)/shard_map/ppermute | solution.py:328
  (18 other events, 182.7 us)

commit v2 on v1

v2 whole, which is shorter than its diff:
```python
import functools
import math

import numpy as np
import jax, jax.numpy as jnp
from jax import lax
from jax.sharding import PartitionSpec as P
from jax.experimental import pallas as pl
from jax.experimental.pallas import tpu as pltpu

HD=64; ROT=16; PIECE=256; EPS=1e-5; MASKED=-1e30
F32=jnp.float32; BF=jnp.bfloat16
TB=256
SUB=256

def dot(a,b): return jnp.dot(a,b,preferred_element_type=F32)
def dot_nt(a,b): return lax.dot_general(a,b,(((1,),(1,)),((),())),preferred_element_type=F32)
def dot_tn(a,b): return lax.dot_general(a,b,(((0,),(0,)),((),())),preferred_element_type=F32)

def normalize(x):
    xf=x.astype(F32)
    c=xf-jnp.mean(xf,axis=1,keepdims=True)
    inv=lax.rsqrt(jnp.mean(c*c,axis=1,keepdims=True)+EPS)
    return c*inv, inv

def prologue_body(dp, x_ref,g_ref,g1,b1,g2,b2,w_ref,bq_ref,wo_ref,cos_ref,sin_ref,
             m_out,aT_out,mT_out,gT_out,qkv_out,do_out,gsum_out,wT,bcol):
    step=pl.program_id(0)
    @pl.when(step==0)
    def _():
        wT[...]=w_ref[...].T
        bcol[...]=jnp.broadcast_to(bq_ref[...],(128,bq_ref.shape[1])).T
        gsum_out[...]=jnp.zeros_like(gsum_out)
    d=x_ref.shape[1]
    rows=d//dp
    normed,_=normalize(x_ref[...])
    a=normed*g1[...]+b1[...]
    m=normed*g2[...]+b2[...]
    m_out[...]=m.astype(BF)
    bits=dp.bit_length()-1
    def perm(t,order):
        blocks=[]
        for p in range(dp):
            i=0
            for j,b in enumerate(order):
                i+=((p>>(bits-1-j))&1)<<b
            blocks.append(t[i*rows:(i+1)*rows])
        t=jnp.concatenate(blocks,axis=0)
        return [t[j*(d//4):(j+1)*(d//4)] for j in range(4)]
    order=orders(bits)
    aT=a.T
    mT=m.T
    gf=g_ref[...].astype(F32)
    gsum_out[...]+=jnp.sum(gf,axis=0,keepdims=True)
    gT=gf.T
    for t,o,w in ((aT,aT_out,"qkv"),(mT,mT_out,"fc1"),(gT,gT_out,"fc2")):
        for j,pt in enumerate(perm(t,order[w])):
            o[j]=pt.astype(BF)
    packed=dot(wT[...],aT.astype(BF))
    do_out[...]=dot(wo_ref[...],gT.astype(BF)).astype(BF)
    c=cos_ref[...]; s=sin_ref[...]
    heads=qkv_out.shape[0]
    b2c=jnp.concatenate([bcol[...]]*(TB//128),axis=1)
    packed=packed+b2c
    for h in range(heads):
        base=h*3*HD
        for part in range(3):
            blk=packed[base+part*HD:base+(part+1)*HD]
            if part<2:
                a1=blk[0:8]; a2=blk[8:16]
                blk=jnp.concatenate([a1*c-a2*s,a2*c+a1*s,blk[16:]],axis=0)
            if part==0: blk=blk*(1.0/math.sqrt(HD))
            qkv_out[h,part*HD:(part+1)*HD]=blk.astype(BF)

def prologue(dp,x,g,g1,b1,g2,b2,w,bq,wo,cos,sin):
    n,d=x.shape; c=w.shape[1]; inner=wo.shape[0]; heads=c//(3*HD)
    row=lambda v: v.reshape(1,-1)
    full=lambda a: pl.BlockSpec(a.shape,lambda i:(0,)*a.ndim)
    tspec=pl.BlockSpec((4,d//4,TB),lambda i:(0,0,i))
    args=(x,g,row(g1),row(b1),row(g2),row(b2),w,row(bq),wo,cos,sin)
    xs=pl.BlockSpec((TB,d),lambda i:(i,0))
    ts=pl.BlockSpec((8,TB),lambda i:(0,i))
    return pl.pallas_call(functools.partial(prologue_body,dp),name="prologue",
        grid=(n//TB,),
        in_specs=[xs,xs]+[full(a) for a in args[2:9]]+[ts,ts],
        out_specs=[xs,tspec,tspec,tspec,pl.BlockSpec((heads,3*HD,TB),lambda i:(0,0,i)),
                   pl.BlockSpec((inner,TB),lambda i:(0,i)),pl.BlockSpec((1,d),lambda i:(0,0))],
        out_shape=[jax.ShapeDtypeStruct((n,d),BF)]+[jax.ShapeDtypeStruct((4,d//4,n),BF)]*3+
            [jax.ShapeDtypeStruct((heads,3*HD,n),BF),jax.ShapeDtypeStruct((inner,n),BF),jax.ShapeDtypeStruct((1,d),F32)],
        scratch_shapes=[pltpu.VMEM((c,d),BF),pltpu.VMEM((c,128),F32)],
        compiler_params=pltpu.CompilerParams(vmem_limit_bytes=60*2**20),
        cost_estimate=pl.CostEstimate(flops=2*n*d*(c+inner),bytes_accessed=20*2**20,transcendentals=0),
    )(*args)


CW=512
WEIGHTS=("fc2","fc1","out","qkv")

def orders(bits):
    up=list(range(bits))
    return {"fc2":up,"out":up,"fc1":up,"qkv":up[:1]+up[2:]+up[1:2]}

def mega_body(names,bits,dims,*refs):
    r=dict(zip(names,refs))
    class R: pass
    v=R(); v.__dict__.update(r)
    n,d,ff,inner,c,heads=dims
    nb=n//TB; quarter=d//4
    cols={"fc2":ff,"fc1":ff,"out":inner,"qkv":c}
    order=orders(bits)
    idx=lax.axis_index("dp"); ten=lax.axis_index("tensor")
    bit=[(idx//(1<<b))%2 for b in range(bits)]
    peer=[{"dp":idx+(1-2*bit[b])*(1<<b)} for b in range(bits)]
    twin={"tensor":1-ten}
    MESH=pl.DeviceIdType.MESH
    def load(src,dst,sem):
        cp=pltpu.make_async_copy(src,dst,sem); cp.start(); return cp
    def remote(src,dst,ss,rs,dev):
        return pltpu.make_async_remote_copy(src_ref=src,dst_ref=dst,send_sem=ss,recv_sem=rs,device_id=dev,device_id_type=MESH)

    L={}
    def fetch(key,src,dst,k): L[key]=load(src,dst,v.lsem.at[k])
    rowsl=lambda i: pl.ds(i*TB,TB)
    fetch("m0",v.m.at[rowsl(0)],v.mbuf.at[0],0)
    fetch("g0",v.g.at[rowsl(0)],v.gbuf.at[0],1)
    fetch("w1",v.w1,v.w1v,2); fetch("w2",v.w2,v.w2v,3)
    fetch("qkv",v.qkv,v.qv,4); fetch("do",v.do,v.dov,5)
    fetch("wo",v.wo,v.wov,6); fetch("w",v.w,v.wv,7)
    bar=pltpu.get_barrier_semaphore()
    for dev in [twin]+peer: pl.semaphore_signal(bar,inc=1,device_id=dev,device_id_type=MESH)
    pl.semaphore_wait(bar,bits+1)

    def wait(key): L.pop(key).wait()

    def mlp(i):
        s=i%2
        wait("m%d"%i); wait("g%d"%i)
        if i+1<nb:
            fetch("m%d"%(i+1),v.m.at[rowsl(i+1)],v.mbuf.at[1-s],8+2*(1-s))
            fetch("g%d"%(i+1),v.g.at[rowsl(i+1)],v.gbuf.at[1-s],9+2*(1-s))
        if i==0: wait("w1"); wait("w2")
        r0=i*TB
        mi=v.mbuf.at[s]; gi=v.gbuf.at[s]
        @pl.loop(0,ff//CW)
        def _(f):
            for j in range(CW//SUB):
                sl=pl.ds(pl.multiple_of(f*CW+j*SUB,SUB),SUB)
                u=dot(mi[...],v.w1v[:,sl])+v.b1[:,sl]
                hb=dot_nt(gi[...],v.w2v[sl,:])
                cum=0.5*(1.0+lax.erf(u*(1.0/math.sqrt(2.0))))
                den=jnp.exp(-0.5*u*u)*(1.0/math.sqrt(2.0*math.pi))
                v.act[r0:r0+TB,sl]=(u*cum).astype(BF)
                pg=(hb*(cum+u*den)).astype(BF)
                v.pg[r0:r0+TB,sl]=pg
                bs=jnp.sum(pg.astype(F32),axis=0,keepdims=True)
                if i==0: v.fb[:,sl]=bs
                else: v.fb[:,sl]+=bs
        @pl.loop(0,d//CW)
        def _(f):
            sl=pl.ds(pl.multiple_of(f*CW,CW),CW)
            v.part[r0:r0+TB,sl]=dot(v.act[r0:r0+TB,:],v.w2v[:,sl])
            v.e[r0:r0+TB,sl]=dot_nt(v.pg[r0:r0+TB,:],v.w1v[sl,:])

    def back(b,cc,s):
        b1=b[0:8]; b2=b[8:16]
        return jnp.concatenate([b1*cc+b2*s,b2*cc-b1*s,b[16:]],axis=0)

    def attn(i):
        KL=min((i+2)*TB,n); W0=i*TB; WN=KL-W0
        kp=W0+lax.broadcasted_iota(jnp.int32,(WN,TB),0)
        qp=W0+lax.broadcasted_iota(jnp.int32,(WN,TB),1)
        ok=kp<=qp
        for p in range(v.starts.shape[1]):
            s=v.starts[0,p]
            ok=ok|((kp>=s)&(kp<s+PIECE)&(qp>=s)&(qp<s+PIECE))
        v.bias[0:WN]=jnp.where(ok,0.0,MASKED)
        if i==0: wait("qkv"); wait("do")
        @pl.loop(0,heads)
        def _(h):
            qT=v.qv[h,0:HD,W0:W0+TB]
            kT=v.qv[h,HD:2*HD,0:KL]
            vT=v.qv[h,2*HD:3*HD,0:KL]
            doT=v.dov[h,:,W0:W0+TB]
            k=kT.T; vv=vT.T
            S=dot(k,qT)
            if W0>0: S=jnp.concatenate([S[:W0],S[W0:]+v.bias[0:WN]],axis=0)
            else: S=S+v.bias[0:WN]
            mx=jnp.max(S,axis=0,keepdims=True)
            e=jnp.exp(S-mx)
            inv=1.0/jnp.sum(e,axis=0,keepdims=True)
            p=e*inv
            pb=p.astype(BF)
            dP=dot(vv,doT)
            v.o[h,:,W0:W0+TB]=dot(vT,pb).astype(BF)
            rd=jnp.sum(p*dP,axis=0,keepdims=True)
            ds=(p*(dP-rd)).astype(BF)
            dq=dot(kT,ds)
            v.pgT[h,0:HD,W0:W0+TB]=back(dq*(1.0/math.sqrt(HD)),v.cos[:,W0:W0+TB],v.sin[:,W0:W0+TB]).astype(BF)
            dk=dot_nt(qT,ds)
            dv=dot_nt(doT,pb)
            nh=n//CW
            for t in range(nh):
                lo=t*CW; hi=min(KL,lo+CW)
                at=h*nh+t
                for j,x in ((0,dk),(1,dv)):
                    rs=slice(j*HD,(j+1)*HD)
                    if i==0:
                        if lo>=KL: v.acc[at,rs]=jnp.zeros((HD,CW),F32)
                        else:
                            v.acc[at,rs,0:hi-lo]=x[:,lo:hi]
                            if hi-lo<CW: v.acc[at,rs,hi-lo:CW]=jnp.zeros((HD,CW-hi+lo),F32)
                    elif lo<KL:
                        if i<nb-1: v.acc[at,rs,0:hi-lo]+=x[:,lo:hi]
                        else:
                            tot=v.acc[at,rs]+x[:,lo:hi]
                            if j==0: tot=back(tot,v.cos[:,lo:hi],v.sin[:,lo:hi])
                            v.pgT[h,(1+j)*HD:(2+j)*HD,lo:hi]=tot.astype(BF)
        if i==0: wait("wo")
        oc=v.o[:,:,W0:W0+TB].reshape(inner,TB)
        v.part[W0:W0+TB]+=dot_tn(oc,v.wov[...])

    Y={}
    def ysend(kind,i):
        src,dst=(v.part,v.yrecv) if kind=="p" else (v.e,v.erecv)
        k=i if kind=="p" else nb+i
        cp=remote(src.at[rowsl(i)],dst.at[rowsl(i)],v.ysend.at[k],v.yrecv_sem.at[k],twin)
        cp.start(); Y[kind,i]=cp
    def yfinish(kind,i):
        if kind=="p": fetch("res",v.x.at[rowsl(i)],v.mbuf.at[0],8)
        else: fetch("res",v.g.at[rowsl(i)],v.mbuf.at[0],8)
        cp=Y.pop((kind,i)); cp.wait()
        mine,recv,out=(v.part,v.yrecv,v.hidden) if kind=="p" else (v.e,v.erecv,v.hgrad)
        fetch("recv",recv.at[rowsl(i)],v.fbuf,10)
        wait("res"); wait("recv")
        t=v.mbuf[0].astype(F32)+(mine[i*TB:(i+1)*TB]+v.fbuf[...])
        if kind=="p": t=t+v.bias_out[...]
        v.gbuf[0]=t.astype(BF)
        fetch("st",v.gbuf.at[0],out.at[rowsl(i)],11)
        wait("st")

    def rhs(w,cb):
        cs=pl.ds(pl.multiple_of(cb*CW,CW),CW)
        if w=="fc2": return v.act[:,cs],False
        if w=="fc1": return v.pg[:,cs],False
        if w=="out": return v.o[...].reshape(inner,n),True
        return None,True
    lhs={"fc2":v.gT,"out":v.gT,"fc1":v.mT,"qkv":v.aT}
    per=CW//HD
    def product(w,a,cb):
        if w=="qkv":
            b=v.pgF[pl.ds(pl.multiple_of(cb*CW,CW),CW),:]
            return dot_nt(a,b)
        b,nt=rhs(w,cb)
        return dot_nt(a,b) if nt else dot(a,b)
    C0={}
    def other(w):
        nc=cols[w]//CW
        b0=order[w][0]
        cp=load(lhs[w].at[pl.ds(2*(1-bit[b0]),2)],v.abuf,v.lsem.at[12]); cp.wait()
        dst=getattr(v,"r0_"+w)
        def send(t,slot):
            xi=t//nc; cb=t%nc
            return remote(v.ring.at[slot],dst.at[xi,:,pl.ds(pl.multiple_of(cb*CW,CW),CW)],v.csend.at[slot],v.crecv.at[WEIGHTS.index(w)],peer[b0])
        @pl.loop(0,2*nc)
        def _(t):
            slot=t%2
            @pl.when(t>=2)
            def _(): send(t,slot).wait_send()
            v.ring[slot]=product(w,v.abuf[t//nc],t%nc)
            send(t,slot).start()
        for slot in range(2): send(slot,slot).wait_send()
    def sent(w,j,dev_bit):
        s=getattr(v,"s%d_"%j+w); q=getattr(v,"r%d_"%j+w)
        k=WEIGHTS.index(w)*(bits-1)+j-1
        return remote(s,q,v.xsend.at[k],v.xrecv.at[k],peer[dev_bit])
    def own(w):
        nc=cols[w]//CW
        o=order[w]; b0,b1=o[0],o[1]
        r0=getattr(v,"r0_"+w)
        cp=load(lhs[w].at[pl.ds(2*bit[b0],2)],v.abuf,v.lsem.at[12])
        remote(r0,r0,v.csend.at[0],v.crecv.at[WEIGHTS.index(w)],peer[b0]).wait_recv()
        cp.wait()
        def place(ref,cb):
            return ref.at[:,:,pl.ds(pl.multiple_of(cb*CW,CW),CW)] if len(ref.shape)==3 else ref.at[:,pl.ds(pl.multiple_of(cb*CW,CW),CW)]
        for which in range(2):
            xi=(1-bit[b1]) if which==0 else bit[b1]
            ref=getattr(v,("s1_" if which==0 else "k1_")+w)
            hh=ref.shape[-2]
            def get(cb,slot): return pltpu.make_async_copy(r0.at[xi,:,pl.ds(pl.multiple_of(cb*CW,CW),CW)],v.rin.at[slot],v.osem.at[slot])
            def put(cb,slot): return pltpu.make_async_copy(v.ring2.at[slot] if len(ref.shape)==3 else v.ring2.at[slot,0],place(ref,cb),v.osem.at[2+slot])
            get(0,0).start()
            @pl.loop(0,nc)
            def _(t):
                slot=t%2
                @pl.when(t+1<nc)
                def _(): get(t+1,1-slot).start()
                y=product(w,v.abuf[xi],t)
                get(t,slot).wait()
                @pl.when(t>=2)
                def _(): put(t,slot).wait()
                y=y+v.rin[slot]
                v.ring2[slot]=y.reshape(2,quarter//2,CW)
                put(t,slot).start()
            for t in range(max(0,nc-2),nc): put(t,t%2).wait()
            if which==0: sent(w,1,b1).start()
    def stage(w,j):
        nc=cols[w]//CW; o=order[w]
        cp=sent(w,j,o[j])
        k=getattr(v,"k%d_"%j+w); q=getattr(v,"r%d_"%j+w)
        last=j==bits-1
        half=k.shape[-2]
        def cut(ref,t): return ref.at[:,pl.ds(t*CW,CW)] if last else ref.at[:,:,pl.ds(t*CW,CW)]
        def buf(base,t): return v.acc.at[base+2*t,0:half] if last else v.acc.at[base+2*t:base+2*t+2,0:half]
        ka=[load(cut(k,t),buf(0,t),v.tsem.at[t]) for t in range(nc)]
        cp.wait()
        ra=[load(cut(q,t),buf(8,t),v.tsem.at[4+t]) for t in range(nc)]
        outs=[]
        for t in range(nc):
            ka[t].wait(); ra[t].wait()
            if last:
                v.acc[2*t,0:half]+=v.acc[8+2*t,0:half]
                outs.append(load(buf(0,t),cut(getattr(v,"f_"+w),t),v.tsem.at[t]))
            else:
                v.acc[2*t:2*t+2,0:half]+=v.acc[8+2*t:8+2*t+2,0:half]
                b=bit[o[j+1]]
                for name,which in (("s",1-b),("k",b)):
                    ref=getattr(v,name+"%d_"%(j+1)+w)
                    if len(ref.shape)==2:
                        outs.append(load(v.acc.at[2*t+which,0:half],ref.at[:,pl.ds(t*CW,CW)],v.tsem.at[t+(0 if name=="s" else 4)]))
                    else:
                        for z in range(2):
                            outs.append(load(v.acc.at[2*t+which,pl.ds(z*(half//2),half//2)],ref.at[z,:,pl.ds(t*CW,CW)],v.usem.at[t,z+(0 if name=="s" else 2)]))
        for cp in outs: cp.wait()
        if not last: sent(w,j+1,o[j+1]).start()

    def dgrad(i):
        W0=i*TB
        if i==0:
            wait("w")
            fetch("x0",v.x.at[rowsl(0)],v.mbuf.at[0],8)
        wait("x%d"%i)
        if i+1<nb: fetch("x%d"%(i+1),v.x.at[rowsl(i+1)],v.mbuf.at[(i+1)%2],8+2*((i+1)%2))
        pgc=v.pgF[:,W0:W0+TB].T
        qb=jnp.sum(pgc.astype(F32),axis=0,keepdims=True)
        ag=dot_nt(pgc,v.wv[...])
        mg=v.e[W0:W0+TB]
        normed,inv=normalize(v.mbuf[i%2])
        cs=[jnp.sum(t,axis=0,keepdims=True) for t in (ag*normed,ag,mg*normed,mg)]
        if i==0: v.qb[...]=qb
        else: v.qb[...]+=qb
        for j in range(4):
            if i==0: v.vec[0,j:j+1]=cs[j]
            else: v.vec[0,j:j+1]+=cs[j]
        e=ag*v.g1[...]+mg*v.g2[...]
        v.e[W0:W0+TB]=inv*(e-jnp.mean(e,axis=1,keepdims=True)-normed*jnp.mean(e*normed,axis=1,keepdims=True))

    def vfill():
        v.vec[0,4:5]=v.gsum[...]
        at=5
        for ref in (v.fb,v.qb):
            w=ref.shape[1]
            for lo in range(0,w,d):
                hi=min(w,lo+d)
                v.vec[0,at:at+1,0:hi-lo]=ref[:,lo:hi]
                if hi-lo<d: v.vec[0,at:at+1,hi-lo:d]=jnp.zeros((1,d-hi+lo),F32)
                at+=1
        if at<v.vec.shape[1]: v.vec[0,at:]=jnp.zeros((v.vec.shape[1]-at,d),F32)
    def vcopy(j): return remote(v.vec.at[j],v.vrecv.at[j],v.vsend.at[j],v.vrecv_sem.at[j],twin if j==0 else peer[j-1])
    def vstep(j):
        vcopy(j).wait()
        if j==0:
            v.vec[1,0:4]=v.vec[0,0:4]+v.vrecv[0,0:4]
            v.vec[1,4:]=v.vec[0,4:]
        else: v.vec[j+1]=v.vec[j]+v.vrecv[j]
        if j<bits: vcopy(j+1).start()

    def flat():
        v.pgF[...]=v.pgT[...].reshape(c,n)

    mlp(0); attn(0); ysend("p",0)
    mlp(1); attn(1); ysend("p",1)
    mlp(2); mlp(3)
    other("fc2"); other("fc1")
    attn(2); ysend("p",2)
    own("fc2"); own("fc1")
    attn(3); ysend("p",3)
    flat()
    other("qkv"); other("out")
    for i in range(nb):
        dgrad(i); ysend("e",i)
    own("qkv"); own("out")
    vfill(); vcopy(0).start()
    for j in range(bits+1): vstep(j)
    cp=load(v.vec.at[bits+1],v.sums,v.lsem.at[12]); cp.wait()
    yfinish("p",0); yfinish("p",1)
    top=bits-1
    stage("fc2",1); stage("qkv",1)
    yfinish("p",2)
    for j in range(2,top+1): stage("fc2",j)
    stage("fc1",1); stage("qkv",2); yfinish("p",3)
    stage("out",1)
    for j in range(2,top+1): stage("fc1",j); stage("out",j)
    for j in range(3,top+1): stage("qkv",j)
    for i in range(nb): yfinish("e",i)

def mega(dp,args):
    x=args["x"]; n,d=x.shape; ff=args["w1"].shape[1]; inner=args["wo"].shape[0]; c=args["w"].shape[1]; heads=c//(3*HD)
    bits=dp.bit_length()-1
    cols={"fc2":ff,"fc1":ff,"out":inner,"qkv":c}
    S=jax.ShapeDtypeStruct
    vrows=16
    small=("cos","sin","g1","g2","bias_out","b1","gsum")
    ins=["starts"]+list(small)+["x","g","m","w1","w2","wo","w","qkv","do","gT","mT","aT"]
    specs=[]
    for k in ins:
        specs.append(pl.BlockSpec(memory_space=pltpu.SMEM if k=="starts" else pltpu.VMEM if k in small else pl.ANY))
    outs={"hidden":S((n,d),BF),"hgrad":S((n,d),BF),"sums":S((vrows,d),F32)}
    for w in WEIGHTS: outs["f_"+w]=S((d//dp,cols[w]),F32)
    outs["yrecv"]=S((n,d),F32); outs["erecv"]=S((n,d),F32)
    for w in WEIGHTS:
        outs["r0_"+w]=S((2,d//4,cols[w]),F32)
        size=d//4
        for j in range(1,bits):
            sh=(size,cols[w]) if j==bits-1 else (2,size//2,cols[w])
            for p in "skr": outs[p+"%d_"%j+w]=S(sh,F32)
            size//=2
    V=pltpu.VMEM; D=pltpu.SemaphoreType.DMA
    scratch=dict(w1v=V((d,ff),BF),w2v=V((ff,d),BF),wov=V((inner,d),BF),wv=V((d,c),BF),qv=V((heads,3*HD,n),BF),dov=V((heads,HD,n),BF),
        mbuf=V((2,TB,d),BF),gbuf=V((2,TB,d),BF),fbuf=V((TB,d),F32),act=V((n,ff),BF),pg=V((n,ff),BF),o=V((heads,HD,n),BF),pgT=V((heads,3*HD,n),BF),pgF=V((c,n),BF),
        part=V((n,d),F32),e=V((n,d),F32),acc=V((heads*n//CW,2*HD,CW),F32),bias=V((2*TB,TB),F32),abuf=V((2,d//4,n),BF),ring=V((2,d//4,CW),F32),
        ring2=V((2,2,d//8,CW),F32),rin=V((2,d//4,CW),F32),fb=V((1,ff),F32),qb=V((1,c),F32),vec=V((bits+2,vrows,d),F32),vrecv=V((bits+1,vrows,d),F32),
        lsem=D((13,)),ysend=D((2*(n//TB),)),yrecv_sem=D((2*(n//TB),)),csend=D((2,)),crecv=D((4,)),xsend=D((4*(bits-1),)),xrecv=D((4*(bits-1),)),
        osem=D((4,)),tsem=D((8,)),usem=D((4,4)),vsend=D((bits+1,)),vrecv_sem=D((bits+1,)))
    names=ins+list(outs)+list(scratch)
    res=pl.pallas_call(functools.partial(mega_body,names,bits,(n,d,ff,inner,c,heads)),name="layer",
        in_specs=specs,out_specs=[pl.BlockSpec(memory_space=pl.ANY)]*len(outs),out_shape=list(outs.values()),
        scratch_shapes=list(scratch.values()),
        compiler_params=pltpu.CompilerParams(collective_id=0,has_side_effects=True,vmem_limit_bytes=67043328),
    )(*[args[k] for k in ins])
    return dict(zip(outs,res))

def tables(n):
    angles=np.arange(n,dtype=np.float64)[None,:]*(10000.0**(-np.arange(ROT//2)*2.0/ROT))[:,None]
    return jnp.asarray(np.cos(angles),F32),jnp.asarray(np.sin(angles),F32)

def local(dp,x,starts,g1,b1,g2,b2,w,bq,wo,bo,w1,bf1,w2,bf2,g):
    n,d=x.shape; c=w.shape[1]; ff=w1.shape[1]
    cos,sin=tables(n)
    row=lambda t:t.reshape(1,-1)
    m,aT,mT,gT,qkv,do,gsum=prologue(dp,x,g,g1,b1,g2,b2,w,bq,wo,cos,sin)
    o=mega(dp,dict(starts=starts,cos=cos,sin=sin,g1=row(g1),g2=row(g2),bias_out=row(bo+bf2),b1=row(bf1),gsum=gsum,x=x,g=g,m=m,w1=w1,w2=w2,wo=wo,w=w,
        qkv=qkv,do=do.reshape(-1,HD,n),gT=gT,mT=mT,aT=aT))
    s=o["sums"]
    fr=5+-(-ff//d)
    fb=s[5:fr].reshape(-1)[:ff]; qb=s[fr:fr+-(-c//d)].reshape(-1)[:c]
    return (o["hidden"],o["hgrad"],s[0],s[1],o["f_qkv"],qb,o["f_out"].T,s[4],s[2],s[3],o["f_fc1"],fb,o["f_fc2"].T,s[4])

def solution(mesh):
    A=P("dp",None); R=P()
    col=P(None,"tensor"); vt=P("tensor"); rw=P("tensor",None)
    in_specs=(A,A,R,R,R,R,col,vt,rw,R,col,vt,rw,R,A)
    out_specs=(A,A,R,R,P("dp","tensor"),vt,P("tensor","dp"),R,R,R,P("dp","tensor"),vt,P("tensor","dp"),R)
    return jax.shard_map(functools.partial(local,mesh.shape["dp"]),mesh=mesh,in_specs=in_specs,out_specs=out_specs,check_vma=False)
```

time: 470 us -> 423 us (0.900)
  Pallas kernels: 183 us -> 407 us
  waiting for transfers between devices: 221 us -> 0 us
  starting transfers between devices: 34.5 us -> 0 us
  other arithmetic: 22.7 us -> 1.3 us
  local copies, waits for them, and re-layouts: 6.71 us -> 12.6 us
    pallas_call x16 -> x1, Pallas kernels: 170 us -> 394 us  [mega(): pl.pallas_call(functools.partial(mega_body, names, bits, (n, d, ff, inner...]
    ppermute x27 -> x0, waiting for transfers between devices: 221 us -> none  [the longest x7 117 us: local(): across = lambda v: lax.ppermute(v, 'tensor', [(0, 1), (1, 0)])]
    ppermute x27 -> x0, starting transfers between devices: 34.5 us -> none  [the longest x20 22.1 us: local(): lax.ppermute(v, 'dp', [(i, i ^ 1 << b) for i in range(dp)])]
    another operation x4 -> x0, other arithmetic: 11.1 us -> none
    unnamed x48 -> x20, local copies, waits for them, and re-layouts: 3.19 us -> 9.08 us
  transfers between devices with their start and end apart: 27 -> 0, of which waited for: 15 -> 0; matrix products, arithmetic and copies ran while one was open for 5% -> 0% of each run, Pallas kernels for 27% -> 0%
where the time goes in v2:
time: 423 us; the launch traced here: 421 us
  Pallas kernels  407 us (96%)
  local copies, waits for them, and re-layouts  12.6 us (3%)
    pallas_call x1, Pallas kernels, mega(): pl.pallas_call(functools.partial(mega_body, names, bits, (n, d, ff, inner...  394 us
    pallas_call x1, Pallas kernels, prologue(): pl.pallas_call(functools.partial(prologue_body, dp), name='prologue', gri...  12.7 us
    unnamed x20, local copies, waits for them, and re-layouts  9.08 us

profile of v2, /device:TPU:0, one launch (start us, length us, event | category | flops | bytes accessed | tf_op | source)
XLA Modules:
  0.0 421.2 jit_solution(13611196823150985968)
XLA Ops:
  0.6 1.3 add.3
  1.9 1.3 reshape.66.bq_ref
  3.2 12.7 %prologue.1 = (bf16[1024,1024]{1,0:T(8,128)(2,1)}, bf16[4,256,1024]{2,1,0:T(8,128)(2,1)}, bf16[4,256,1024]{2,1,0:T(8,128)(2,1)}, bf16[4,256,1024]{2,1,0:T(8,128)...) custom-call(bf16[1024,1024]{1,0:T(8,128)(2,1)} %refs_8_.1, ...), custom_call_target="tpu_custom_call" | custom-call | flops 4294967296 | bytes 20971520 | tf_op jit(solution)/shard_map/prologue/pallas_call | solution.py:83
  15.9 393.9 %layer.1 = (bf16[1024,1024]{1,0:T(8,128)(2,1)}, bf16[1024,1024]{1,0:T(8,128)(2,1)}, f32[16,1024]{1,0:T(8,128)}, f32[64,2048]{1,0:T(8,128)}, f32[64,2048]{1,0:T(8...) custom-call(s32[1,2]{1,0:T(1,128)} %refs_0_.1, ...), custom_call_target="tpu_custom_call" | custom-call | tf_op jit(solution)/shard_map/layer/pallas_call | solution.py:435
  409.9 0.9 slice_bitcast_fusion
  410.8 1.6 fusion
  412.4 0.0 copy-start.5
  412.4 0.6 copy_bitcast_fusion
  413.0 0.6 copy.42
  413.6 0.0 copy-start
  413.6 3.2 copy.43
  416.9 0.0 copy-done.5
  416.9 0.0 copy-done
  416.9 0.0 copy-start.3
  416.9 0.0 copy-start.4
  416.9 0.0 copy-start.2
  416.9 1.3 copy.44
  418.2 0.0 copy-done.3
  418.2 0.0 copy-start.1
  418.2 0.7 copy.45
  418.9 0.0 copy-done.4
  418.9 0.7 copy.46
  419.6 0.0 copy-done.2
  419.6 0.8 copy.47
  420.4 0.0 copy-done.1
  420.4 0.8 copy.48
Async XLA Ops:
  412.4 4.4 %copy-start.5 = (f32[1,1024]{1,0:T(1,128)}, f32[1,1024]{1,0:T(1,128)S(1)}, u32[]{:S(2)}) copy-start(f32[1,1024]{1,0:T(1,128)S(1)} %get-tuple-element.46) | copy-start | bytes 12292
  413.6 3.2 copy-start
  416.9 1.3 copy-start.3
  416.9 2.1 copy-start.4
  416.9 2.7 copy-start.2
  418.2 2.2 copy-start.1

commit v3 on v2

--- a/solution.py
+++ b/solution.py
@@ -195,7 +195,7 @@
             rd=jnp.sum(p*dP,axis=0,keepdims=True)
             ds=(p*(dP-rd)).astype(BF)
             dq=dot(kT,ds)
-            v.pgT[h,0:HD,W0:W0+TB]=back(dq*(1.0/math.sqrt(HD)),v.cos[:,W0:W0+TB],v.sin[:,W0:W0+TB]).astype(BF)
+            v.pgT[pl.ds(pl.multiple_of(h*3*HD,HD),HD),W0:W0+TB]=back(dq*(1.0/math.sqrt(HD)),v.cos[:,W0:W0+TB],v.sin[:,W0:W0+TB]).astype(BF)
             dk=dot_nt(qT,ds)
             dv=dot_nt(doT,pb)
             nh=n//CW
@@ -214,7 +214,7 @@
                         else:
                             tot=v.acc[at,rs]+x[:,lo:hi]
                             if j==0: tot=back(tot,v.cos[:,lo:hi],v.sin[:,lo:hi])
-                            v.pgT[h,(1+j)*HD:(2+j)*HD,lo:hi]=tot.astype(BF)
+                            v.pgT[pl.ds(pl.multiple_of(h*3*HD+(1+j)*HD,HD),HD),lo:hi]=tot.astype(BF)
         if i==0: wait("wo")
         oc=v.o[:,:,W0:W0+TB].reshape(inner,TB)
         v.part[W0:W0+TB]+=dot_tn(oc,v.wov[...])
@@ -226,15 +226,18 @@
         cp=remote(src.at[rowsl(i)],dst.at[rowsl(i)],v.ysend.at[k],v.yrecv_sem.at[k],twin)
         cp.start(); Y[kind,i]=cp
     def yfinish(kind,i):
-        if kind=="p": fetch("res",v.x.at[rowsl(i)],v.mbuf.at[0],8)
-        else: fetch("res",v.g.at[rowsl(i)],v.mbuf.at[0],8)
-        cp=Y.pop((kind,i)); cp.wait()
+        fetch("res",(v.x if kind=="p" else v.g).at[rowsl(i)],v.mbuf.at[0],8)
+        Y.pop((kind,i)).wait()
         mine,recv,out=(v.part,v.yrecv,v.hidden) if kind=="p" else (v.e,v.erecv,v.hgrad)
-        fetch("recv",recv.at[rowsl(i)],v.fbuf,10)
-        wait("res"); wait("recv")
-        t=v.mbuf[0].astype(F32)+(mine[i*TB:(i+1)*TB]+v.fbuf[...])
-        if kind=="p": t=t+v.bias_out[...]
-        v.gbuf[0]=t.astype(BF)
+        tiles=[(a,b) for a in range(TB//128) for b in range(d//CW)]
+        for k,(a,b) in enumerate(tiles): fetch("recv%d"%k,recv.at[pl.ds(i*TB+a*128,128),pl.ds(b*CW,CW)],v.acc.at[k],19+k)
+        wait("res")
+        for k,(a,b) in enumerate(tiles):
+            wait("recv%d"%k)
+            rs=slice(a*128,(a+1)*128); cs=slice(b*CW,(b+1)*CW)
+            t=v.mbuf[0,rs,cs].astype(F32)+(v.part if kind=="p" else v.e)[i*TB+a*128:i*TB+(a+1)*128,cs]+v.acc[k]
+            if kind=="p": t=t+v.bias_out[:,cs]
+            v.gbuf[0,rs,cs]=t.astype(BF)
         fetch("st",v.gbuf.at[0],out.at[rowsl(i)],11)
         wait("st")
 
@@ -243,95 +246,92 @@
         if w=="fc2": return v.act[:,cs],False
         if w=="fc1": return v.pg[:,cs],False
         if w=="out": return v.o[...].reshape(inner,n),True
-        return None,True
+        return v.pgT[cs,:],True
     lhs={"fc2":v.gT,"out":v.gT,"fc1":v.mT,"qkv":v.aT}
-    per=CW//HD
     def product(w,a,cb):
-        if w=="qkv":
-            b=v.pgF[pl.ds(pl.multiple_of(cb*CW,CW),CW),:]
-            return dot_nt(a,b)
         b,nt=rhs(w,cb)
-        return dot_nt(a,b) if nt else dot(a,b)
-    C0={}
+        y=dot_nt(a,b) if nt else dot(a,b)
+        return y
+    def colsl(cb): return pl.ds(pl.multiple_of(cb*CW,CW),CW)
+    first={}; at=0
+    for w in WEIGHTS: first[w]=at; at+=cols[w]//CW
+    NP=at
+    def level(j): return getattr(v,"r%d"%j)
     def other(w):
-        nc=cols[w]//CW
-        b0=order[w][0]
+        nc=cols[w]//CW; b0,b1=order[w][0],order[w][1]; k=WEIGHTS.index(w)
         cp=load(lhs[w].at[pl.ds(2*(1-bit[b0]),2)],v.abuf,v.lsem.at[12]); cp.wait()
-        dst=getattr(v,"r0_"+w)
-        def send(t,slot):
-            xi=t//nc; cb=t%nc
-            return remote(v.ring.at[slot],dst.at[xi,:,pl.ds(pl.multiple_of(cb*CW,CW),CW)],v.csend.at[slot],v.crecv.at[WEIGHTS.index(w)],peer[b0])
+        stg=getattr(v,"o_"+w); dst=getattr(v,"r0_"+w)
+        def half(t): return (t//nc)*bit[b1]+(1-t//nc)*(1-bit[b1])
+        def put(t): return pltpu.make_async_copy(v.ring.at[t%3],stg.at[half(t),:,colsl(t%nc)],v.osem.at[t%3])
+        def send(t): return remote(stg.at[half(t),:,colsl(t%nc)],dst.at[half(t),:,colsl(t%nc)],v.csend.at[k],v.crecv.at[k,t//nc],peer[b0])
         @pl.loop(0,2*nc)
         def _(t):
-            slot=t%2
+            y=product(w,v.abuf[half(t)],t%nc)
             @pl.when(t>=2)
-            def _(): send(t,slot).wait_send()
-            v.ring[slot]=product(w,v.abuf[t//nc],t%nc)
-            send(t,slot).start()
-        for slot in range(2): send(slot,slot).wait_send()
-    def sent(w,j,dev_bit):
-        s=getattr(v,"s%d_"%j+w); q=getattr(v,"r%d_"%j+w)
-        k=WEIGHTS.index(w)*(bits-1)+j-1
-        return remote(s,q,v.xsend.at[k],v.xrecv.at[k],peer[dev_bit])
-    def own(w):
-        nc=cols[w]//CW
-        o=order[w]; b0,b1=o[0],o[1]
+            def _(): put(t-2).wait(); send(t-2).start()
+            v.ring[t%3]=y
+            put(t).start()
+        for t in range(2*nc-2,2*nc): put(t).wait(); send(t).start()
+    owns=[("fc2",0),("fc1",0),("fc2",1),("qkv",0),("out",0),("fc1",1),("qkv",1),("out",1)]
+    def fetch_own(n):
+        w,which=owns[n]; b0,b1=order[w][0],order[w][1]
+        xi=2*bit[b0]+((1-bit[b1]) if which==0 else bit[b1])
+        fetch("own%d"%n,lhs[w].at[xi],v.abuf.at[n%2],13+n%2)
+    def sent(w,cb,j):
+        p=first[w]+cb; o=order[w]
+        b=bit[o[j]]
+        rows=d>>(j+1)
+        src=getattr(v,"s1_"+w).at[:,colsl(cb)] if j==1 else level(j-1).at[p,pl.ds(pl.multiple_of((1-b)*rows,rows),rows)]
+        return remote(src,level(j).at[p],v.xsend.at[j-1,p],v.xrecv.at[j-1,p],peer[o[j]])
+    def own(n):
+        w,which=owns[n]
+        nc=cols[w]//CW; b0,b1=order[w][0],order[w][1]; k=WEIGHTS.index(w)
+        xi=(1-bit[b1]) if which==0 else bit[b1]
+        if "own%d"%n not in L: fetch_own(n)
         r0=getattr(v,"r0_"+w)
-        cp=load(lhs[w].at[pl.ds(2*bit[b0],2)],v.abuf,v.lsem.at[12])
-        remote(r0,r0,v.csend.at[0],v.crecv.at[WEIGHTS.index(w)],peer[b0]).wait_recv()
-        cp.wait()
-        def place(ref,cb):
-            return ref.at[:,:,pl.ds(pl.multiple_of(cb*CW,CW),CW)] if len(ref.shape)==3 else ref.at[:,pl.ds(pl.multiple_of(cb*CW,CW),CW)]
-        for which in range(2):
-            xi=(1-bit[b1]) if which==0 else bit[b1]
-            ref=getattr(v,("s1_" if which==0 else "k1_")+w)
-            hh=ref.shape[-2]
-            def get(cb,slot): return pltpu.make_async_copy(r0.at[xi,:,pl.ds(pl.multiple_of(cb*CW,CW),CW)],v.rin.at[slot],v.osem.at[slot])
-            def put(cb,slot): return pltpu.make_async_copy(v.ring2.at[slot] if len(ref.shape)==3 else v.ring2.at[slot,0],place(ref,cb),v.osem.at[2+slot])
-            get(0,0).start()
-            @pl.loop(0,nc)
-            def _(t):
-                slot=t%2
-                @pl.when(t+1<nc)
-                def _(): get(t+1,1-slot).start()
-                y=product(w,v.abuf[xi],t)
-                get(t,slot).wait()
-                @pl.when(t>=2)
-                def _(): put(t,slot).wait()
-                y=y+v.rin[slot]
-                v.ring2[slot]=y.reshape(2,quarter//2,CW)
-                put(t,slot).start()
-            for t in range(max(0,nc-2),nc): put(t,t%2).wait()
-            if which==0: sent(w,1,b1).start()
-    def stage(w,j):
-        nc=cols[w]//CW; o=order[w]
-        cp=sent(w,j,o[j])
-        k=getattr(v,"k%d_"%j+w); q=getattr(v,"r%d_"%j+w)
-        last=j==bits-1
-        half=k.shape[-2]
-        def cut(ref,t): return ref.at[:,pl.ds(t*CW,CW)] if last else ref.at[:,:,pl.ds(t*CW,CW)]
-        def buf(base,t): return v.acc.at[base+2*t,0:half] if last else v.acc.at[base+2*t:base+2*t+2,0:half]
-        ka=[load(cut(k,t),buf(0,t),v.tsem.at[t]) for t in range(nc)]
-        cp.wait()
-        ra=[load(cut(q,t),buf(8,t),v.tsem.at[4+t]) for t in range(nc)]
-        outs=[]
-        for t in range(nc):
-            ka[t].wait(); ra[t].wait()
-            if last:
-                v.acc[2*t,0:half]+=v.acc[8+2*t,0:half]
-                outs.append(load(buf(0,t),cut(getattr(v,"f_"+w),t),v.tsem.at[t]))
-            else:
-                v.acc[2*t:2*t+2,0:half]+=v.acc[8+2*t:8+2*t+2,0:half]
-                b=bit[o[j+1]]
-                for name,which in (("s",1-b),("k",b)):
-                    ref=getattr(v,name+"%d_"%(j+1)+w)
-                    if len(ref.shape)==2:
-                        outs.append(load(v.acc.at[2*t+which,0:half],ref.at[:,pl.ds(t*CW,CW)],v.tsem.at[t+(0 if name=="s" else 4)]))
-                    else:
-                        for z in range(2):
-                            outs.append(load(v.acc.at[2*t+which,pl.ds(z*(half//2),half//2)],ref.at[z,:,pl.ds(t*CW,CW)],v.usem.at[t,z+(0 if name=="s" else 2)]))
-        for cp in outs: cp.wait()
-        if not last: sent(w,j+1,o[j+1]).start()
+        ref=getattr(v,("s1_" if which==0 else "k1_")+w)
+        remote(r0.at[xi],r0.at[xi],v.csend.at[k],v.crecv.at[k,which],peer[b0]).wait_recv()
+        def get(cb): return pltpu.make_async_copy(r0.at[xi,:,colsl(cb)],v.rin.at[cb%2],v.isem.at[cb%2])
+        def put(cb): return pltpu.make_async_copy(v.ring.at[cb%3],ref.at[:,colsl(cb)],v.osem.at[cb%3])
+        get(0).start()
+        if nc>1: get(1).start()
+        wait("own%d"%n)
+        if n+1<len(owns) and n!=2: fetch_own(n+1)
+        @pl.loop(0,nc)
+        def _(t):
+            y=product(w,v.abuf[n%2],t)
+            @pl.when(t>=1)
+            def _():
+                put(t-1).wait()
+                if which==0: sent(w,t-1,1).start()
+            get(t).wait()
+            v.ring[t%3]=y+v.rin[t%2]
+            @pl.when(t+2<nc)
+            def _(): get(t+2).start()
+            put(t).start()
+        put(nc-1).wait()
+        if which==0: sent(w,nc-1,1).start()
+    kept=[]; moved=[0]
+    def fetch_kept():
+        m=moved[0]
+        if m<len(kept):
+            w,cb=kept[m]
+            fetch("k%s%d"%(w,cb),getattr(v,"k1_"+w).at[:,colsl(cb)],v.ring.at[m%3],15+m%3)
+            moved[0]=m+1
+    def stage(w,cb,j):
+        p=first[w]+cb; o=order[w]; last=j==bits-1
+        sent(w,cb,j).wait_recv()
+        r=level(j)
+        if j==1:
+            m=kept.index((w,cb))
+            wait("k%s%d"%(w,cb))
+            r[p]=r[p]+v.ring[m%3]
+            fetch_kept()
+        else:
+            rows=d>>(j+1)
+            r[p]=r[p]+level(j-1)[p,pl.ds(pl.multiple_of(bit[o[j]]*rows,rows),rows)]
+        if last: load(r.at[p],getattr(v,"f_"+w).at[:,colsl(cb)],v.fsem.at[p])
+        else: sent(w,cb,j+1).start()
 
     def dgrad(i):
         W0=i*TB
@@ -340,7 +340,7 @@
             fetch("x0",v.x.at[rowsl(0)],v.mbuf.at[0],8)
         wait("x%d"%i)
         if i+1<nb: fetch("x%d"%(i+1),v.x.at[rowsl(i+1)],v.mbuf.at[(i+1)%2],8+2*((i+1)%2))
-        pgc=v.pgF[:,W0:W0+TB].T
+        pgc=v.pgT[:,W0:W0+TB].T
         qb=jnp.sum(pgc.astype(F32),axis=0,keepdims=True)
         ag=dot_nt(pgc,v.wv[...])
         mg=v.e[W0:W0+TB]
@@ -349,59 +349,63 @@
         if i==0: v.qb[...]=qb
         else: v.qb[...]+=qb
         for j in range(4):
-            if i==0: v.vec[0,j:j+1]=cs[j]
-            else: v.vec[0,j:j+1]+=cs[j]
+            if i==0: v.vec[j:j+1]=cs[j]
+            else: v.vec[j:j+1]+=cs[j]
         e=ag*v.g1[...]+mg*v.g2[...]
         v.e[W0:W0+TB]=inv*(e-jnp.mean(e,axis=1,keepdims=True)-normed*jnp.mean(e*normed,axis=1,keepdims=True))
 
     def vfill():
-        v.vec[0,4:5]=v.gsum[...]
+        v.vec[4:5]=v.gsum[...]
         at=5
         for ref in (v.fb,v.qb):
             w=ref.shape[1]
             for lo in range(0,w,d):
                 hi=min(w,lo+d)
-                v.vec[0,at:at+1,0:hi-lo]=ref[:,lo:hi]
-                if hi-lo<d: v.vec[0,at:at+1,hi-lo:d]=jnp.zeros((1,d-hi+lo),F32)
+                v.vec[at:at+1,0:hi-lo]=ref[:,lo:hi]
+                if hi-lo<d: v.vec[at:at+1,hi-lo:d]=jnp.zeros((1,d-hi+lo),F32)
                 at+=1
-        if at<v.vec.shape[1]: v.vec[0,at:]=jnp.zeros((v.vec.shape[1]-at,d),F32)
-    def vcopy(j): return remote(v.vec.at[j],v.vrecv.at[j],v.vsend.at[j],v.vrecv_sem.at[j],twin if j==0 else peer[j-1])
+        if at<v.vec.shape[0]: v.vec[at:]=jnp.zeros((v.vec.shape[0]-at,d),F32)
+    def vcopy(j): return remote(v.vec,v.vrecv.at[j],v.vsend.at[j],v.vrecv_sem.at[j],twin if j==0 else peer[order["qkv"][j-1]])
     def vstep(j):
         vcopy(j).wait()
-        if j==0:
-            v.vec[1,0:4]=v.vec[0,0:4]+v.vrecv[0,0:4]
-            v.vec[1,4:]=v.vec[0,4:]
-        else: v.vec[j+1]=v.vec[j]+v.vrecv[j]
+        rows=slice(0,4) if j==0 else slice(None)
+        v.vec[rows]=v.vec[rows]+v.vrecv[j,rows]
         if j<bits: vcopy(j+1).start()
-
-    def flat():
-        v.pgF[...]=v.pgT[...].reshape(c,n)
 
     mlp(0); attn(0); ysend("p",0)
     mlp(1); attn(1); ysend("p",1)
     mlp(2); mlp(3)
     other("fc2"); other("fc1")
     attn(2); ysend("p",2)
-    own("fc2"); own("fc1")
+    own(0); own(1); own(2)
     attn(3); ysend("p",3)
-    flat()
+    for i in range(nb): dgrad(i)
+    vfill(); vcopy(0).start()
+    for i in range(nb): ysend("e",i)
     other("qkv"); other("out")
+    for q in range(3,len(owns)): own(q)
+    todo=[]
+    wide=[(w,cb) for w in ("fc2","fc1","out") for cb in range(cols[w]//CW)]
+    for k,(w,cb) in enumerate(wide):
+        for j in range(1,bits): todo.append((94+12*k+12*(j-1),"s",(w,cb,j)))
+    for k in range(c//CW):
+        for j in range(1,bits): todo.append((132+14*k+18*(j-1),"s",("qkv",k,j)))
     for i in range(nb):
-        dgrad(i); ysend("e",i)
-    own("qkv"); own("out")
-    vfill(); vcopy(0).start()
-    for j in range(bits+1): vstep(j)
-    cp=load(v.vec.at[bits+1],v.sums,v.lsem.at[12]); cp.wait()
-    yfinish("p",0); yfinish("p",1)
-    top=bits-1
-    stage("fc2",1); stage("qkv",1)
-    yfinish("p",2)
-    for j in range(2,top+1): stage("fc2",j)
-    stage("fc1",1); stage("qkv",2); yfinish("p",3)
-    stage("out",1)
-    for j in range(2,top+1): stage("fc1",j); stage("out",j)
-    for j in range(3,top+1): stage("qkv",j)
-    for i in range(nb): yfinish("e",i)
+        todo.append((115+5*i if i<nb-1 else 130,"y",("p",i)))
+        todo.append((154+24*i,"y",("e",i)))
+    for j in range(bits+1): todo.append(((131,136,158,175,195,215,220,225)[j],"v",(j,)))
+    todo.sort(key=lambda t:t[0])
+    kept.extend(t[2][:2] for t in todo if t[1]=="s" and t[2][2]==1)
+    for _ in range(3): fetch_kept()
+    for _,kind,what in todo: {"s":stage,"y":yfinish,"v":vstep}[kind](*what)
+    cp=load(v.vec,v.sums,v.lsem.at[12]); cp.wait()
+    for w in WEIGHTS:
+        b0=order[w][0]; k=WEIGHTS.index(w)
+        r0=getattr(v,"r0_"+w)
+        remote(getattr(v,"o_"+w),r0,v.csend.at[k],v.crecv.at[k,0],peer[b0]).wait_send()
+        for cb in range(cols[w]//CW):
+            for j in range(1,bits): sent(w,cb,j).wait_send()
+            pltpu.make_async_copy(level(bits-1).at[first[w]+cb],getattr(v,"f_"+w).at[:,colsl(cb)],v.fsem.at[first[w]+cb]).wait()
 
 def mega(dp,args):
     x=args["x"]; n,d=x.shape; ff=args["w1"].shape[1]; inner=args["wo"].shape[0]; c=args["w"].shape[1]; heads=c//(3*HD)
@@ -418,19 +422,19 @@
     for w in WEIGHTS: outs["f_"+w]=S((d//dp,cols[w]),F32)
     outs["yrecv"]=S((n,d),F32); outs["erecv"]=S((n,d),F32)
     for w in WEIGHTS:
-        outs["r0_"+w]=S((2,d//4,cols[w]),F32)
-        size=d//4
-        for j in range(1,bits):
-            sh=(size,cols[w]) if j==bits-1 else (2,size//2,cols[w])
-            for p in "skr": outs[p+"%d_"%j+w]=S(sh,F32)
-            size//=2
+        for p in ("o_","r0_"): outs[p+w]=S((2,d//4,cols[w]),F32)
+        for p in ("s1_","k1_"): outs[p+w]=S((d//4,cols[w]),F32)
+    NP=sum(cols.values())//CW
     V=pltpu.VMEM; D=pltpu.SemaphoreType.DMA
     scratch=dict(w1v=V((d,ff),BF),w2v=V((ff,d),BF),wov=V((inner,d),BF),wv=V((d,c),BF),qv=V((heads,3*HD,n),BF),dov=V((heads,HD,n),BF),
-        mbuf=V((2,TB,d),BF),gbuf=V((2,TB,d),BF),fbuf=V((TB,d),F32),act=V((n,ff),BF),pg=V((n,ff),BF),o=V((heads,HD,n),BF),pgT=V((heads,3*HD,n),BF),pgF=V((c,n),BF),
-        part=V((n,d),F32),e=V((n,d),F32),acc=V((heads*n//CW,2*HD,CW),F32),bias=V((2*TB,TB),F32),abuf=V((2,d//4,n),BF),ring=V((2,d//4,CW),F32),
-        ring2=V((2,2,d//8,CW),F32),rin=V((2,d//4,CW),F32),fb=V((1,ff),F32),qb=V((1,c),F32),vec=V((bits+2,vrows,d),F32),vrecv=V((bits+1,vrows,d),F32),
-        lsem=D((13,)),ysend=D((2*(n//TB),)),yrecv_sem=D((2*(n//TB),)),csend=D((2,)),crecv=D((4,)),xsend=D((4*(bits-1),)),xrecv=D((4*(bits-1),)),
-        osem=D((4,)),tsem=D((8,)),usem=D((4,4)),vsend=D((bits+1,)),vrecv_sem=D((bits+1,)))
+        mbuf=V((2,TB,d),BF),gbuf=V((2,TB,d),BF),act=V((n,ff),BF),pg=V((n,ff),BF),o=V((heads,HD,n),BF),pgT=V((c,n),BF),
+        part=V((n,d),F32),e=V((n,d),F32),acc=V((heads*n//CW,2*HD,CW),F32),bias=V((2*TB,TB),F32),abuf=V((2,d//4,n),BF),
+        ring=V((3,d//4,CW),F32),rin=V((2,d//4,CW),F32),fb=V((1,ff),F32),qb=V((1,c),F32),vec=V((vrows,d),F32),vrecv=V((bits+1,vrows,d),F32),
+        lsem=D((23,)),ysend=D((2*(n//TB),)),yrecv_sem=D((2*(n//TB),)),csend=D((4,)),crecv=D((4,2)),xsend=D((bits-1,NP)),xrecv=D((bits-1,NP)),
+        osem=D((4,)),isem=D((2,)),fsem=D((NP,)),vsend=D((bits+1,)),vrecv_sem=D((bits+1,)))
+    size=d//4
+    for j in range(1,bits):
+        scratch["r%d"%j]=V((NP,size,CW),F32); size//=2
     names=ins+list(outs)+list(scratch)
     res=pl.pallas_call(functools.partial(mega_body,names,bits,(n,d,ff,inner,c,heads)),name="layer",
         in_specs=specs,out_specs=[pl.BlockSpec(memory_space=pl.ANY)]*len(outs),out_shape=list(outs.values()),

time: 423 us -> 304 us (0.72)
  Pallas kernels: 407 us -> 289 us
    pallas_call x1, Pallas kernels: 394 us -> 276 us  [mega(): pl.pallas_call(functools.partial(mega_body, names, bits, (n, d, ff, inner...]
where the time goes in v3:
time: 304 us; the launch traced here: 303 us
  Pallas kernels  289 us (95%)
  local copies, waits for them, and re-layouts  12.6 us (4%)
    pallas_call x1, Pallas kernels, mega(): pl.pallas_call(functools.partial(mega_body, names, bits, (n, d, ff, inner...  276 us
    pallas_call x1, Pallas kernels, prologue(): pl.pallas_call(functools.partial(prologue_body, dp), name='prologue', gri...  12.6 us
    unnamed x20, local copies, waits for them, and re-layouts  9.08 us

profile of v3, /device:TPU:0, one launch (start us, length us, event | category | flops | bytes accessed | tf_op | source)
XLA Modules:
  0.0 303.1 jit_solution(2195297812932727918)
XLA Ops:
  0.6 1.3 add.3
  1.9 1.3 reshape.66.bq_ref
  3.2 12.6 %prologue.1 = (bf16[1024,1024]{1,0:T(8,128)(2,1)}, bf16[4,256,1024]{2,1,0:T(8,128)(2,1)}, bf16[4,256,1024]{2,1,0:T(8,128)(2,1)}, bf16[4,256,1024]{2,1,0:T(8,128)...) custom-call(bf16[1024,1024]{1,0:T(8,128)(2,1)} %refs_8_.1, ...), custom_call_target="tpu_custom_call" | custom-call | flops 4294967296 | bytes 20971520 | tf_op jit(solution)/shard_map/prologue/pallas_call | solution.py:83
  15.9 275.9 %layer.1 = (bf16[1024,1024]{1,0:T(8,128)(2,1)}, bf16[1024,1024]{1,0:T(8,128)(2,1)}, f32[16,1024]{1,0:T(8,128)}, f32[64,2048]{1,0:T(8,128)}, f32[64,2048]{1,0:T(8...) custom-call(s32[1,2]{1,0:T(1,128)} %refs_0_.1, ...), custom_call_target="tpu_custom_call" | custom-call | tf_op jit(solution)/shard_map/layer/pallas_call | solution.py:439
  291.8 0.9 slice_bitcast_fusion
  292.7 1.6 fusion
  294.4 0.0 copy-start.5
  294.4 0.6 copy_bitcast_fusion
  295.0 0.6 copy.42
  295.6 0.0 copy-start
  295.6 3.2 %copy.43 = bf16[1024,1024]{1,0:T(8,128)(2,1)} copy(bf16[1024,1024]{1,0:T(8,128)(2,1)} %get-tuple-element.93) | data formatting | bytes 4194304
  298.8 0.0 copy-done.5
  298.8 0.0 copy-done
  298.8 0.0 copy-start.3
  298.8 0.0 copy-start.4
  298.8 0.0 copy-start.2
  298.8 1.3 copy.44
  300.1 0.0 copy-done.3
  300.1 0.0 copy-start.1
  300.2 0.7 copy.45
  300.9 0.0 copy-done.4
  300.9 0.7 copy.46
  301.6 0.0 copy-done.2
  301.6 0.8 copy.47
  302.4 0.0 copy-done.1
  302.4 0.8 copy.48
Async XLA Ops:
  294.4 4.4 %copy-start.5 = (f32[1,1024]{1,0:T(1,128)}, f32[1,1024]{1,0:T(1,128)S(1)}, u32[]{:S(2)}) copy-start(f32[1,1024]{1,0:T(1,128)S(1)} %get-tuple-element.46) | copy-start | bytes 12292
  295.6 3.2 %copy-start = (bf16[1024,1024]{1,0:T(8,128)(2,1)S(1)}, bf16[1024,1024]{1,0:T(8,128)(2,1)}, u32[]{:S(2)}) copy-start(bf16[1024,1024]{1,0:T(8,128)(2,1)} %get-tuple-element.94) | copy-start | bytes 6291460
  298.8 1.3 copy-start.3
  298.8 2.1 copy-start.4
  298.8 2.7 copy-start.2
  300.1 2.2 copy-start.1

commit v4 on v3

--- a/solution.py
+++ b/solution.py
@@ -24,7 +24,7 @@
     return c*inv, inv
 
 def prologue_body(dp, x_ref,g_ref,g1,b1,g2,b2,w_ref,bq_ref,wo_ref,cos_ref,sin_ref,
-             m_out,aT_out,mT_out,gT_out,qkv_out,do_out,gsum_out,wT,bcol):
+             m_out,aT_out,mT_out,gT_out,hT_out,qkv_out,do_out,gsum_out,wT,bcol):
     step=pl.program_id(0)
     @pl.when(step==0)
     def _():
@@ -53,7 +53,7 @@
     gf=g_ref[...].astype(F32)
     gsum_out[...]+=jnp.sum(gf,axis=0,keepdims=True)
     gT=gf.T
-    for t,o,w in ((aT,aT_out,"qkv"),(mT,mT_out,"fc1"),(gT,gT_out,"fc2")):
+    for t,o,w in ((aT,aT_out,"qkv"),(mT,mT_out,"fc1"),(gT,gT_out,"fc2"),(gT,hT_out,"out")):
         for j,pt in enumerate(perm(t,order[w])):
             o[j]=pt.astype(BF)
     packed=dot(wT[...],aT.astype(BF))
@@ -83,9 +83,9 @@
     return pl.pallas_call(functools.partial(prologue_body,dp),name="prologue",
         grid=(n//TB,),
         in_specs=[xs,xs]+[full(a) for a in args[2:9]]+[ts,ts],
-        out_specs=[xs,tspec,tspec,tspec,pl.BlockSpec((heads,3*HD,TB),lambda i:(0,0,i)),
+        out_specs=[xs,tspec,tspec,tspec,tspec,pl.BlockSpec((heads,3*HD,TB),lambda i:(0,0,i)),
                    pl.BlockSpec((inner,TB),lambda i:(0,i)),pl.BlockSpec((1,d),lambda i:(0,0))],
-        out_shape=[jax.ShapeDtypeStruct((n,d),BF)]+[jax.ShapeDtypeStruct((4,d//4,n),BF)]*3+
+        out_shape=[jax.ShapeDtypeStruct((n,d),BF)]+[jax.ShapeDtypeStruct((4,d//4,n),BF)]*4+
             [jax.ShapeDtypeStruct((heads,3*HD,n),BF),jax.ShapeDtypeStruct((inner,n),BF),jax.ShapeDtypeStruct((1,d),F32)],
         scratch_shapes=[pltpu.VMEM((c,d),BF),pltpu.VMEM((c,128),F32)],
         compiler_params=pltpu.CompilerParams(vmem_limit_bytes=60*2**20),
@@ -98,7 +98,68 @@
 
 def orders(bits):
     up=list(range(bits))
-    return {"fc2":up,"out":up,"fc1":up,"qkv":up[:1]+up[2:]+up[1:2]}
+    return {"fc2":up,"fc1":up,"qkv":up,"out":up[:1]+up[2:]+up[1:2]}
+
+def plan(bits,nb,count):
+    unit=1.048576*2/88*1000
+    order=orders(bits)
+    free={}; arr=[]; out=[]; r0={}; whole=set(); clock=[18.0]; corelink=[0.0]
+    def xfer(dim,mb,t):
+        key=min(dim,2); us=mb*unit
+        s=max(t,free.get(key,0.0)); free[key]=s+us
+        if dim<3: return s+us+2
+        m=max(s,free.get("mid",0.0))+2*us; free["mid"]=m
+        return m+2
+    def push(at,rank,item): arr.append((at,rank,len(out),item))
+    def do(item):
+        clock[0]+={"stage":0.7,"finish":2.3,"vstep":0.4}[item[0]]
+        out.append(item)
+        if item[0]=="stage":
+            _,w,cb,j=item
+            if j<bits-1: push(xfer(order[w][j+1],0.5**(j+1),clock[0]),4-min(j,3),("stage",w,cb,j+1))
+        elif item[0]=="vstep":
+            j=item[1]
+            if j<bits:
+                dim=order["out"][j]
+                push(xfer(dim,1/16,clock[0]) if dim else clock[0]+2.5,0,("vstep",j+1))
+    def ready(tail):
+        def ok(it):
+            if it[0]=="stage": return it[3]>1 or it[1] in whole
+            return tail or it[0]=="vstep"
+        return [a for a in arr if a[0]<=clock[0] and ok(a[3])]
+    def poll(tail,most):
+        while most:
+            r=ready(tail)
+            if not r: return
+            a=min(r,key=lambda a:(a[1],a[0],a[2])); arr.remove(a); do(a[3]); most-=1
+    head=[]
+    for i in range(nb-2): head+=[("mlp",i),("attn",i),("send","p",i)]
+    head+=[("mlp",i) for i in range(nb-2,nb)]+[("other","fc2"),("other","fc1"),("attn",nb-2),("send","p",nb-2)]
+    head+=[("own","fc2",0),("own","fc1",0),("own","fc2",1),("attn",nb-1),("send","p",nb-1)]
+    head+=[("dgrad",i) for i in range(nb)]+[("vec",)]+[("send","e",i) for i in range(nb)]
+    head+=[("other","out"),("other","qkv"),("own","out",0),("own","qkv",0),("own","fc1",1),("own","out",1),("own","qkv",1)]
+    for h in head:
+        poll(False,6)
+        out.append(h); k=h[0]
+        if k=="mlp": clock[0]+=6.1
+        elif k=="attn": clock[0]+=3.35*min(h[1]+2,nb)
+        elif k=="dgrad": clock[0]+=1.6
+        elif k=="send": push(xfer(1.5,1,clock[0]),9 if h[1]=="p" else 6,("finish",)+h[1:])
+        elif k=="vec": push(xfer(1.5,1/16,clock[0]),0,("vstep",0))
+        elif k=="other":
+            for i in range(2*count[h[1]]):
+                clock[0]+=0.55; corelink[0]=max(corelink[0],clock[0])+1.15
+                r0[h[1],i//count[h[1]]]=corelink[0]+1
+        elif k=="own":
+            clock[0]=max(clock[0],r0[h[1:]])+1
+            if h[2]==1: whole.add(h[1])
+            for i in range(count[h[1]]):
+                clock[0]+=0.9
+                if h[2]==0: push(xfer(order[h[1]][1],0.5,clock[0]),5,("stage",h[1],i,1))
+    while arr:
+        clock[0]=max(clock[0],min(a[0] for a in arr))
+        poll(True,1)
+    return out
 
 def mega_body(names,bits,dims,*refs):
     r=dict(zip(names,refs))
@@ -247,7 +308,7 @@
         if w=="fc1": return v.pg[:,cs],False
         if w=="out": return v.o[...].reshape(inner,n),True
         return v.pgT[cs,:],True
-    lhs={"fc2":v.gT,"out":v.gT,"fc1":v.mT,"qkv":v.aT}
+    lhs={"fc2":v.gT,"out":v.hT,"fc1":v.mT,"qkv":v.aT}
     def product(w,a,cb):
         b,nt=rhs(w,cb)
         y=dot_nt(a,b) if nt else dot(a,b)
@@ -262,70 +323,70 @@
         cp=load(lhs[w].at[pl.ds(2*(1-bit[b0]),2)],v.abuf,v.lsem.at[12]); cp.wait()
         stg=getattr(v,"o_"+w); dst=getattr(v,"r0_"+w)
         def half(t): return (t//nc)*bit[b1]+(1-t//nc)*(1-bit[b1])
-        def put(t): return pltpu.make_async_copy(v.ring.at[t%3],stg.at[half(t),:,colsl(t%nc)],v.osem.at[t%3])
+        def put(t): return pltpu.make_async_copy(v.ring.at[t%2],stg.at[half(t),:,colsl(t%nc)],v.osem.at[t%2])
         def send(t): return remote(stg.at[half(t),:,colsl(t%nc)],dst.at[half(t),:,colsl(t%nc)],v.csend.at[k],v.crecv.at[k,t//nc],peer[b0])
         @pl.loop(0,2*nc)
         def _(t):
             y=product(w,v.abuf[half(t)],t%nc)
             @pl.when(t>=2)
             def _(): put(t-2).wait(); send(t-2).start()
-            v.ring[t%3]=y
+            v.ring[t%2]=y
             put(t).start()
         for t in range(2*nc-2,2*nc): put(t).wait(); send(t).start()
-    owns=[("fc2",0),("fc1",0),("fc2",1),("qkv",0),("out",0),("fc1",1),("qkv",1),("out",1)]
-    def fetch_own(n):
-        w,which=owns[n]; b0,b1=order[w][0],order[w][1]
+    slots=[0]
+    def fetch_own(w,which):
+        b0,b1=order[w][0],order[w][1]
         xi=2*bit[b0]+((1-bit[b1]) if which==0 else bit[b1])
-        fetch("own%d"%n,lhs[w].at[xi],v.abuf.at[n%2],13+n%2)
+        k=slots[0]%2; slots[0]+=1
+        fetch("own",lhs[w].at[xi],v.abuf.at[k],13+k)
+        return k
     def sent(w,cb,j):
         p=first[w]+cb; o=order[w]
         b=bit[o[j]]
         rows=d>>(j+1)
         src=getattr(v,"s1_"+w).at[:,colsl(cb)] if j==1 else level(j-1).at[p,pl.ds(pl.multiple_of((1-b)*rows,rows),rows)]
         return remote(src,level(j).at[p],v.xsend.at[j-1,p],v.xrecv.at[j-1,p],peer[o[j]])
-    def own(n):
-        w,which=owns[n]
+    def own(w,which):
         nc=cols[w]//CW; b0,b1=order[w][0],order[w][1]; k=WEIGHTS.index(w)
         xi=(1-bit[b1]) if which==0 else bit[b1]
-        if "own%d"%n not in L: fetch_own(n)
+        slot=fetch_own(w,which)
         r0=getattr(v,"r0_"+w)
         ref=getattr(v,("s1_" if which==0 else "k1_")+w)
         remote(r0.at[xi],r0.at[xi],v.csend.at[k],v.crecv.at[k,which],peer[b0]).wait_recv()
         def get(cb): return pltpu.make_async_copy(r0.at[xi,:,colsl(cb)],v.rin.at[cb%2],v.isem.at[cb%2])
-        def put(cb): return pltpu.make_async_copy(v.ring.at[cb%3],ref.at[:,colsl(cb)],v.osem.at[cb%3])
+        def put(cb): return pltpu.make_async_copy(v.ring.at[cb%2],ref.at[:,colsl(cb)],v.osem.at[cb%2])
         get(0).start()
         if nc>1: get(1).start()
-        wait("own%d"%n)
-        if n+1<len(owns) and n!=2: fetch_own(n+1)
+        wait("own")
         @pl.loop(0,nc)
         def _(t):
-            y=product(w,v.abuf[n%2],t)
+            y=product(w,v.abuf[slot],t)
             @pl.when(t>=1)
             def _():
                 put(t-1).wait()
                 if which==0: sent(w,t-1,1).start()
             get(t).wait()
-            v.ring[t%3]=y+v.rin[t%2]
+            v.ring[t%2]=y+v.rin[t%2]
             @pl.when(t+2<nc)
             def _(): get(t+2).start()
             put(t).start()
         put(nc-1).wait()
         if which==0: sent(w,nc-1,1).start()
-    kept=[]; moved=[0]
+        else: whole.add(w); fetch_kept()
+    kept=[]; whole=set()
     def fetch_kept():
-        m=moved[0]
-        if m<len(kept):
-            w,cb=kept[m]
-            fetch("k%s%d"%(w,cb),getattr(v,"k1_"+w).at[:,colsl(cb)],v.ring.at[m%3],15+m%3)
-            moved[0]=m+1
+        if kept and kept[0][0] in whole and "k0" not in L:
+            w,cb=kept[0]; rows=quarter//2
+            for q in range(2): fetch("k%d"%q,getattr(v,"k1_"+w).at[pl.ds(q*rows,rows),colsl(cb)],v.kin.at[q],15+q)
     def stage(w,cb,j):
         p=first[w]+cb; o=order[w]; last=j==bits-1
         sent(w,cb,j).wait_recv()
         r=level(j)
         if j==1:
-            m=kept.index((w,cb))
-            wait("k%s%d"%(w,cb))
-            r[p]=r[p]+v.ring[m%3]
+            kept.pop(0); rows=quarter//2
+            for q in range(2):
+                wait("k%d"%q)
+                r[p,q*rows:(q+1)*rows]=r[p,q*rows:(q+1)*rows]+v.kin[q]
             fetch_kept()
         else:
             rows=d>>(j+1)
@@ -365,39 +426,19 @@
                 if hi-lo<d: v.vec[at:at+1,hi-lo:d]=jnp.zeros((1,d-hi+lo),F32)
                 at+=1
         if at<v.vec.shape[0]: v.vec[at:]=jnp.zeros((v.vec.shape[0]-at,d),F32)
-    def vcopy(j): return remote(v.vec,v.vrecv.at[j],v.vsend.at[j],v.vrecv_sem.at[j],twin if j==0 else peer[order["qkv"][j-1]])
+    def vcopy(j): return remote(v.vec,v.vrecv.at[j],v.vsend.at[j],v.vrecv_sem.at[j],twin if j==0 else peer[order["out"][j-1]])
     def vstep(j):
         vcopy(j).wait()
         rows=slice(0,4) if j==0 else slice(None)
         v.vec[rows]=v.vec[rows]+v.vrecv[j,rows]
         if j<bits: vcopy(j+1).start()
 
-    mlp(0); attn(0); ysend("p",0)
-    mlp(1); attn(1); ysend("p",1)
-    mlp(2); mlp(3)
-    other("fc2"); other("fc1")
-    attn(2); ysend("p",2)
-    own(0); own(1); own(2)
-    attn(3); ysend("p",3)
-    for i in range(nb): dgrad(i)
-    vfill(); vcopy(0).start()
-    for i in range(nb): ysend("e",i)
-    other("qkv"); other("out")
-    for q in range(3,len(owns)): own(q)
-    todo=[]
-    wide=[(w,cb) for w in ("fc2","fc1","out") for cb in range(cols[w]//CW)]
-    for k,(w,cb) in enumerate(wide):
-        for j in range(1,bits): todo.append((94+12*k+12*(j-1),"s",(w,cb,j)))
-    for k in range(c//CW):
-        for j in range(1,bits): todo.append((132+14*k+18*(j-1),"s",("qkv",k,j)))
-    for i in range(nb):
-        todo.append((115+5*i if i<nb-1 else 130,"y",("p",i)))
-        todo.append((154+24*i,"y",("e",i)))
-    for j in range(bits+1): todo.append(((131,136,158,175,195,215,220,225)[j],"v",(j,)))
-    todo.sort(key=lambda t:t[0])
-    kept.extend(t[2][:2] for t in todo if t[1]=="s" and t[2][2]==1)
-    for _ in range(3): fetch_kept()
-    for _,kind,what in todo: {"s":stage,"y":yfinish,"v":vstep}[kind](*what)
+    todo=plan(bits,nb,{w:cols[w]//CW for w in WEIGHTS})
+    kept.extend((t[1],t[2]) for t in todo if t[0]=="stage" and t[3]==1)
+    def vec():
+        vfill(); vcopy(0).start()
+    run={"mlp":mlp,"attn":attn,"send":ysend,"other":other,"own":own,"dgrad":dgrad,"vec":vec,"stage":stage,"finish":yfinish,"vstep":vstep}
+    for t in todo: run[t[0]](*t[1:])
     cp=load(v.vec,v.sums,v.lsem.at[12]); cp.wait()
     for w in WEIGHTS:
         b0=order[w][0]; k=WEIGHTS.index(w)
@@ -414,7 +455,7 @@
     S=jax.ShapeDtypeStruct
     vrows=16
     small=("cos","sin","g1","g2","bias_out","b1","gsum")
-    ins=["starts"]+list(small)+["x","g","m","w1","w2","wo","w","qkv","do","gT","mT","aT"]
+    ins=["starts"]+list(small)+["x","g","m","w1","w2","wo","w","qkv","do","gT","hT","mT","aT"]
     specs=[]
     for k in ins:
         specs.append(pl.BlockSpec(memory_space=pltpu.SMEM if k=="starts" else pltpu.VMEM if k in small else pl.ANY))
@@ -429,7 +470,7 @@
     scratch=dict(w1v=V((d,ff),BF),w2v=V((ff,d),BF),wov=V((inner,d),BF),wv=V((d,c),BF),qv=V((heads,3*HD,n),BF),dov=V((heads,HD,n),BF),
         mbuf=V((2,TB,d),BF),gbuf=V((2,TB,d),BF),act=V((n,ff),BF),pg=V((n,ff),BF),o=V((heads,HD,n),BF),pgT=V((c,n),BF),
         part=V((n,d),F32),e=V((n,d),F32),acc=V((heads*n//CW,2*HD,CW),F32),bias=V((2*TB,TB),F32),abuf=V((2,d//4,n),BF),
-        ring=V((3,d//4,CW),F32),rin=V((2,d//4,CW),F32),fb=V((1,ff),F32),qb=V((1,c),F32),vec=V((vrows,d),F32),vrecv=V((bits+1,vrows,d),F32),
+        ring=V((2,d//4,CW),F32),kin=V((2,d//8,CW),F32),rin=V((2,d//4,CW),F32),fb=V((1,ff),F32),qb=V((1,c),F32),vec=V((vrows,d),F32),vrecv=V((bits+1,vrows,d),F32),
         lsem=D((23,)),ysend=D((2*(n//TB),)),yrecv_sem=D((2*(n//TB),)),csend=D((4,)),crecv=D((4,2)),xsend=D((bits-1,NP)),xrecv=D((bits-1,NP)),
         osem=D((4,)),isem=D((2,)),fsem=D((NP,)),vsend=D((bits+1,)),vrecv_sem=D((bits+1,)))
     size=d//4
@@ -451,9 +492,9 @@
     n,d=x.shape; c=w.shape[1]; ff=w1.shape[1]
     cos,sin=tables(n)
     row=lambda t:t.reshape(1,-1)
-    m,aT,mT,gT,qkv,do,gsum=prologue(dp,x,g,g1,b1,g2,b2,w,bq,wo,cos,sin)
+    m,aT,mT,gT,hT,qkv,do,gsum=prologue(dp,x,g,g1,b1,g2,b2,w,bq,wo,cos,sin)
     o=mega(dp,dict(starts=starts,cos=cos,sin=sin,g1=row(g1),g2=row(g2),bias_out=row(bo+bf2),b1=row(bf1),gsum=gsum,x=x,g=g,m=m,w1=w1,w2=w2,wo=wo,w=w,
-        qkv=qkv,do=do.reshape(-1,HD,n),gT=gT,mT=mT,aT=aT))
+        qkv=qkv,do=do.reshape(-1,HD,n),gT=gT,hT=hT,mT=mT,aT=aT))
     s=o["sums"]
     fr=5+-(-ff//d)
     fb=s[5:fr].reshape(-1)[:ff]; qb=s[fr:fr+-(-c//d)].reshape(-1)[:c]

time: 304 us -> 259 us (0.85)
  Pallas kernels: 289 us -> 244 us
    pallas_call x1, Pallas kernels: 276 us -> 231 us  [mega(): pl.pallas_call(functools.partial(mega_body, names, bits, (n, d, ff, inner...]
where the time goes in v4:
time: 259 us; the launch traced here: 258 us
  Pallas kernels  244 us (94%)
  local copies, waits for them, and re-layouts  12.6 us (5%)
    pallas_call x1, Pallas kernels, mega(): pl.pallas_call(functools.partial(mega_body, names, bits, (n, d, ff, inner...  231 us
    pallas_call x1, Pallas kernels, prologue(): pl.pallas_call(functools.partial(prologue_body, dp), name='prologue', gri...  12.8 us
    unnamed x20, local copies, waits for them, and re-layouts  9.08 us

profile of v4, /device:TPU:0, one launch (start us, length us, event | category | flops | bytes accessed | tf_op | source)
XLA Modules:
  0.0 258.4 jit_solution(13097044861825425017)
XLA Ops:
  0.6 1.3 add.3
  1.9 1.3 reshape.66.bq_ref
  3.2 12.8 %prologue.1 = (bf16[1024,1024]{1,0:T(8,128)(2,1)}, bf16[4,256,1024]{2,1,0:T(8,128)(2,1)}, bf16[4,256,1024]{2,1,0:T(8,128)(2,1)}, bf16[4,256,1024]{2,1,0:T(8,128)...) custom-call(bf16[1024,1024]{1,0:T(8,128)(2,1)} %refs_8_.1, ...), custom_call_target="tpu_custom_call" | custom-call | flops 4294967296 | bytes 20971520 | tf_op jit(solution)/shard_map/prologue/pallas_call | solution.py:83
  16.0 231.1 %layer.1 = (bf16[1024,1024]{1,0:T(8,128)(2,1)}, bf16[1024,1024]{1,0:T(8,128)(2,1)}, f32[16,1024]{1,0:T(8,128)}, f32[64,2048]{1,0:T(8,128)}, f32[64,2048]{1,0:T(8...) custom-call(s32[1,2]{1,0:T(1,128)} %refs_0_.1, ...), custom_call_target="tpu_custom_call" | custom-call | tf_op jit(solution)/shard_map/layer/pallas_call | solution.py:480
  247.1 0.9 slice_bitcast_fusion
  248.0 1.6 fusion
  249.6 0.0 copy-start.5
  249.6 0.6 copy_bitcast_fusion
  250.2 0.6 copy.42
  250.8 0.0 copy-start
  250.8 3.2 %copy.43 = bf16[1024,1024]{1,0:T(8,128)(2,1)} copy(bf16[1024,1024]{1,0:T(8,128)(2,1)} %get-tuple-element.95) | data formatting | bytes 4194304
  254.0 0.0 copy-done.5
  254.1 0.0 copy-done
  254.1 0.0 copy-start.3
  254.1 0.0 copy-start.4
  254.1 0.0 copy-start.2
  254.1 1.3 copy.44
  255.4 0.0 copy-done.3
  255.4 0.0 copy-start.1
  255.4 0.7 copy.45
  256.1 0.0 copy-done.4
  256.1 0.7 copy.46
  256.8 0.0 copy-done.2
  256.8 0.8 copy.47
  257.6 0.0 copy-done.1
  257.6 0.8 copy.48
Async XLA Ops:
  249.6 4.4 %copy-start.5 = (f32[1,1024]{1,0:T(1,128)}, f32[1,1024]{1,0:T(1,128)S(1)}, u32[]{:S(2)}) copy-start(f32[1,1024]{1,0:T(1,128)S(1)} %get-tuple-element.48) | copy-start | bytes 12292
  250.8 3.2 %copy-start = (bf16[1024,1024]{1,0:T(8,128)(2,1)S(1)}, bf16[1024,1024]{1,0:T(8,128)(2,1)}, u32[]{:S(2)}) copy-start(bf16[1024,1024]{1,0:T(8,128)(2,1)} %get-tuple-element.96) | copy-start | bytes 6291460
  254.1 1.3 copy-start.3
  254.1 2.1 copy-start.4
  254.1 2.7 %copy-start.2 = (f32[64,2048]{1,0:T(8,128)S(1)}, f32[64,2048]{1,0:T(8,128)}, u32[]{:S(2)}) copy-start(f32[64,2048]{1,0:T(8,128)} %get-tuple-element.105) | copy-start | bytes 1572868
  255.4 2.2 copy-start.1

commit v5 on v4

--- a/solution.py
+++ b/solution.py
@@ -24,12 +24,12 @@
     return c*inv, inv
 
 def prologue_body(dp, x_ref,g_ref,g1,b1,g2,b2,w_ref,bq_ref,wo_ref,cos_ref,sin_ref,
-             m_out,aT_out,mT_out,gT_out,hT_out,qkv_out,do_out,gsum_out,wT,bcol):
+             m_out,aT_out,mT_out,gT_out,qkv_out,do_out,gsum_out,wT,bcol):
     step=pl.program_id(0)
     @pl.when(step==0)
     def _():
         wT[...]=w_ref[...].T
-        bcol[...]=jnp.broadcast_to(bq_ref[...],(128,bq_ref.shape[1])).T
+        bcol[...]=jnp.broadcast_to(bq_ref[...][None,:],(128,bq_ref.shape[0])).T
         gsum_out[...]=jnp.zeros_like(gsum_out)
     d=x_ref.shape[1]
     rows=d//dp
@@ -48,12 +48,13 @@
         t=jnp.concatenate(blocks,axis=0)
         return [t[j*(d//4):(j+1)*(d//4)] for j in range(4)]
     order=orders(bits)
-    aT=a.T
-    mT=m.T
+    turn=(lambda t: t.astype(BF).T) if rows%16==0 else (lambda t: t.T)
+    aT=turn(a)
+    mT=turn(m)
     gf=g_ref[...].astype(F32)
     gsum_out[...]+=jnp.sum(gf,axis=0,keepdims=True)
-    gT=gf.T
-    for t,o,w in ((aT,aT_out,"qkv"),(mT,mT_out,"fc1"),(gT,gT_out,"fc2"),(gT,hT_out,"out")):
+    gT=turn(gf)
+    for t,o,w in ((aT,aT_out,"qkv"),(mT,mT_out,"fc1"),(gT,gT_out,"fc2")):
         for j,pt in enumerate(perm(t,order[w])):
             o[j]=pt.astype(BF)
     packed=dot(wT[...],aT.astype(BF))
@@ -77,15 +78,15 @@
     row=lambda v: v.reshape(1,-1)
     full=lambda a: pl.BlockSpec(a.shape,lambda i:(0,)*a.ndim)
     tspec=pl.BlockSpec((4,d//4,TB),lambda i:(0,0,i))
-    args=(x,g,row(g1),row(b1),row(g2),row(b2),w,row(bq),wo,cos,sin)
+    args=(x,g,row(g1),row(b1),row(g2),row(b2),w,bq,wo,cos,sin)
     xs=pl.BlockSpec((TB,d),lambda i:(i,0))
     ts=pl.BlockSpec((8,TB),lambda i:(0,i))
     return pl.pallas_call(functools.partial(prologue_body,dp),name="prologue",
         grid=(n//TB,),
         in_specs=[xs,xs]+[full(a) for a in args[2:9]]+[ts,ts],
-        out_specs=[xs,tspec,tspec,tspec,tspec,pl.BlockSpec((heads,3*HD,TB),lambda i:(0,0,i)),
+        out_specs=[xs,tspec,tspec,tspec,pl.BlockSpec((heads,3*HD,TB),lambda i:(0,0,i)),
                    pl.BlockSpec((inner,TB),lambda i:(0,i)),pl.BlockSpec((1,d),lambda i:(0,0))],
-        out_shape=[jax.ShapeDtypeStruct((n,d),BF)]+[jax.ShapeDtypeStruct((4,d//4,n),BF)]*4+
+        out_shape=[jax.ShapeDtypeStruct((n,d),BF)]+[jax.ShapeDtypeStruct((4,d//4,n),BF)]*3+
             [jax.ShapeDtypeStruct((heads,3*HD,n),BF),jax.ShapeDtypeStruct((inner,n),BF),jax.ShapeDtypeStruct((1,d),F32)],
         scratch_shapes=[pltpu.VMEM((c,d),BF),pltpu.VMEM((c,128),F32)],
         compiler_params=pltpu.CompilerParams(vmem_limit_bytes=60*2**20),
@@ -98,17 +99,17 @@
 
 def orders(bits):
     up=list(range(bits))
-    return {"fc2":up,"fc1":up,"qkv":up,"out":up[:1]+up[2:]+up[1:2]}
+    return {"fc2":up,"fc1":up,"qkv":up,"out":up}
 
 def plan(bits,nb,count):
-    unit=1.048576*2/88*1000
+    unit=1.048576*2/80*1000
     order=orders(bits)
-    free={}; arr=[]; out=[]; r0={}; whole=set(); clock=[18.0]; corelink=[0.0]
+    free={}; arr=[]; out=[]; r0={}; whole=set(); clock=[13.0]; corelink=[0.0]
     def xfer(dim,mb,t):
         key=min(dim,2); us=mb*unit
         s=max(t,free.get(key,0.0)); free[key]=s+us
         if dim<3: return s+us+2
-        m=max(s,free.get("mid",0.0))+2*us; free["mid"]=m
+        m=max(s,free.get("mid",0.0))+2*us; free["mid"]=m; free[key]=s+2*us
         return m+2
     def push(at,rank,item): arr.append((at,rank,len(out),item))
     def do(item):
@@ -116,11 +117,11 @@
         out.append(item)
         if item[0]=="stage":
             _,w,cb,j=item
-            if j<bits-1: push(xfer(order[w][j+1],0.5**(j+1),clock[0]),4-min(j,3),("stage",w,cb,j+1))
+            if j<bits-1: push(xfer(order[w][j+1],0.5**(j+1),clock[0])+(12 if j==bits-2 else 0),4-min(j,3),("stage",w,cb,j+1))
         elif item[0]=="vstep":
             j=item[1]
             if j<bits:
-                dim=order["out"][j]
+                dim=([0]+list(range(2,bits))+[1])[j]
                 push(xfer(dim,1/16,clock[0]) if dim else clock[0]+2.5,0,("vstep",j+1))
     def ready(tail):
         def ok(it):
@@ -133,18 +134,20 @@
             if not r: return
             a=min(r,key=lambda a:(a[1],a[0],a[2])); arr.remove(a); do(a[3]); most-=1
     head=[]
-    for i in range(nb-2): head+=[("mlp",i),("attn",i),("send","p",i)]
-    head+=[("mlp",i) for i in range(nb-2,nb)]+[("other","fc2"),("other","fc1"),("attn",nb-2),("send","p",nb-2)]
-    head+=[("own","fc2",0),("own","fc1",0),("own","fc2",1),("attn",nb-1),("send","p",nb-1)]
+    for i in range(nb-2): head+=[("mlp",i),("ends",i),("attn",i),("send","p",i)]
+    head+=[("mlp",i) for i in range(nb-2,nb)]+[("other","fc2"),("own","fc2",0)]+[("ends",nb-2),("attn",nb-2),("send","p",nb-2)]
+    head+=[("own","fc2",1)]+[("ends",nb-1),("attn",nb-1),("send","p",nb-1)]+[("back",i) for i in range(nb)]+[("other","fc1"),("own","fc1",0)]
     head+=[("dgrad",i) for i in range(nb)]+[("vec",)]+[("send","e",i) for i in range(nb)]
-    head+=[("other","out"),("other","qkv"),("own","out",0),("own","qkv",0),("own","fc1",1),("own","out",1),("own","qkv",1)]
+    head+=[("own","fc1",1)]
+    head+=[("other","out"),("other","qkv"),("own","out",0),("own","qkv",0),("own","out",1),("own","qkv",1)]
     for h in head:
         poll(False,6)
         out.append(h); k=h[0]
-        if k=="mlp": clock[0]+=6.1
+        if k=="mlp": clock[0]+=3.5
+        elif k in ("ends","back"): clock[0]+=1.3
         elif k=="attn": clock[0]+=3.35*min(h[1]+2,nb)
         elif k=="dgrad": clock[0]+=1.6
-        elif k=="send": push(xfer(1.5,1,clock[0]),9 if h[1]=="p" else 6,("finish",)+h[1:])
+        elif k=="send": push(xfer(1.5,1,clock[0])+4,9 if h[1]=="p" else 6,("finish",)+h[1:])
         elif k=="vec": push(xfer(1.5,1/16,clock[0]),0,("vstep",0))
         elif k=="other":
             for i in range(2*count[h[1]]):
@@ -216,10 +219,18 @@
                 bs=jnp.sum(pg.astype(F32),axis=0,keepdims=True)
                 if i==0: v.fb[:,sl]=bs
                 else: v.fb[:,sl]+=bs
+    def back_mlp(i):
+        r0=i*TB
         @pl.loop(0,d//CW)
         def _(f):
             sl=pl.ds(pl.multiple_of(f*CW,CW),CW)
             v.part[r0:r0+TB,sl]=dot(v.act[r0:r0+TB,:],v.w2v[:,sl])
+
+    def back_in(i):
+        r0=i*TB
+        @pl.loop(0,d//CW)
+        def _(f):
+            sl=pl.ds(pl.multiple_of(f*CW,CW),CW)
             v.e[r0:r0+TB,sl]=dot_nt(v.pg[r0:r0+TB,:],v.w1v[sl,:])
 
     def back(b,cc,s):
@@ -297,7 +308,7 @@
             wait("recv%d"%k)
             rs=slice(a*128,(a+1)*128); cs=slice(b*CW,(b+1)*CW)
             t=v.mbuf[0,rs,cs].astype(F32)+(v.part if kind=="p" else v.e)[i*TB+a*128:i*TB+(a+1)*128,cs]+v.acc[k]
-            if kind=="p": t=t+v.bias_out[:,cs]
+            if kind=="p": t=t+(v.bo[:,cs]+v.bf2[:,cs])
             v.gbuf[0,rs,cs]=t.astype(BF)
         fetch("st",v.gbuf.at[0],out.at[rowsl(i)],11)
         wait("st")
@@ -308,7 +319,7 @@
         if w=="fc1": return v.pg[:,cs],False
         if w=="out": return v.o[...].reshape(inner,n),True
         return v.pgT[cs,:],True
-    lhs={"fc2":v.gT,"out":v.hT,"fc1":v.mT,"qkv":v.aT}
+    lhs={"fc2":v.gT,"out":v.gT,"fc1":v.mT,"qkv":v.aT}
     def product(w,a,cb):
         b,nt=rhs(w,cb)
         y=dot_nt(a,b) if nt else dot(a,b)
@@ -426,7 +437,8 @@
                 if hi-lo<d: v.vec[at:at+1,hi-lo:d]=jnp.zeros((1,d-hi+lo),F32)
                 at+=1
         if at<v.vec.shape[0]: v.vec[at:]=jnp.zeros((v.vec.shape[0]-at,d),F32)
-    def vcopy(j): return remote(v.vec,v.vrecv.at[j],v.vsend.at[j],v.vrecv_sem.at[j],twin if j==0 else peer[order["out"][j-1]])
+    vorder=[0]+list(range(2,bits))+[1]
+    def vcopy(j): return remote(v.vec,v.vrecv.at[j],v.vsend.at[j],v.vrecv_sem.at[j],twin if j==0 else peer[vorder[j-1]])
     def vstep(j):
         vcopy(j).wait()
         rows=slice(0,4) if j==0 else slice(None)
@@ -437,7 +449,7 @@
     kept.extend((t[1],t[2]) for t in todo if t[0]=="stage" and t[3]==1)
     def vec():
         vfill(); vcopy(0).start()
-    run={"mlp":mlp,"attn":attn,"send":ysend,"other":other,"own":own,"dgrad":dgrad,"vec":vec,"stage":stage,"finish":yfinish,"vstep":vstep}
+    run={"mlp":mlp,"ends":back_mlp,"back":back_in,"attn":attn,"send":ysend,"other":other,"own":own,"dgrad":dgrad,"vec":vec,"stage":stage,"finish":yfinish,"vstep":vstep}
     for t in todo: run[t[0]](*t[1:])
     cp=load(v.vec,v.sums,v.lsem.at[12]); cp.wait()
     for w in WEIGHTS:
@@ -454,8 +466,8 @@
     cols={"fc2":ff,"fc1":ff,"out":inner,"qkv":c}
     S=jax.ShapeDtypeStruct
     vrows=16
-    small=("cos","sin","g1","g2","bias_out","b1","gsum")
-    ins=["starts"]+list(small)+["x","g","m","w1","w2","wo","w","qkv","do","gT","hT","mT","aT"]
+    small=("cos","sin","g1","g2","bo","bf2","b1","gsum")
+    ins=["starts"]+list(small)+["x","g","m","w1","w2","wo","w","qkv","do","gT","mT","aT"]
     specs=[]
     for k in ins:
         specs.append(pl.BlockSpec(memory_space=pltpu.SMEM if k=="starts" else pltpu.VMEM if k in small else pl.ANY))
@@ -484,6 +496,30 @@
     )(*[args[k] for k in ins])
     return dict(zip(outs,res))
 
+def outputs_body(spans,count,*refs):
+    ins=refs[:count]; s_ref=refs[count]; outs=refs[count+1:]
+    for i in range(count): outs[i][...]=ins[i][...]
+    @pl.when(pl.program_id(0)==0)
+    def _():
+        for o,at in zip(outs[count:],spans):
+            n=o.shape[0]; d=s_ref.shape[1]
+            for k in range(-(-n//d)):
+                hi=min(n,(k+1)*d)
+                o[k*d:hi]=s_ref[at+k,0:hi-k*d]
+
+def outputs(big,sums,spans,sizes):
+    steps=4
+    def spec(t):
+        if t.dtype==BF: return pl.BlockSpec((t.shape[0]//steps,t.shape[1]),lambda i:(i,0))
+        return pl.BlockSpec((t.shape[0],t.shape[1]//steps),lambda i:(0,i))
+    S=jax.ShapeDtypeStruct
+    return pl.pallas_call(functools.partial(outputs_body,spans,len(big)),name="outputs",grid=(steps,),
+        in_specs=[spec(t) for t in big]+[pl.BlockSpec(sums.shape,lambda i:(0,0))],
+        out_specs=[spec(t) for t in big]+[pl.BlockSpec((n,),lambda i:(0,)) for n in sizes],
+        out_shape=[S(t.shape,t.dtype) for t in big]+[S((n,),F32) for n in sizes],
+        compiler_params=pltpu.CompilerParams(vmem_limit_bytes=67043328),
+    )(*big,sums)
+
 def tables(n):
     angles=np.arange(n,dtype=np.float64)[None,:]*(10000.0**(-np.arange(ROT//2)*2.0/ROT))[:,None]
     return jnp.asarray(np.cos(angles),F32),jnp.asarray(np.sin(angles),F32)
@@ -492,13 +528,14 @@
     n,d=x.shape; c=w.shape[1]; ff=w1.shape[1]
     cos,sin=tables(n)
     row=lambda t:t.reshape(1,-1)
-    m,aT,mT,gT,hT,qkv,do,gsum=prologue(dp,x,g,g1,b1,g2,b2,w,bq,wo,cos,sin)
-    o=mega(dp,dict(starts=starts,cos=cos,sin=sin,g1=row(g1),g2=row(g2),bias_out=row(bo+bf2),b1=row(bf1),gsum=gsum,x=x,g=g,m=m,w1=w1,w2=w2,wo=wo,w=w,
-        qkv=qkv,do=do.reshape(-1,HD,n),gT=gT,hT=hT,mT=mT,aT=aT))
-    s=o["sums"]
+    m,aT,mT,gT,qkv,do,gsum=prologue(dp,x,g,g1,b1,g2,b2,w,bq,wo,cos,sin)
+    o=mega(dp,dict(starts=starts,cos=cos,sin=sin,g1=row(g1),g2=row(g2),bo=row(bo),bf2=row(bf2),b1=row(bf1),gsum=gsum,x=x,g=g,m=m,w1=w1,w2=w2,wo=wo,w=w,
+        qkv=qkv,do=do.reshape(-1,HD,n),gT=gT,mT=mT,aT=aT))
     fr=5+-(-ff//d)
-    fb=s[5:fr].reshape(-1)[:ff]; qb=s[fr:fr+-(-c//d)].reshape(-1)[:c]
-    return (o["hidden"],o["hgrad"],s[0],s[1],o["f_qkv"],qb,o["f_out"].T,s[4],s[2],s[3],o["f_fc1"],fb,o["f_fc2"].T,s[4])
+    hidden,hgrad,fq,fo,f1,f2,*vs=outputs([o[k] for k in ("hidden","hgrad","f_qkv","f_out","f_fc1","f_fc2")],o["sums"],
+        (0,1,2,3,4,4,5,fr),(d,d,d,d,d,d,ff,c))
+    g1g,b1g,g2g,b2g,bog,b2o,fb,qb=vs
+    return (hidden,hgrad,g1g,b1g,fq,qb,fo.T,bog,g2g,b2g,f1,fb,f2.T,b2o)
 
 def solution(mesh):
     A=P("dp",None); R=P()

time: 259 us -> 238 us (0.919)
  local copies, waits for them, and re-layouts: 12.6 us -> 0 us
  Pallas kernels: 244 us -> 236 us
    pallas_call x1, Pallas kernels: 231 us -> 218 us  [mega(): pl.pallas_call(functools.partial(mega_body, names, bits, (n, d, ff, inner...]
    unnamed x20 -> x0, local copies, waits for them, and re-layouts: 9.08 us -> none
    pallas_call x0 -> x1, Pallas kernels: none -> 5.83 us  [outputs(): pl.pallas_call(functools.partial(outputs_body, spans, len(big)), name='ou...]
where the time goes in v5:
time: 238 us; the launch traced here: 237 us
  Pallas kernels  236 us (99%)
    pallas_call x1, Pallas kernels, mega(): pl.pallas_call(functools.partial(mega_body, names, bits, (n, d, ff, inner...  218 us
    pallas_call x1, Pallas kernels, prologue(): pl.pallas_call(functools.partial(prologue_body, dp), name='prologue', gri...  12.4 us
    pallas_call x1, Pallas kernels, outputs(): pl.pallas_call(functools.partial(outputs_body, spans, len(big)), name='ou...  5.83 us

profile of v5, /device:TPU:0, one launch (start us, length us, event | category | flops | bytes accessed | tf_op | source)
XLA Modules:
  0.0 237.0 jit_solution(6336353328463640041)
XLA Ops:
  0.6 12.4 %prologue.1 = (bf16[1024,1024]{1,0:T(8,128)(2,1)}, bf16[4,256,1024]{2,1,0:T(8,128)(2,1)}, bf16[4,256,1024]{2,1,0:T(8,128)(2,1)}, bf16[4,256,1024]{2,1,0:T(8,128)...) custom-call(bf16[1024,1024]{1,0:T(8,128)(2,1)} %refs_9_.1, ...), custom_call_target="tpu_custom_call" | custom-call | flops 4294967296 | bytes 20971520 | tf_op jit(solution)/shard_map/prologue/pallas_call | solution.py:84
  13.1 217.8 %layer.1 = (bf16[1024,1024]{1,0:T(8,128)(2,1)}, bf16[1024,1024]{1,0:T(8,128)(2,1)}, f32[16,1024]{1,0:T(8,128)}, f32[64,2048]{1,0:T(8,128)}, f32[64,2048]{1,0:T(8...) custom-call(s32[1,2]{1,0:T(1,128)} %refs_0_.1, ...), custom_call_target="tpu_custom_call" | custom-call | tf_op jit(solution)/shard_map/layer/pallas_call | solution.py:492
  230.9 5.8 %outputs.1 = (bf16[1024,1024]{1,0:T(8,128)(2,1)}, bf16[1024,1024]{1,0:T(8,128)(2,1)}, f32[64,1536]{1,0:T(8,128)}, f32[64,512]{1,0:T(8,128)}, f32[64,2048]{1,0:T(...) custom-call(bf16[1024,1024]{1,0:T(8,128)(2,1)} %get-tuple-element.49, ...), custom_call_target="tpu_custom_call" | custom-call | tf_op jit(solution)/shard_map/outputs/pallas_call | solution.py:516

commit v6 on v5

--- a/solution.py
+++ b/solution.py
@@ -497,26 +497,27 @@
     return dict(zip(outs,res))
 
 def outputs_body(spans,count,*refs):
-    ins=refs[:count]; s_ref=refs[count]; outs=refs[count+1:]
-    for i in range(count): outs[i][...]=ins[i][...]
-    @pl.when(pl.program_id(0)==0)
-    def _():
-        for o,at in zip(outs[count:],spans):
-            n=o.shape[0]; d=s_ref.shape[1]
-            for k in range(-(-n//d)):
-                hi=min(n,(k+1)*d)
-                o[k*d:hi]=s_ref[at+k,0:hi-k*d]
+    ins=refs[:count]; s_ref=refs[count]; outs=refs[count+1:2*count+1]
+    vs=refs[2*count+1:2*count+1+len(spans)]; bufs=refs[2*count+1+len(spans):-1]; sem=refs[-1]
+    into=[pltpu.make_async_copy(ins[i],bufs[i],sem.at[0,i]) for i in range(count)]
+    for cp in into: cp.start()
+    for o,at in zip(vs,spans):
+        n=o.shape[0]; d=s_ref.shape[1]
+        for k in range(-(-n//d)):
+            hi=min(n,(k+1)*d)
+            o[k*d:hi]=s_ref[at+k,0:hi-k*d]
+    back=[pltpu.make_async_copy(bufs[i],outs[i],sem.at[1,i]) for i in range(count)]
+    for i in range(count):
+        into[i].wait(); back[i].start()
+    for cp in back: cp.wait()
 
 def outputs(big,sums,spans,sizes):
-    steps=4
-    def spec(t):
-        if t.dtype==BF: return pl.BlockSpec((t.shape[0]//steps,t.shape[1]),lambda i:(i,0))
-        return pl.BlockSpec((t.shape[0],t.shape[1]//steps),lambda i:(0,i))
     S=jax.ShapeDtypeStruct
-    return pl.pallas_call(functools.partial(outputs_body,spans,len(big)),name="outputs",grid=(steps,),
-        in_specs=[spec(t) for t in big]+[pl.BlockSpec(sums.shape,lambda i:(0,0))],
-        out_specs=[spec(t) for t in big]+[pl.BlockSpec((n,),lambda i:(0,)) for n in sizes],
+    anywhere=pl.BlockSpec(memory_space=pl.ANY); near=pl.BlockSpec(memory_space=pltpu.VMEM)
+    return pl.pallas_call(functools.partial(outputs_body,spans,len(big)),name="outputs",
+        in_specs=[anywhere]*len(big)+[near],out_specs=[anywhere]*len(big)+[near]*len(sizes),
         out_shape=[S(t.shape,t.dtype) for t in big]+[S((n,),F32) for n in sizes],
+        scratch_shapes=[pltpu.VMEM(t.shape,t.dtype) for t in big]+[pltpu.SemaphoreType.DMA((2,len(big)))],
         compiler_params=pltpu.CompilerParams(vmem_limit_bytes=67043328),
     )(*big,sums)
 

time: 238 us -> 238 us (level)
  no operation moved by 1% of the time
where the time goes in v6:
time: 238 us; the launch traced here: 237 us
  Pallas kernels  236 us (99%)
    pallas_call x1, Pallas kernels, mega(): pl.pallas_call(functools.partial(mega_body, names, bits, (n, d, ff, inner...  218 us
    pallas_call x1, Pallas kernels, prologue(): pl.pallas_call(functools.partial(prologue_body, dp), name='prologue', gri...  12.4 us
    pallas_call x1, Pallas kernels, outputs(): pl.pallas_call(functools.partial(outputs_body, spans, len(big)), name='ou...  5.66 us

profile of v6, /device:TPU:0, one launch (start us, length us, event | category | flops | bytes accessed | tf_op | source)
XLA Modules:
  0.0 236.8 jit_solution(15484045645948843817)
XLA Ops:
  0.6 12.4 %prologue.1 = (bf16[1024,1024]{1,0:T(8,128)(2,1)}, bf16[4,256,1024]{2,1,0:T(8,128)(2,1)}, bf16[4,256,1024]{2,1,0:T(8,128)(2,1)}, bf16[4,256,1024]{2,1,0:T(8,128)...) custom-call(bf16[1024,1024]{1,0:T(8,128)(2,1)} %refs_9_.1, ...), custom_call_target="tpu_custom_call" | custom-call | flops 4294967296 | bytes 20971520 | tf_op jit(solution)/shard_map/prologue/pallas_call | solution.py:84
  13.1 217.8 %layer.1 = (bf16[1024,1024]{1,0:T(8,128)(2,1)}, bf16[1024,1024]{1,0:T(8,128)(2,1)}, f32[16,1024]{1,0:T(8,128)}, f32[64,2048]{1,0:T(8,128)}, f32[64,2048]{1,0:T(8...) custom-call(s32[1,2]{1,0:T(1,128)} %refs_0_.1, ...), custom_call_target="tpu_custom_call" | custom-call | tf_op jit(solution)/shard_map/layer/pallas_call | solution.py:492
  230.9 5.7 %outputs.1 = (bf16[1024,1024]{1,0:T(8,128)(2,1)}, bf16[1024,1024]{1,0:T(8,128)(2,1)}, f32[64,1536]{1,0:T(8,128)}, f32[64,512]{1,0:T(8,128)}, f32[64,2048]{1,0:T(...) custom-call(bf16[1024,1024]{1,0:T(8,128)(2,1)} %get-tuple-element.49, ...), custom_call_target="tpu_custom_call" | custom-call | tf_op jit(solution)/shard_map/outputs/pallas_call | solution.py:517
